TPU v7x, 128 devices: a whole 4x4x4 slice. The times are simulated.
128 devices in a mesh: slab: 32 (over y, z_hi, x), coil: 4 (over z_lo, core).
Axes of the slice: x: 4, y: 4, z: 4 (z_hi: 2, z_lo: 2; z = z_hi * 2 + z_lo), core: 2. Of those that a mesh axis runs over, the one named last changes fastest.
Arguments:
- image: float32 [256, 2, 32, 384], P(('slab', 'coil')), may hold values from -6 to 6
- noise: float32 [256, 2, 32, 384], P(('slab', 'coil')), may hold values from -1.2 to 1.2
- sens: bfloat16 [16, 2, 32, 384, 256], P('coil', None, 'slab'), may hold values from -1 to 1
- measured: bfloat16 [16, 2, 32, 384, 256], P('coil', None, 'slab'), may hold values from -3 to 3
- mask: int32 [384, 256], replicated, may hold values 0 or 1
- w_first: bfloat16 [3, 3, 10, 128], replicated, may hold values from -0.625 to 0.625
- b_first: float32 [128], replicated, may hold values from -3 to 3
- w_second: bfloat16 [128, 128], replicated, may hold values from -0.5 to 0.5
- b_second: float32 [128], replicated, may hold values from -3 to 3
- w_third: bfloat16 [128, 128], replicated, may hold values from -0.5 to 0.5
- b_third: float32 [128], replicated, may hold values from -3 to 3
- w_last: bfloat16 [3, 3, 2, 128], replicated, may hold values from -0.1875 to 0.1875
Outputs:
- updated: float32 [256, 2, 32, 384], P(('slab', 'coil'))
Inputs may be any that keep to these rules, and one draw needn't show every extreme that they name: `mask`: 1 where the (ky, kz) line was measured, else 0.
All inputs are finite; a program needn't handle non-finite values.
Results may differ from a plain program's by a relative error of at most 0.0035.
Values may be sent and summed in bfloat16 or wider, within the bound.
A program may use at most 256 MiB of HBM per device.

v0:
```python
import jax
import jax.numpy as jnp
from jax import lax
from jax.sharding import PartitionSpec as P
from jax.experimental import pallas as pl
from jax.experimental.pallas import tpu as pltpu

STEP_SIZE = 0.5


def with_halo(shard, sides, width):
    for axis, dim in sides:
        devices, length = (lax.axis_size(axis), shard.shape[dim])
        up = [(i, (i + 1) % devices) for i in range(devices - 1)]
        down = [(j, i) for i, j in up]
        last = lax.slice_in_dim(shard, length - width, length, axis=dim)
        first = lax.slice_in_dim(shard, 0, width, axis=dim)
        before = lax.ppermute(last, axis, up)
        after = lax.ppermute(first, axis, down)
        shard = jnp.concatenate([before, shard, after], axis=dim)
    return shard


def dft_tables(length):
    line_index = jnp.arange(length, dtype=jnp.int32)
    phase_turns = line_index[:, None] * line_index[None, :] % length
    phase_angle = phase_turns.astype(jnp.float32) * (2.0 * jnp.pi / length)
    norm_scale = 1.0 / jnp.sqrt(jnp.float32(length))
    return (
        (jnp.cos(phase_angle) * norm_scale).astype(jnp.bfloat16),
        (jnp.sin(phase_angle) * norm_scale).astype(jnp.bfloat16),
    )


def along_y(values, table):
    return jnp.einsum("...yz,yk->...kz", values, table, preferred_element_type=jnp.float32)


def along_z(values, table):
    return jnp.einsum("...z,zk->...k", values, table, preferred_element_type=jnp.float32)


def spectrum(real_part, imag_part, cos_y, sin_y, cos_z, sin_z, forward):
    sign = 1.0 if forward else -1.0
    out_real = (along_y(real_part, cos_y) + sign * along_y(imag_part, sin_y)).astype(jnp.bfloat16)
    out_imag = (along_y(imag_part, cos_y) - sign * along_y(real_part, sin_y)).astype(jnp.bfloat16)
    last_real = along_z(out_real, cos_z) + sign * along_z(out_imag, sin_z)
    last_imag = along_z(out_imag, cos_z) - sign * along_z(out_real, sin_z)
    return (last_real, last_imag)


def adjoint_kernel(planes_ref, sens_ref, meas_ref, mask_ref, ty_ref, tz_ref, out_ref):
    ny = planes_ref.shape[1]
    nz = planes_ref.shape[2]

    @pl.when(pl.program_id(0) == 0)
    def _():
        out_ref[...] = jnp.zeros_like(out_ref)

    ty = ty_ref[...]
    tz = tz_ref[...]
    sens_real = sens_ref[0].astype(jnp.float32)
    sens_imag = sens_ref[1].astype(jnp.float32)
    image_real = planes_ref[0]
    image_imag = planes_ref[1]
    coil_real = (sens_real * image_real - sens_imag * image_imag).astype(jnp.bfloat16)
    coil_imag = (sens_real * image_imag + sens_imag * image_real).astype(jnp.bfloat16)
    half = jnp.dot(ty, jnp.concatenate([coil_real, coil_imag], axis=1), preferred_element_type=jnp.float32)
    half_real = (half[:ny, :nz] + half[ny:, nz:]).astype(jnp.bfloat16)
    half_imag = (half[:ny, nz:] - half[ny:, :nz]).astype(jnp.bfloat16)
    full = jnp.dot(jnp.concatenate([half_real, half_imag], axis=0), tz, preferred_element_type=jnp.float32)
    spec_real = full[:ny, :nz] + full[ny:, nz:]
    spec_imag = full[ny:, :nz] - full[:ny, nz:]
    sampled = mask_ref[...].astype(jnp.float32)
    miss_real = (sampled * (spec_real - meas_ref[0].astype(jnp.float32))).astype(jnp.bfloat16)
    miss_imag = (sampled * (spec_imag - meas_ref[1].astype(jnp.float32))).astype(jnp.bfloat16)
    half = jnp.dot(ty, jnp.concatenate([miss_real, miss_imag], axis=1), preferred_element_type=jnp.float32)
    back_real = (half[:ny, :nz] - half[ny:, nz:]).astype(jnp.bfloat16)
    back_imag = (half[:ny, nz:] + half[ny:, :nz]).astype(jnp.bfloat16)
    full = jnp.dot(jnp.concatenate([back_real, back_imag], axis=0), tz, preferred_element_type=jnp.float32)
    grad_real = full[:ny, :nz] - full[ny:, nz:]
    grad_imag = full[ny:, :nz] + full[:ny, nz:]
    out_ref[0] += sens_real * grad_real + sens_imag * grad_imag
    out_ref[1] += sens_real * grad_imag - sens_imag * grad_real


def coil_adjoint(planes, sens, measured, mask):
    ny = planes.shape[2]
    nz = planes.shape[3]
    cos_y, sin_y = dft_tables(ny)
    cos_z, sin_z = dft_tables(nz)
    ty = jnp.concatenate([cos_y, sin_y], axis=0)
    tz = jnp.concatenate([cos_z, sin_z], axis=1)
    coils = sens.shape[0]
    return pl.pallas_call(
        adjoint_kernel,
        grid=(coils,),
        in_specs=[
            pl.BlockSpec((2, None, ny, nz), lambda c: (0, 0, 0, 0)),
            pl.BlockSpec((None, 2, None, ny, nz), lambda c: (c, 0, 0, 0, 0)),
            pl.BlockSpec((None, 2, None, ny, nz), lambda c: (c, 0, 0, 0, 0)),
            pl.BlockSpec((ny, nz), lambda c: (0, 0)),
            pl.BlockSpec((2 * ny, ny), lambda c: (0, 0)),
            pl.BlockSpec((nz, 2 * nz), lambda c: (0, 0)),
        ],
        out_specs=pl.BlockSpec((2, None, ny, nz), lambda c: (0, 0, 0, 0)),
        out_shape=jax.ShapeDtypeStruct(planes.shape, jnp.float32),
    )(planes, sens, measured, mask, ty, tz)


def net_kernel(x_ref, w1_ref, b1_ref, w2_ref, b2_ref, w3_ref, b3_ref, wl_ref, q_ref):
    h = jnp.dot(w1_ref[...], x_ref[0], preferred_element_type=jnp.float32) + b1_ref[...]
    h = jax.nn.silu(h).astype(jnp.bfloat16)
    h = jnp.dot(w2_ref[...], h, preferred_element_type=jnp.float32) + b2_ref[...]
    h = jax.nn.silu(h).astype(jnp.bfloat16)
    h = jnp.dot(w3_ref[...], h, preferred_element_type=jnp.float32) + b3_ref[...]
    h = jax.nn.silu(h).astype(jnp.bfloat16)
    q = jnp.dot(wl_ref[...], h, preferred_element_type=jnp.float32)
    cols = q_ref.shape[3]
    for row in range(q_ref.shape[1]):
        q_ref[0, row] = q[:, row * cols : (row + 1) * cols]


def score_net(window, w_first, b_first, w_second, b_second, w_third, b_third, w_last):
    slice_count = window.shape[0] - 4
    row_count = window.shape[2]
    col_count = window.shape[3]
    width = w_first.shape[-1]
    pixels = row_count * col_count
    stacked = jnp.concatenate(
        [window[offset : offset + slice_count] for offset in range(5)], axis=1
    )
    framed = jnp.pad(stacked, ((0, 0), (0, 0), (1, 1), (1, 1)))
    columns = jnp.concatenate(
        [
            framed[:, :, shift_x : shift_x + row_count, shift_y : shift_y + col_count]
            for shift_x in range(3)
            for shift_y in range(3)
        ],
        axis=1,
    ).reshape(slice_count, -1, pixels)
    taps_in = columns.shape[1]
    w1 = w_first.reshape(taps_in, width).T
    wl = w_last.reshape(-1, width)
    outs = wl.shape[0]
    chunk = 1536
    full = lambda z, n: (0, 0)
    q = pl.pallas_call(
        net_kernel,
        grid=(slice_count, pixels // chunk),
        in_specs=[
            pl.BlockSpec((1, taps_in, chunk), lambda z, n: (z, 0, n)),
            pl.BlockSpec((width, taps_in), full),
            pl.BlockSpec((width, 1), full),
            pl.BlockSpec((width, width), full),
            pl.BlockSpec((width, 1), full),
            pl.BlockSpec((width, width), full),
            pl.BlockSpec((width, 1), full),
            pl.BlockSpec((outs, width), full),
        ],
        out_specs=pl.BlockSpec((1, chunk // col_count, outs, col_count), lambda z, n: (z, n, 0, 0)),
        out_shape=jax.ShapeDtypeStruct((slice_count, row_count, outs, col_count), jnp.float32),
    )(
        columns,
        w1,
        b_first.reshape(width, 1),
        w_second.T,
        b_second.reshape(width, 1),
        w_third.T,
        b_third.reshape(width, 1),
        wl,
    )
    q = jnp.pad(q, ((0, 0), (1, 1), (0, 0), (1, 1)))
    score_field = jnp.zeros((slice_count, row_count, 2, col_count), jnp.float32)
    for shift_x in range(3):
        for shift_y in range(3):
            tap = (shift_x * 3 + shift_y) * 2
            score_field = score_field + q[
                :, shift_x : shift_x + row_count, tap : tap + 2, shift_y : shift_y + col_count
            ]
    score_field = jnp.transpose(score_field, (0, 2, 1, 3))
    return score_field


def slab_slices(image):
    return lax.all_gather(image, "coil", axis=0, tiled=True)


def on_device(
    image,
    noise,
    sens,
    measured,
    mask,
    w_first,
    b_first,
    w_second,
    b_second,
    w_third,
    b_third,
    w_last,
):
    window = with_halo(image.astype(jnp.bfloat16), ((("slab", "coil"), 0),), 2)
    score_field = score_net(window, w_first, b_first, w_second, b_second, w_third, b_third, w_last)
    planes_in = lax.all_to_all(slab_slices(image), "slab", split_axis=2, concat_axis=0, tiled=True)
    planes = jnp.transpose(planes_in, (1, 2, 3, 0))
    partial_sum = coil_adjoint(planes, sens, measured, mask)
    by_depth = jnp.transpose(partial_sum, (3, 0, 1, 2))
    slab_part = lax.all_to_all(
        by_depth.astype(jnp.bfloat16), "slab", split_axis=0, concat_axis=2, tiled=True
    ).astype(by_depth.dtype)
    gradient = lax.psum_scatter(
        slab_part.astype(jnp.bfloat16), "coil", scatter_dimension=0, tiled=True
    ).astype(jnp.float32)
    return image + STEP_SIZE * (score_field - gradient) + noise


def solution(mesh):
    in_specs = (
        P(("slab", "coil"), None, None, None),
        P(("slab", "coil"), None, None, None),
        P("coil", None, "slab", None, None),
        P("coil", None, "slab", None, None),
        P(),
        P(),
        P(),
        P(),
        P(),
        P(),
        P(),
        P(),
    )
    out_specs = P(("slab", "coil"), None, None, None)
    return jax.shard_map(
        on_device, mesh=mesh, in_specs=in_specs, out_specs=out_specs, check_vma=False
    )
```

profile of v0, /device:TPU:1, one launch (start us, length us, event | category | flops | bytes accessed | tf_op | source)
XLA Modules:
  0.0 126.7 jit_solution(11315243106816783987)
XLA Ops:
  6.6 1.0 convert_element_type.40
  7.6 4.9 %collective-permute-start = (bf16[2,2,32,384]{3,2,1,0:T(8,128)(2,1)S(1)}, bf16[2,2,32,384]{3,2,1,0:T(8,128)(2,1)S(1)}, u32[]{:S(2)}, u32[]{:S(2)}) collective-permute-start(bf16[2,2,32,384]{3,2,1,0:T(8,128)(2,1)S(1)} %convert_element_type.40), channel_id=1, source_target_pairs={{0,1},{1,2},{2,3},{3,4},{4,5},{5,6},{6,7},{7,8},{8,9},{9,10},{10,1... | collective-permute-start | bytes 294920 | tf_op jit(solution)/shard_map/ppermute | solution.py:18
  12.6 1.9 %collective-permute-start.1 = (bf16[2,2,32,384]{3,2,1,0:T(8,128)(2,1)S(1)}, bf16[2,2,32,384]{3,2,1,0:T(8,128)(2,1)S(1)}, u32[]{:S(2)}, u32[]{:S(2)}) collective-permute-start(bf16[2,2,32,384]{3,2,1,0:T(8,128)(2,1)S(1)} %convert_element_type.40), channel_id=1, source_target_pairs={{1,0},{2,1},{3,2},{4,3},{5,4},{6,5},{7,6},{8,7},{9,8},{10,9},{11,1... | collective-permute-start | bytes 294920 | tf_op jit(solution)/shard_map/ppermute | solution.py:19
  14.5 9.6 %all_gather.3 = f32[8,2,32,384]{3,2,1,0:T(8,128)S(1)} all-gather(f32[2,2,32,384]{3,2,1,0:T(8,128)} %param.12), channel_id=1, replica_groups=mesh['slab'=32,'coil'=4] {'coil'}, dimensions={0}, use_global_device_ids=true | all-gather | bytes 983040 | tf_op jit(solution)/shard_map/all_gather | solution.py:186
  24.1 1.4 %copy.87 = f32[8,2,32,384]{3,0,1,2:T(8,128)} copy(f32[8,2,32,384]{3,2,1,0:T(8,128)S(1)} %all_gather.3) | data formatting | bytes 1572864 | tf_op jit(solution)/shard_map/all_gather | solution.py:186
  25.5 10.1 %all-to-all-start = ((f32[8,2,32,384]{3,0,1,2:T(8,128)}), f32[8,2,32,384]{3,0,1,2:T(8,128)S(1)}, u32[]{:S(2)}, u32[]{:S(2)}) async-start(f32[8,2,32,384]{3,0,1,2:T(8,128)} %copy.87), calls=%async_computation | async-start | bytes 1572864 | tf_op jit(solution)/shard_map/all_to_all | solution.py:205
  35.6 2.6 %multiply_convert_fusion = (bf16[384,384]{1,0:T(8,128)(2,1)S(1)}, bf16[384,384]{1,0:T(8,128)(2,1)S(1)}) fusion(), kind=kLoop, calls=%fused_computation.21 | loop fusion | flops 1916928 | bytes 589824 | tf_op jit(solution)/shard_map/convert_element_type | solution.py:31
  38.2 1.1 multiply_convert_fusion.2
  40.0 0.7 copy.84.b1_ref
  40.8 0.7 copy.85.b2_ref
  41.5 0.7 copy.86.b3_ref
  44.3 0.9 pad_maximum_fusion.ty_ref
  46.0 1.1 fusion.5
  47.1 0.9 fusion.6
  48.0 2.3 %all-to-all-done = f32[8,2,32,384]{3,0,1,2:T(8,128)S(1)} async-done(((f32[8,2,32,384]{3,0,1,2:T(8,128)}), f32[8,2,32,384]{3,0,1,2:T(8,128)S(1)}, u32[]{:S(2)}, u32[]{:S(2)}) %all-to-all-start) | async-done | bytes 786464 | tf_op jit(solution)/shard_map/all_to_all | solution.py:205
  50.3 1.2 copy.89
  51.5 13.9 %shard_map.119 = f32[2,1,384,256]{3,2,1,0:T(8,128)} custom-call(f32[2,1,384,256]{3,2,1,0:T(8,128)} %bitcast.34, bf16[4,2,1,384,256]{4,3,2,1,0:T(8,128)(2,1)} %sens_ref.1, bf16[4,2,1,384,256]{4,3,2,1,0:T(8,128)(2,1)} %meas_ref.1, s32[384,256]{1,0:T(8,128)} %mask_ref.1, bf16[768,384]{1,0:T(8,128)(2,1)} %pad_maximum_fusion.ty_ref, ...), custom_call_target="tpu_custom_call" | custom-call | tf_op jit(solution)/shard_map/pallas_call | solution.py:95
  65.4 1.2 convert_bitcast_fusion
  66.6 1.1 copy.90
  67.7 7.0 %all-to-all-start.1 = ((bf16[256,2,1,384]{3,1,2,0:T(2,128)(2,1)}), bf16[256,2,1,384]{3,1,2,0:T(2,128)(2,1)S(1)}, u32[]{:S(2)}, u32[]{:S(2)}) async-start(bf16[256,2,1,384]{3,1,2,0:T(2,128)(2,1)} %copy.90), calls=%async_computation.1 | async-start | bytes 786432 | tf_op jit(solution)/shard_map/all_to_all | solution.py:209
  74.7 1.2 fusion.7
  75.9 1.1 fusion.8
  78.3 6.6 %all-to-all-done.1 = bf16[256,2,1,384]{3,1,2,0:T(2,128)(2,1)S(1)} async-done(((bf16[256,2,1,384]{3,1,2,0:T(2,128)(2,1)}), bf16[256,2,1,384]{3,1,2,0:T(2,128)(2,1)S(1)}, u32[]{:S(2)}, u32[]{:S(2)}) %all-to-all-start.1) | async-done | bytes 393248 | tf_op jit(solution)/shard_map/all_to_all | solution.py:209
  84.9 0.8 copy.92
  87.7 1.0 fusion.9
  88.7 1.1 fusion.10
  89.9 0.9 fusion.11
  90.8 1.2 fusion.12
  92.0 5.2 %reshape.24.x_ref = bf16[2,90,12288]{2,1,0:T(8,128)(2,1)} reshape(bf16[2,90,32,384]{3,2,1,0:T(8,128)(2,1)} %fusion.12) | data formatting | bytes 8847360 | tf_op jit(solution)/shard_map/reshape | solution.py:141
  97.1 16.1 %shard_map.118 = f32[2,32,18,384]{3,2,1,0:T(8,128)} custom-call(bf16[2,90,12288]{2,1,0:T(8,128)(2,1)} %reshape.24.x_ref, bf16[128,90]{1,0:T(8,128)(2,1)} %bitcast.36, f32[128,1]{1,0:T(8,128)} %copy.84.b1_ref, bf16[128,128]{1,0:T(8,128)(2,1)} %bitcast.37, f32[128,1]{1,0:T(8,128)} %copy.85.b2_ref, bf16[128,128]{1,0:T(8,128)(2,1)} %bitcast.38, ...), custom_call_target="tpu_custom_call" | custom-call | tf_op jit(solution)/shard_map/pallas_call | solution.py:148
  113.3 0.9 convert_element_type.49
  114.2 5.0 %fusion.29 = f32[2,2,32,384]{3,1,2,0:T(2,128)S(1)} fusion(f32[2,2,32,384]{3,2,1,0:T(8,128)S(1)} %copy-done.1, f32[2,2,32,384]{3,2,1,0:T(8,128)S(1)} %copy-done, f32[2,2,32,384]{3,2,1,0:T(8,128)S(1)} %convert_element_type.49, f32[2,32,18,384]{3,2,1,0:T(8,128)} %shard_map.118), kind=kLoop, calls=%fused_computation.60 | loop fusion | flops 589824 | bytes 3342336 | tf_op jit(solution)/shard_map/add | solution.py:215
  (43 shorter events, 7.7 us)
Async XLA Ops:
  6.5 39.4 %copy-start = (f32[2,2,32,384]{3,2,1,0:T(8,128)S(1)}, f32[2,2,32,384]{3,2,1,0:T(8,128)}, u32[]{:S(2)}) copy-start(f32[2,2,32,384]{3,2,1,0:T(8,128)} %param.12) | copy-start | bytes 589828
  6.5 32.7 %copy-start.4 = (bf16[3,3,10,128]{3,1,2,0:T(4,128)(2,1)S(1)}, bf16[3,3,10,128]{3,1,2,0:T(4,128)(2,1)}, u32[]{:S(2)}) copy-start(bf16[3,3,10,128]{3,1,2,0:T(4,128)(2,1)} %param.17) | copy-start | bytes 69124
  6.5 33.5 %copy-start.6 = (f32[128]{0:T(128)S(1)}, f32[128]{0:T(128)}, u32[]{:S(2)}) copy-start(f32[128]{0:T(128)} %param.18) | copy-start | bytes 1540
  6.5 34.2 %copy-start.7 = (f32[128]{0:T(128)S(1)}, f32[128]{0:T(128)}, u32[]{:S(2)}) copy-start(f32[128]{0:T(128)} %param.20) | copy-start | bytes 1540
  6.5 35.0 %copy-start.8 = (f32[128]{0:T(128)S(1)}, f32[128]{0:T(128)}, u32[]{:S(2)}) copy-start(f32[128]{0:T(128)} %param.22) | copy-start | bytes 1540
  6.5 35.7 %copy-start.2 = (bf16[128,128]{1,0:T(8,128)(2,1)S(1)}, bf16[128,128]{1,0:T(8,128)(2,1)}, u32[]{:S(2)}) copy-start(bf16[128,128]{1,0:T(8,128)(2,1)} %param.19) | copy-start | bytes 98308
  6.6 36.4 %copy-start.3 = (bf16[128,128]{1,0:T(8,128)(2,1)S(1)}, bf16[128,128]{1,0:T(8,128)(2,1)}, u32[]{:S(2)}) copy-start(bf16[128,128]{1,0:T(8,128)(2,1)} %param.21) | copy-start | bytes 98308
  6.6 37.1 %copy-start.5 = (bf16[3,3,2,128]{3,2,1,0:T(2,128)(2,1)S(1)}, bf16[3,3,2,128]{3,2,1,0:T(2,128)(2,1)}, u32[]{:S(2)}) copy-start(bf16[3,3,2,128]{3,2,1,0:T(2,128)(2,1)} %param.23) | copy-start | bytes 13828
  7.6 38.3 %collective-permute-start = (bf16[2,2,32,384]{3,2,1,0:T(8,128)(2,1)S(1)}, bf16[2,2,32,384]{3,2,1,0:T(8,128)(2,1)S(1)}, u32[]{:S(2)}, u32[]{:S(2)}) collective-permute-start(bf16[2,2,32,384]{3,2,1,0:T(8,128)(2,1)S(1)} %convert_element_type.40), channel_id=1, source_target_pairs={{0,1},{1,2},{2,3},{3,4},{4,5},{5,6},{6,7},{7,8},{8,9},{9,10},{10,1... | collective-permute-start | bytes 294920 | tf_op jit(solution)/shard_map/ppermute | solution.py:18
  12.6 33.4 %collective-permute-start.1 = (bf16[2,2,32,384]{3,2,1,0:T(8,128)(2,1)S(1)}, bf16[2,2,32,384]{3,2,1,0:T(8,128)(2,1)S(1)}, u32[]{:S(2)}, u32[]{:S(2)}) collective-permute-start(bf16[2,2,32,384]{3,2,1,0:T(8,128)(2,1)S(1)} %convert_element_type.40), channel_id=1, source_target_pairs={{1,0},{2,1},{3,2},{4,3},{5,4},{6,5},{7,6},{8,7},{9,8},{10,9},{11,1... | collective-permute-start | bytes 294920 | tf_op jit(solution)/shard_map/ppermute | solution.py:19
  25.5 24.8 %all-to-all-start = ((f32[8,2,32,384]{3,0,1,2:T(8,128)}), f32[8,2,32,384]{3,0,1,2:T(8,128)S(1)}, u32[]{:S(2)}, u32[]{:S(2)}) async-start(f32[8,2,32,384]{3,0,1,2:T(8,128)} %copy.87), calls=%async_computation | async-start | bytes 1572864 | tf_op jit(solution)/shard_map/all_to_all | solution.py:205
  67.7 17.1 %all-to-all-start.1 = ((bf16[256,2,1,384]{3,1,2,0:T(2,128)(2,1)}), bf16[256,2,1,384]{3,1,2,0:T(2,128)(2,1)S(1)}, u32[]{:S(2)}, u32[]{:S(2)}) async-start(bf16[256,2,1,384]{3,1,2,0:T(2,128)(2,1)} %copy.90), calls=%async_computation.1 | async-start | bytes 786432 | tf_op jit(solution)/shard_map/all_to_all | solution.py:209
  74.7 38.6 %reduce-scatter.2.cloned.1.call-start = ((), (), s32[]{:S(2)}) async-start(), calls=%async_computation.3 | async-start | bytes 491520 | tf_op jit(solution)/shard_map/reduce_scatter | solution.py:212
  97.1 17.0 %copy-start.1 = (f32[2,2,32,384]{3,2,1,0:T(8,128)S(1)}, f32[2,2,32,384]{3,2,1,0:T(8,128)}, u32[]{:S(2)}) copy-start(f32[2,2,32,384]{3,2,1,0:T(8,128)} %param.13) | copy-start | bytes 589828
Sparse Core Ops, SparseCore 0:
  85.8 16.2 reduce-scatter.1
where the time goes:
time: 129 us; the launch traced here: 127 us
  Pallas kernels  30 us (23%)
  local copies, waits for them, and re-layouts  25.3 us (20%)
  starting transfers between devices  23.9 us (19%)
  other arithmetic  15.4 us (12%)
  between operations  13.6 us (11%)
  blocking collectives  9.63 us (7%)
  waiting for transfers between devices  8.84 us (7%)
    pallas_call x1, Pallas kernels, score_net(): pl.pallas_call(net_kernel, grid=(slice_count, pixels // chunk), in_specs=...  16.1 us
    pallas_call x1, Pallas kernels, coil_adjoint(): pl.pallas_call(adjoint_kernel, grid=(coils,), in_specs=[pl.BlockSpec((2,...  13.9 us
    unnamed x31, local copies, waits for them, and re-layouts  10.1 us
    all_to_all x1, starting transfers between devices, on_device(): lax.all_to_all(slab_slices(image), 'slab', split_axis=2, concat_axis=0, t...  10.1 us
    all_gather x1, blocking collectives, slab_slices(): return lax.all_gather(image, 'coil', axis=0, tiled=True)  9.63 us
    all_to_all x1, starting transfers between devices, on_device(): lax.all_to_all(by_depth.astype(jnp.bfloat16), 'slab', split_axis=0, conca...  6.98 us
    all_to_all x1, waiting for transfers between devices, on_device(): lax.all_to_all(by_depth.astype(jnp.bfloat16), 'slab', split_axis=0, conca...  6.56 us
    reshape x1, local copies, waits for them, and re-layouts, score_net(): columns = jnp.concatenate([framed[:, :, shift_x:shift_x + row_count, shif...  5.18 us
  transfers between devices with their start and end apart: 5, of which 2 were waited for; matrix products, arithmetic and copies ran while one was open for 23% of the time, Pallas kernels for 13%

commit v1 on v0

--- a/solution.py
+++ b/solution.py
@@ -202,15 +202,19 @@
 ):
     window = with_halo(image.astype(jnp.bfloat16), ((("slab", "coil"), 0),), 2)
     score_field = score_net(window, w_first, b_first, w_second, b_second, w_third, b_third, w_last)
-    planes_in = lax.all_to_all(slab_slices(image), "slab", split_axis=2, concat_axis=0, tiled=True)
-    planes = jnp.transpose(planes_in, (1, 2, 3, 0))
-    partial_sum = coil_adjoint(planes, sens, measured, mask)
-    by_depth = jnp.transpose(partial_sum, (3, 0, 1, 2))
-    slab_part = lax.all_to_all(
-        by_depth.astype(jnp.bfloat16), "slab", split_axis=0, concat_axis=2, tiled=True
-    ).astype(by_depth.dtype)
-    gradient = lax.psum_scatter(
-        slab_part.astype(jnp.bfloat16), "coil", scatter_dimension=0, tiled=True
+    slabs = lax.axis_size("slab")
+    groups = lax.axis_size("coil")
+    depth, parts, _, lines = image.shape
+    sent = lax.all_to_all(image, "slab", split_axis=2, concat_axis=0, tiled=True)
+    gathered = lax.all_gather(sent, "coil", axis=0, tiled=False)
+    gathered = gathered.reshape(groups, slabs, depth, parts, 1, lines)
+    planes = jnp.transpose(gathered, (3, 4, 5, 1, 0, 2)).reshape(parts, 1, lines, -1)
+    partial_sum = coil_adjoint(planes, sens, measured, mask).astype(jnp.bfloat16)
+    partial_sum = partial_sum.reshape(parts, 1, lines, slabs, groups, depth)
+    by_group = jnp.transpose(partial_sum, (4, 3, 5, 0, 1, 2)).reshape(-1, parts, 1, lines)
+    group_sum = lax.psum_scatter(by_group, "coil", scatter_dimension=0, tiled=True)
+    gradient = lax.all_to_all(
+        group_sum, "slab", split_axis=0, concat_axis=2, tiled=True
     ).astype(jnp.float32)
     return image + STEP_SIZE * (score_field - gradient) + noise
 

time: 129 us -> 141 us (1.093); the launches traced: 127 us -> 140 us
  local copies, waits for them, and re-layouts: 25.3 us -> 32.6 us
  waiting for transfers between devices: 8.84 us -> 14.8 us
  starting transfers between devices: 23.9 us -> 26.3 us
    unnamed x1 -> x2, waiting for transfers between devices: 0.02 us -> 14.8 us
    all_to_all x2, waiting for transfers between devices: 8.82 us -> 0.01 us  [the longest x1 0.01 us: on_device(): lax.all_to_all(image, 'slab', split_axis=2, concat_axis=0, tiled=True)]
    unnamed x31 -> x20, local copies, waits for them, and re-layouts: 10.1 us -> 16.5 us
    all_to_all x2, starting transfers between devices: 17 us -> 19.4 us  [the longest x1 10.1 us: on_device(): lax.all_to_all(image, 'slab', split_axis=2, concat_axis=0, tiled=True)]
    all_to_all x4 -> x0, local copies, waits for them, and re-layouts: 2.06 us -> none  [the longest x2 1.22 us: on_device(): lax.all_to_all(slab_slices(image), 'slab', split_axis=2, concat_axis=0, t...]
  transfers between devices with their start and end apart: 5 -> 5, of which waited for: 2 -> 1; matrix products, arithmetic and copies ran while one was open for 23% -> 24% of each run, Pallas kernels for 13% -> 11%
where the time goes in v1:
time: 141 us; the launch traced here: 140 us
  local copies, waits for them, and re-layouts  32.6 us (23%)
  Pallas kernels  30 us (21%)
  starting transfers between devices  26.3 us (19%)
  waiting for transfers between devices  14.8 us (10%)
  other arithmetic  14.3 us (10%)
  between operations  13.6 us (10%)
  blocking collectives  8.76 us (6%)
    unnamed x20, local copies, waits for them, and re-layouts  16.5 us
    pallas_call x1, Pallas kernels, score_net(): pl.pallas_call(net_kernel, grid=(slice_count, pixels // chunk), in_specs=...  16.1 us
    unnamed x2, waiting for transfers between devices  14.8 us
    pallas_call x1, Pallas kernels, coil_adjoint(): pl.pallas_call(adjoint_kernel, grid=(coils,), in_specs=[pl.BlockSpec((2,...  13.9 us
    all_to_all x1, starting transfers between devices, on_device(): lax.all_to_all(image, 'slab', split_axis=2, concat_axis=0, tiled=True)  10.1 us
    all_to_all x1, starting transfers between devices, on_device(): lax.all_to_all(group_sum, 'slab', split_axis=0, concat_axis=2, tiled=True)  9.31 us
    all_gather x1, blocking collectives, on_device(): gathered = lax.all_gather(sent, 'coil', axis=0, tiled=False)  8.76 us
    reshape x1, local copies, waits for them, and re-layouts, score_net(): columns = jnp.concatenate([framed[:, :, shift_x:shift_x + row_count, shif...  5.12 us
  transfers between devices with their start and end apart: 5, of which 1 were waited for; matrix products, arithmetic and copies ran while one was open for 24% of the time, Pallas kernels for 11%

profile of v1, /device:TPU:1, one launch (start us, length us, event | category | flops | bytes accessed | tf_op | source)
XLA Modules:
  0.0 140.2 jit_solution(9971377812979405926)
XLA Ops:
  6.5 1.0 convert_element_type.44
  7.6 4.9 %collective-permute-start = (bf16[2,2,32,384]{3,2,1,0:T(8,128)(2,1)S(1)}, bf16[2,2,32,384]{3,2,1,0:T(8,128)(2,1)S(1)}, u32[]{:S(2)}, u32[]{:S(2)}) collective-permute-start(bf16[2,2,32,384]{3,2,1,0:T(8,128)(2,1)S(1)} %convert_element_type.44), channel_id=1, source_target_pairs={{0,1},{1,2},{2,3},{3,4},{4,5},{5,6},{6,7},{7,8},{8,9},{9,10},{10,1... | collective-permute-start | bytes 294920 | tf_op jit(solution)/shard_map/ppermute | solution.py:18
  12.5 1.9 %collective-permute-start.1 = (bf16[2,2,32,384]{3,2,1,0:T(8,128)(2,1)S(1)}, bf16[2,2,32,384]{3,2,1,0:T(8,128)(2,1)S(1)}, u32[]{:S(2)}, u32[]{:S(2)}) collective-permute-start(bf16[2,2,32,384]{3,2,1,0:T(8,128)(2,1)S(1)} %convert_element_type.44), channel_id=1, source_target_pairs={{1,0},{2,1},{3,2},{4,3},{5,4},{6,5},{7,6},{8,7},{9,8},{10,9},{11,1... | collective-permute-start | bytes 294920 | tf_op jit(solution)/shard_map/ppermute | solution.py:19
  14.4 1.8 %copy.70 = f32[2,2,32,384]{3,1,0,2:T(2,128)} copy(f32[2,2,32,384]{3,2,1,0:T(8,128)} %param.12) | data formatting | bytes 393216 | tf_op args[0]
  16.2 10.1 %all-to-all-start = ((f32[2,2,32,384]{3,1,0,2:T(2,128)}), f32[2,2,32,384]{3,1,0,2:T(2,128)S(1)}, u32[]{:S(2)}, u32[]{:S(2)}) async-start(f32[2,2,32,384]{3,1,0,2:T(2,128)} %copy.70), calls=%async_computation | async-start | bytes 393216 | tf_op jit(solution)/shard_map/all_to_all | solution.py:208
  26.3 2.6 %multiply_convert_fusion = (bf16[384,384]{1,0:T(8,128)(2,1)S(1)}, bf16[384,384]{1,0:T(8,128)(2,1)S(1)}) fusion(), kind=kLoop, calls=%fused_computation.20 | loop fusion | flops 1916928 | bytes 589824 | tf_op jit(solution)/shard_map/convert_element_type | solution.py:31
  28.9 1.1 multiply_convert_fusion.2
  31.5 1.4 copy.67.b1_ref
  32.9 1.4 copy.68.b2_ref
  34.3 1.4 copy.69.b3_ref
  35.7 1.5 %copy.64 = bf16[128,128]{0,1:T(8,128)(2,1)} copy(bf16[128,128]{1,0:T(8,128)(2,1)} %param.19) | data formatting | bytes 65536 | tf_op args[7]
  37.1 1.5 %copy.65 = bf16[128,128]{0,1:T(8,128)(2,1)} copy(bf16[128,128]{1,0:T(8,128)(2,1)} %param.21) | data formatting | bytes 65536 | tf_op args[9]
  38.6 1.3 reshape.40.wl_ref
  39.9 0.9 pad_maximum_fusion.ty_ref
  41.6 1.1 fusion.5
  42.7 0.9 fusion.6
  43.7 1.2 fusion.7
  44.8 1.0 fusion.8
  47.2 8.8 %all_gather.7 = f32[4,64,2,1,384]{4,1,3,2,0:T(8,128)S(1)} all-gather(f32[1,64,2,1,384]{4,1,3,2,0:T(8,128)S(1)} %copy.71), channel_id=1, replica_groups=mesh['slab'=32,'coil'=4] {'coil'}, dimensions={0}, use_global_device_ids=true | all-gather | bytes 983040 | tf_op jit(solution)/shard_map/all_gather | solution.py:209
  56.9 1.2 copy.74.planes_ref
  58.1 13.9 %shard_map.119 = f32[2,1,384,256]{3,2,1,0:T(8,128)} custom-call(f32[2,1,384,256]{3,2,1,0:T(8,128)} %copy.74.planes_ref, bf16[4,2,1,384,256]{4,3,2,1,0:T(8,128)(2,1)} %sens_ref.1, bf16[4,2,1,384,256]{4,3,2,1,0:T(8,128)(2,1)} %meas_ref.1, s32[384,256]{1,0:T(8,128)} %mask_ref.1, bf16[768,384]{1,0:T(8,128)(2,1)} %pad_maximum_fusion.ty_ref, ...), custom_call_target="tpu_custom_call" | custom-call | tf_op jit(solution)/shard_map/pallas_call | solution.py:95
  72.0 1.2 convert_element_type.51
  76.7 1.0 fusion.9
  77.8 1.2 fusion.10
  78.9 0.9 fusion.11
  79.8 14.8 %reduce-scatter.5.cloned.1.call-done = bf16[64,768]{1,0:T(8,128)(2,1)} async-done(((bf16[256,768]{1,0:T(8,128)(2,1)}), bf16[64,768]{1,0:T(8,128)(2,1)}) %reduce-scatter.5.cloned.1.call-update) | async-done | bytes 98320
  94.6 1.6 %reshape.48 = bf16[64,1,2,384]{3,2,1,0:T(2,128)(2,1)} reshape(bf16[64,768]{1,0:T(8,128)(2,1)} %reduce-scatter.5.cloned.1.call-done) | data formatting | bytes 196608
  96.2 9.3 %all-to-all-start.1 = ((bf16[64,2,1,384]{3,1,2,0:T(2,128)(2,1)}), bf16[64,2,1,384]{3,1,2,0:T(2,128)(2,1)S(1)}, u32[]{:S(2)}, u32[]{:S(2)}) async-start(bf16[64,2,1,384]{3,1,2,0:T(2,128)(2,1)} %bitcast.25), calls=%async_computation.1 | async-start | bytes 196608 | tf_op jit(solution)/shard_map/all_to_all | solution.py:216
  105.5 1.2 fusion.12
  106.7 5.1 %reshape.49.x_ref = bf16[2,90,12288]{2,1,0:T(8,128)(2,1)} reshape(bf16[2,90,32,384]{3,2,1,0:T(8,128)(2,1)} %fusion.12) | data formatting | bytes 8847360 | tf_op jit(solution)/shard_map/reshape | solution.py:141
  111.8 16.1 %shard_map.118 = f32[2,32,18,384]{3,2,1,0:T(8,128)} custom-call(bf16[2,90,12288]{2,1,0:T(8,128)(2,1)} %reshape.49.x_ref, bf16[128,90]{1,0:T(8,128)(2,1)} %bitcast.57, f32[128,1]{1,0:T(8,128)} %copy.67.b1_ref, bf16[128,128]{1,0:T(8,128)(2,1)} %bitcast.58, f32[128,1]{1,0:T(8,128)} %copy.68.b2_ref, bf16[128,128]{1,0:T(8,128)(2,1)} %bitcast.59, ...), custom_call_target="tpu_custom_call" | custom-call | tf_op jit(solution)/shard_map/pallas_call | solution.py:148
  127.9 4.8 %fusion.29 = f32[2,2,32,384]{3,1,2,0:T(2,128)S(1)} fusion(f32[2,2,32,384]{3,2,1,0:T(8,128)S(1)} %copy-done.1, f32[2,2,32,384]{3,2,1,0:T(8,128)S(1)} %copy-done, f32[2,32,18,384]{3,2,1,0:T(8,128)} %shard_map.118, bf16[32,2,2,1,384]{4,2,1,0,3:T(2,128)(2,1)S(1)} %bitcast.56), kind=kLoop, calls=%fused_computation.57 | loop fusion | flops 638976 | bytes 3244032 | tf_op jit(solution)/shard_map/add | solution.py:219
  (31 shorter events, 8.8 us)
Async XLA Ops:
  6.5 35.0 %copy-start = (f32[2,2,32,384]{3,2,1,0:T(8,128)S(1)}, f32[2,2,32,384]{3,2,1,0:T(8,128)}, u32[]{:S(2)}) copy-start(f32[2,2,32,384]{3,2,1,0:T(8,128)} %param.12) | copy-start | bytes 589828
  7.6 34.0 %collective-permute-start = (bf16[2,2,32,384]{3,2,1,0:T(8,128)(2,1)S(1)}, bf16[2,2,32,384]{3,2,1,0:T(8,128)(2,1)S(1)}, u32[]{:S(2)}, u32[]{:S(2)}) collective-permute-start(bf16[2,2,32,384]{3,2,1,0:T(8,128)(2,1)S(1)} %convert_element_type.44), channel_id=1, source_target_pairs={{0,1},{1,2},{2,3},{3,4},{4,5},{5,6},{6,7},{7,8},{8,9},{9,10},{10,1... | collective-permute-start | bytes 294920 | tf_op jit(solution)/shard_map/ppermute | solution.py:18
  12.5 29.1 %collective-permute-start.1 = (bf16[2,2,32,384]{3,2,1,0:T(8,128)(2,1)S(1)}, bf16[2,2,32,384]{3,2,1,0:T(8,128)(2,1)S(1)}, u32[]{:S(2)}, u32[]{:S(2)}) collective-permute-start(bf16[2,2,32,384]{3,2,1,0:T(8,128)(2,1)S(1)} %convert_element_type.44), channel_id=1, source_target_pairs={{1,0},{2,1},{3,2},{4,3},{5,4},{6,5},{7,6},{8,7},{9,8},{10,9},{11,1... | collective-permute-start | bytes 294920 | tf_op jit(solution)/shard_map/ppermute | solution.py:19
  16.2 31.0 %all-to-all-start = ((f32[2,2,32,384]{3,1,0,2:T(2,128)}), f32[2,2,32,384]{3,1,0,2:T(2,128)S(1)}, u32[]{:S(2)}, u32[]{:S(2)}) async-start(f32[2,2,32,384]{3,1,0,2:T(2,128)} %copy.70), calls=%async_computation | async-start | bytes 393216 | tf_op jit(solution)/shard_map/all_to_all | solution.py:208
  26.2 68.4 %reduce-scatter.5.cloned.1.call-start = ((), (), s32[]{:S(2)}) async-start(), calls=%async_computation.3 | async-start | bytes 491520
  96.2 31.8 %all-to-all-start.1 = ((bf16[64,2,1,384]{3,1,2,0:T(2,128)(2,1)}), bf16[64,2,1,384]{3,1,2,0:T(2,128)(2,1)S(1)}, u32[]{:S(2)}, u32[]{:S(2)}) async-start(bf16[64,2,1,384]{3,1,2,0:T(2,128)(2,1)} %bitcast.25), calls=%async_computation.1 | async-start | bytes 196608 | tf_op jit(solution)/shard_map/all_to_all | solution.py:216
  111.8 16.1 %copy-start.1 = (f32[2,2,32,384]{3,2,1,0:T(8,128)S(1)}, f32[2,2,32,384]{3,2,1,0:T(8,128)}, u32[]{:S(2)}) copy-start(f32[2,2,32,384]{3,2,1,0:T(8,128)} %param.13) | copy-start | bytes 589828
Sparse Core Ops, SparseCore 0:
  74.9 19.6 reduce-scatter.4

commit v2 on v1

--- a/solution.py
+++ b/solution.py
@@ -209,12 +209,11 @@
     gathered = lax.all_gather(sent, "coil", axis=0, tiled=False)
     gathered = gathered.reshape(groups, slabs, depth, parts, 1, lines)
     planes = jnp.transpose(gathered, (3, 4, 5, 1, 0, 2)).reshape(parts, 1, lines, -1)
-    partial_sum = coil_adjoint(planes, sens, measured, mask).astype(jnp.bfloat16)
-    partial_sum = partial_sum.reshape(parts, 1, lines, slabs, groups, depth)
-    by_group = jnp.transpose(partial_sum, (4, 3, 5, 0, 1, 2)).reshape(-1, parts, 1, lines)
-    group_sum = lax.psum_scatter(by_group, "coil", scatter_dimension=0, tiled=True)
-    gradient = lax.all_to_all(
-        group_sum, "slab", split_axis=0, concat_axis=2, tiled=True
+    partial_sum = coil_adjoint(planes, sens, measured, mask)
+    by_depth = jnp.transpose(partial_sum, (3, 0, 1, 2)).astype(jnp.bfloat16)
+    slab_part = lax.all_to_all(by_depth, "slab", split_axis=0, concat_axis=2, tiled=True)
+    gradient = lax.psum_scatter(
+        slab_part, "coil", scatter_dimension=0, tiled=True
     ).astype(jnp.float32)
     return image + STEP_SIZE * (score_field - gradient) + noise
 

time: 141 us -> 135 us (0.957)
  waiting for transfers between devices: 14.8 us -> 7.27 us
    unnamed x2 -> x1, waiting for transfers between devices: 14.8 us -> 0.02 us
    all_to_all x1, waiting for transfers between devices: 0.01 us -> 7.24 us  [on_device(): lax.all_to_all(by_depth, 'slab', split_axis=0, concat_axis=2, tiled=True)]
    unnamed x20 -> x18, local copies, waits for them, and re-layouts: 16.5 us -> 14.1 us
  transfers between devices with their start and end apart: 5 -> 5, of which waited for: 1 -> 1; matrix products, arithmetic and copies ran while one was open for 24% -> 25% of each run, Pallas kernels for 11% -> 12%
where the time goes in v2:
time: 135 us; the launch traced here: 133 us
  local copies, waits for them, and re-layouts  31.5 us (23%)
  Pallas kernels  30 us (22%)
  starting transfers between devices  27.3 us (20%)
  other arithmetic  15.2 us (11%)
  between operations  13.6 us (10%)
  blocking collectives  8.76 us (6%)
  waiting for transfers between devices  7.27 us (5%)
    pallas_call x1, Pallas kernels, score_net(): pl.pallas_call(net_kernel, grid=(slice_count, pixels // chunk), in_specs=...  16.1 us
    unnamed x18, local copies, waits for them, and re-layouts  14.1 us
    pallas_call x1, Pallas kernels, coil_adjoint(): pl.pallas_call(adjoint_kernel, grid=(coils,), in_specs=[pl.BlockSpec((2,...  13.9 us
    all_to_all x1, starting transfers between devices, on_device(): lax.all_to_all(by_depth, 'slab', split_axis=0, concat_axis=2, tiled=True)  10.1 us
    all_to_all x1, starting transfers between devices, on_device(): lax.all_to_all(image, 'slab', split_axis=2, concat_axis=0, tiled=True)  10.1 us
    all_gather x1, blocking collectives, on_device(): gathered = lax.all_gather(sent, 'coil', axis=0, tiled=False)  8.76 us
    all_to_all x1, waiting for transfers between devices, on_device(): lax.all_to_all(by_depth, 'slab', split_axis=0, concat_axis=2, tiled=True)  7.24 us
    reshape x1, local copies, waits for them, and re-layouts, score_net(): columns = jnp.concatenate([framed[:, :, shift_x:shift_x + row_count, shif...  5.12 us
  transfers between devices with their start and end apart: 5, of which 1 were waited for; matrix products, arithmetic and copies ran while one was open for 25% of the time, Pallas kernels for 12%

profile of v2, /device:TPU:1, one launch (start us, length us, event | category | flops | bytes accessed | tf_op | source)
XLA Modules:
  0.0 133.5 jit_solution(15769363123419853995)
XLA Ops:
  6.5 1.0 convert_element_type.38
  7.6 4.9 %collective-permute-start = (bf16[2,2,32,384]{3,2,1,0:T(8,128)(2,1)S(1)}, bf16[2,2,32,384]{3,2,1,0:T(8,128)(2,1)S(1)}, u32[]{:S(2)}, u32[]{:S(2)}) collective-permute-start(bf16[2,2,32,384]{3,2,1,0:T(8,128)(2,1)S(1)} %convert_element_type.38), channel_id=1, source_target_pairs={{0,1},{1,2},{2,3},{3,4},{4,5},{5,6},{6,7},{7,8},{8,9},{9,10},{10,1... | collective-permute-start | bytes 294920 | tf_op jit(solution)/shard_map/ppermute | solution.py:18
  12.5 1.9 %collective-permute-start.1 = (bf16[2,2,32,384]{3,2,1,0:T(8,128)(2,1)S(1)}, bf16[2,2,32,384]{3,2,1,0:T(8,128)(2,1)S(1)}, u32[]{:S(2)}, u32[]{:S(2)}) collective-permute-start(bf16[2,2,32,384]{3,2,1,0:T(8,128)(2,1)S(1)} %convert_element_type.38), channel_id=1, source_target_pairs={{1,0},{2,1},{3,2},{4,3},{5,4},{6,5},{7,6},{8,7},{9,8},{10,9},{11,1... | collective-permute-start | bytes 294920 | tf_op jit(solution)/shard_map/ppermute | solution.py:19
  14.4 1.8 %copy.91 = f32[2,2,32,384]{3,1,0,2:T(2,128)} copy(f32[2,2,32,384]{3,2,1,0:T(8,128)} %param.12) | data formatting | bytes 393216 | tf_op args[0]
  16.2 10.1 %all-to-all-start = ((f32[2,2,32,384]{3,1,0,2:T(2,128)}), f32[2,2,32,384]{3,1,0,2:T(2,128)S(1)}, u32[]{:S(2)}, u32[]{:S(2)}) async-start(f32[2,2,32,384]{3,1,0,2:T(2,128)} %copy.91), calls=%async_computation | async-start | bytes 393216 | tf_op jit(solution)/shard_map/all_to_all | solution.py:208
  26.2 2.6 %multiply_convert_fusion = (bf16[384,384]{1,0:T(8,128)(2,1)S(1)}, bf16[384,384]{1,0:T(8,128)(2,1)S(1)}) fusion(), kind=kLoop, calls=%fused_computation.20 | loop fusion | flops 1916928 | bytes 589824 | tf_op jit(solution)/shard_map/convert_element_type | solution.py:31
  28.8 1.1 multiply_convert_fusion.2
  31.5 1.4 %copy.88.b1_ref = f32[128,1]{1,0:T(8,128)} copy(f32[128,1]{0,1:T(1,128)} %bitcast.41) | data formatting | bytes 1024 | tf_op jit(solution)/shard_map/reshape | solution.py:166
  32.9 1.4 %copy.89.b2_ref = f32[128,1]{1,0:T(8,128)} copy(f32[128,1]{0,1:T(1,128)} %bitcast.42) | data formatting | bytes 1024 | tf_op jit(solution)/shard_map/reshape | solution.py:168
  34.2 1.4 %copy.90.b3_ref = f32[128,1]{1,0:T(8,128)} copy(f32[128,1]{0,1:T(1,128)} %bitcast.43) | data formatting | bytes 1024 | tf_op jit(solution)/shard_map/reshape | solution.py:170
  35.6 1.5 %copy.85 = bf16[128,128]{0,1:T(8,128)(2,1)} copy(bf16[128,128]{1,0:T(8,128)(2,1)} %param.19) | data formatting | bytes 65536 | tf_op args[7]
  37.1 1.5 %copy.86 = bf16[128,128]{0,1:T(8,128)(2,1)} copy(bf16[128,128]{1,0:T(8,128)(2,1)} %param.21) | data formatting | bytes 65536 | tf_op args[9]
  38.6 1.3 reshape.30.wl_ref
  41.6 1.1 fusion.5
  42.7 0.9 fusion.6
  43.7 8.8 %all_gather.7 = f32[4,64,2,1,384]{4,1,3,2,0:T(8,128)S(1)} all-gather(f32[1,64,2,1,384]{4,1,3,2,0:T(8,128)S(1)} %copy.92), channel_id=1, replica_groups=mesh['slab'=32,'coil'=4] {'coil'}, dimensions={0}, use_global_device_ids=true | all-gather | bytes 983040 | tf_op jit(solution)/shard_map/all_gather | solution.py:209
  53.3 1.2 copy.95.planes_ref
  54.5 13.9 %shard_map.119 = f32[2,1,384,256]{3,2,1,0:T(8,128)} custom-call(f32[2,1,384,256]{3,2,1,0:T(8,128)} %copy.95.planes_ref, bf16[4,2,1,384,256]{4,3,2,1,0:T(8,128)(2,1)} %sens_ref.1, bf16[4,2,1,384,256]{4,3,2,1,0:T(8,128)(2,1)} %meas_ref.1, s32[384,256]{1,0:T(8,128)} %mask_ref.1, bf16[768,384]{1,0:T(8,128)(2,1)} %pad_maximum_fusion.ty_ref, ...), custom_call_target="tpu_custom_call" | custom-call | tf_op jit(solution)/shard_map/pallas_call | solution.py:95
  68.4 1.2 convert_bitcast_fusion
  69.6 1.1 copy.96
  70.7 10.1 %all-to-all-start.1 = ((bf16[256,2,1,384]{3,1,2,0:T(2,128)(2,1)}), bf16[256,2,1,384]{3,1,2,0:T(2,128)(2,1)S(1)}, u32[]{:S(2)}, u32[]{:S(2)}) async-start(bf16[256,2,1,384]{3,1,2,0:T(2,128)(2,1)} %copy.96), calls=%async_computation.1 | async-start | bytes 786432 | tf_op jit(solution)/shard_map/all_to_all | solution.py:214
  81.0 1.2 fusion.7
  82.2 1.0 fusion.8
  84.6 7.2 %all-to-all-done.1 = bf16[256,2,1,384]{3,1,2,0:T(2,128)(2,1)S(1)} async-done(((bf16[256,2,1,384]{3,1,2,0:T(2,128)(2,1)}), bf16[256,2,1,384]{3,1,2,0:T(2,128)(2,1)S(1)}, u32[]{:S(2)}, u32[]{:S(2)}) %all-to-all-start.1) | async-done | bytes 393248 | tf_op jit(solution)/shard_map/all_to_all | solution.py:214
  94.7 1.0 fusion.9
  95.7 1.2 fusion.10
  96.9 0.9 fusion.11
  97.8 1.2 fusion.12
  99.0 5.1 %reshape.33.x_ref = bf16[2,90,12288]{2,1,0:T(8,128)(2,1)} reshape(bf16[2,90,32,384]{3,2,1,0:T(8,128)(2,1)} %fusion.12) | data formatting | bytes 8847360 | tf_op jit(solution)/shard_map/reshape | solution.py:141
  104.2 16.1 %shard_map.118 = f32[2,32,18,384]{3,2,1,0:T(8,128)} custom-call(bf16[2,90,12288]{2,1,0:T(8,128)(2,1)} %reshape.33.x_ref, bf16[128,90]{1,0:T(8,128)(2,1)} %bitcast.38, f32[128,1]{1,0:T(8,128)} %copy.88.b1_ref, bf16[128,128]{1,0:T(8,128)(2,1)} %bitcast.39, f32[128,1]{1,0:T(8,128)} %copy.89.b2_ref, bf16[128,128]{1,0:T(8,128)(2,1)} %bitcast.40, ...), custom_call_target="tpu_custom_call" | custom-call | tf_op jit(solution)/shard_map/pallas_call | solution.py:148
  120.2 0.9 convert_element_type.47
  121.2 4.8 %fusion.29 = f32[2,2,32,384]{3,1,2,0:T(2,128)S(1)} fusion(f32[2,2,32,384]{3,2,1,0:T(8,128)S(1)} %copy-done.1, f32[2,2,32,384]{3,2,1,0:T(8,128)S(1)} %copy-done, f32[2,2,32,384]{3,2,1,0:T(8,128)S(1)} %convert_element_type.47, f32[2,32,18,384]{3,2,1,0:T(8,128)} %shard_map.118), kind=kLoop, calls=%fused_computation.59 | loop fusion | flops 589824 | bytes 3342336 | tf_op jit(solution)/shard_map/add | solution.py:218
  (31 shorter events, 9.2 us)
Async XLA Ops:
  6.5 35.0 %copy-start = (f32[2,2,32,384]{3,2,1,0:T(8,128)S(1)}, f32[2,2,32,384]{3,2,1,0:T(8,128)}, u32[]{:S(2)}) copy-start(f32[2,2,32,384]{3,2,1,0:T(8,128)} %param.12) | copy-start | bytes 589828
  7.6 33.9 %collective-permute-start = (bf16[2,2,32,384]{3,2,1,0:T(8,128)(2,1)S(1)}, bf16[2,2,32,384]{3,2,1,0:T(8,128)(2,1)S(1)}, u32[]{:S(2)}, u32[]{:S(2)}) collective-permute-start(bf16[2,2,32,384]{3,2,1,0:T(8,128)(2,1)S(1)} %convert_element_type.38), channel_id=1, source_target_pairs={{0,1},{1,2},{2,3},{3,4},{4,5},{5,6},{6,7},{7,8},{8,9},{9,10},{10,1... | collective-permute-start | bytes 294920 | tf_op jit(solution)/shard_map/ppermute | solution.py:18
  12.5 29.1 %collective-permute-start.1 = (bf16[2,2,32,384]{3,2,1,0:T(8,128)(2,1)S(1)}, bf16[2,2,32,384]{3,2,1,0:T(8,128)(2,1)S(1)}, u32[]{:S(2)}, u32[]{:S(2)}) collective-permute-start(bf16[2,2,32,384]{3,2,1,0:T(8,128)(2,1)S(1)} %convert_element_type.38), channel_id=1, source_target_pairs={{1,0},{2,1},{3,2},{4,3},{5,4},{6,5},{7,6},{8,7},{9,8},{10,9},{11,1... | collective-permute-start | bytes 294920 | tf_op jit(solution)/shard_map/ppermute | solution.py:19
  16.2 27.5 %all-to-all-start = ((f32[2,2,32,384]{3,1,0,2:T(2,128)}), f32[2,2,32,384]{3,1,0,2:T(2,128)S(1)}, u32[]{:S(2)}, u32[]{:S(2)}) async-start(f32[2,2,32,384]{3,1,0,2:T(2,128)} %copy.91), calls=%async_computation | async-start | bytes 393216 | tf_op jit(solution)/shard_map/all_to_all | solution.py:208
  70.7 21.1 %all-to-all-start.1 = ((bf16[256,2,1,384]{3,1,2,0:T(2,128)(2,1)}), bf16[256,2,1,384]{3,1,2,0:T(2,128)(2,1)S(1)}, u32[]{:S(2)}, u32[]{:S(2)}) async-start(bf16[256,2,1,384]{3,1,2,0:T(2,128)(2,1)} %copy.96), calls=%async_computation.1 | async-start | bytes 786432 | tf_op jit(solution)/shard_map/all_to_all | solution.py:214
  80.8 39.4 %reduce-scatter.2.cloned.1.call-start = ((), (), s32[]{:S(2)}) async-start(), calls=%async_computation.3 | async-start | bytes 491520 | tf_op jit(solution)/shard_map/reduce_scatter | solution.py:215
  104.2 17.0 %copy-start.1 = (f32[2,2,32,384]{3,2,1,0:T(8,128)S(1)}, f32[2,2,32,384]{3,2,1,0:T(8,128)}, u32[]{:S(2)}) copy-start(f32[2,2,32,384]{3,2,1,0:T(8,128)} %param.13) | copy-start | bytes 589828
Sparse Core Ops, SparseCore 0:
  92.9 14.9 reduce-scatter.1

commit v3 on v0

--- a/solution.py
+++ b/solution.py
@@ -108,16 +108,28 @@
     )(planes, sens, measured, mask, ty, tz)
 
 
-def net_kernel(x_ref, w1_ref, b1_ref, w2_ref, b2_ref, w3_ref, b3_ref, wl_ref, q_ref):
-    h = jnp.dot(w1_ref[...], x_ref[0], preferred_element_type=jnp.float32) + b1_ref[...]
+def net_kernel(x_ref, p_ref, q_ref):
+    width = p_ref.shape[1] // 4
+    taps_in = x_ref.shape[1]
+    rows = x_ref.shape[2]
+    cols = x_ref.shape[3]
+    outs = q_ref.shape[2]
+    x = jnp.concatenate([x_ref[0, :, row, :] for row in range(rows)], axis=1)
+    w1 = p_ref[:width, 0:taps_in].astype(jnp.bfloat16)
+    w2 = p_ref[:width, width : 2 * width].astype(jnp.bfloat16)
+    w3 = p_ref[:width, 2 * width : 3 * width].astype(jnp.bfloat16)
+    wl = p_ref[width : width + outs, 0:width].astype(jnp.bfloat16)
+    b1 = p_ref[:width, 3 * width : 3 * width + 1]
+    b2 = p_ref[:width, 3 * width + 1 : 3 * width + 2]
+    b3 = p_ref[:width, 3 * width + 2 : 3 * width + 3]
+    h = jnp.dot(w1, x, preferred_element_type=jnp.float32) + b1
     h = jax.nn.silu(h).astype(jnp.bfloat16)
-    h = jnp.dot(w2_ref[...], h, preferred_element_type=jnp.float32) + b2_ref[...]
+    h = jnp.dot(w2, h, preferred_element_type=jnp.float32) + b2
     h = jax.nn.silu(h).astype(jnp.bfloat16)
-    h = jnp.dot(w3_ref[...], h, preferred_element_type=jnp.float32) + b3_ref[...]
+    h = jnp.dot(w3, h, preferred_element_type=jnp.float32) + b3
     h = jax.nn.silu(h).astype(jnp.bfloat16)
-    q = jnp.dot(wl_ref[...], h, preferred_element_type=jnp.float32)
-    cols = q_ref.shape[3]
-    for row in range(q_ref.shape[1]):
+    q = jnp.dot(wl, h, preferred_element_type=jnp.float32)
+    for row in range(rows):
         q_ref[0, row] = q[:, row * cols : (row + 1) * cols]
 
 
@@ -126,7 +138,6 @@
     row_count = window.shape[2]
     col_count = window.shape[3]
     width = w_first.shape[-1]
-    pixels = row_count * col_count
     stacked = jnp.concatenate(
         [window[offset : offset + slice_count] for offset in range(5)], axis=1
     )
@@ -138,38 +149,35 @@
             for shift_y in range(3)
         ],
         axis=1,
-    ).reshape(slice_count, -1, pixels)
+    )
     taps_in = columns.shape[1]
-    w1 = w_first.reshape(taps_in, width).T
     wl = w_last.reshape(-1, width)
     outs = wl.shape[0]
-    chunk = 1536
-    full = lambda z, n: (0, 0)
+    top = jnp.concatenate(
+        [
+            jnp.pad(w_first.reshape(taps_in, width).T, ((0, 0), (0, width - taps_in))).astype(jnp.float32),
+            w_second.T.astype(jnp.float32),
+            w_third.T.astype(jnp.float32),
+            jnp.pad(
+                jnp.stack([b_first, b_second, b_third], axis=1),
+                ((0, 0), (0, width - 3)),
+            ),
+        ],
+        axis=1,
+    ).astype(jnp.float32)
+    bottom = jnp.pad(wl.astype(jnp.float32), ((0, -(-outs // 8) * 8 - outs), (0, 3 * width)))
+    packed = jnp.concatenate([top, bottom], axis=0)
+    rows = 16
     q = pl.pallas_call(
         net_kernel,
-        grid=(slice_count, pixels // chunk),
+        grid=(slice_count, row_count // rows),
         in_specs=[
-            pl.BlockSpec((1, taps_in, chunk), lambda z, n: (z, 0, n)),
-            pl.BlockSpec((width, taps_in), full),
-            pl.BlockSpec((width, 1), full),
-            pl.BlockSpec((width, width), full),
-            pl.BlockSpec((width, 1), full),
-            pl.BlockSpec((width, width), full),
-            pl.BlockSpec((width, 1), full),
-            pl.BlockSpec((outs, width), full),
-        ],
-        out_specs=pl.BlockSpec((1, chunk // col_count, outs, col_count), lambda z, n: (z, n, 0, 0)),
+            pl.BlockSpec((1, taps_in, rows, col_count), lambda z, n: (z, 0, n, 0)),
+            pl.BlockSpec(packed.shape, lambda z, n: (0, 0)),
+        ],
+        out_specs=pl.BlockSpec((1, rows, outs, col_count), lambda z, n: (z, n, 0, 0)),
         out_shape=jax.ShapeDtypeStruct((slice_count, row_count, outs, col_count), jnp.float32),
-    )(
-        columns,
-        w1,
-        b_first.reshape(width, 1),
-        w_second.T,
-        b_second.reshape(width, 1),
-        w_third.T,
-        b_third.reshape(width, 1),
-        wl,
-    )
+    )(columns, packed)
     q = jnp.pad(q, ((0, 0), (1, 1), (0, 0), (1, 1)))
     score_field = jnp.zeros((slice_count, row_count, 2, col_count), jnp.float32)
     for shift_x in range(3):
@@ -178,8 +186,7 @@
             score_field = score_field + q[
                 :, shift_x : shift_x + row_count, tap : tap + 2, shift_y : shift_y + col_count
             ]
-    score_field = jnp.transpose(score_field, (0, 2, 1, 3))
-    return score_field
+    return jnp.transpose(score_field, (0, 2, 1, 3))
 
 
 def slab_slices(image):

time: 129 us -> 121 us (0.938)
  local copies, waits for them, and re-layouts: 25.3 us -> 15.5 us
  waiting for transfers between devices: 8.84 us -> 12.3 us
  starting transfers between devices: 23.9 us -> 21.5 us
    reshape x7 -> x2, local copies, waits for them, and re-layouts: 8.72 us -> 0.13 us  [score_net(): w_first.reshape(taps_in, width)]
    all_to_all x1, waiting for transfers between devices: 2.25 us -> 5.89 us  [on_device(): lax.all_to_all(slab_slices(image), 'slab', split_axis=2, concat_axis=0, t...]
    all_to_all x1, starting transfers between devices: 6.98 us -> 4.41 us  [on_device(): lax.all_to_all(by_depth.astype(jnp.bfloat16), 'slab', split_axis=0, conca...]
    unnamed x31, local copies, waits for them, and re-layouts: 10.1 us -> 8.82 us
  transfers between devices with their start and end apart: 5 -> 5, of which waited for: 2 -> 2; matrix products, arithmetic and copies ran while one was open for 23% -> 17% of each run, Pallas kernels for 13% -> 14%
where the time goes in v3:
time: 121 us; the launch traced here: 119 us
  Pallas kernels  30.3 us (25%)
  starting transfers between devices  21.5 us (18%)
  other arithmetic  16.1 us (13%)
  local copies, waits for them, and re-layouts  15.5 us (13%)
  between operations  13.7 us (11%)
  waiting for transfers between devices  12.3 us (10%)
  blocking collectives  9.63 us (8%)
    pallas_call x1, Pallas kernels, score_net(): pl.pallas_call(net_kernel, grid=(slice_count, row_count // rows), in_spec...  16.4 us
    pallas_call x1, Pallas kernels, coil_adjoint(): pl.pallas_call(adjoint_kernel, grid=(coils,), in_specs=[pl.BlockSpec((2,...  13.9 us
    all_to_all x1, starting transfers between devices, on_device(): lax.all_to_all(slab_slices(image), 'slab', split_axis=2, concat_axis=0, t...  10.1 us
    all_gather x1, blocking collectives, slab_slices(): return lax.all_gather(image, 'coil', axis=0, tiled=True)  9.63 us
    unnamed x31, local copies, waits for them, and re-layouts  8.82 us
    all_to_all x1, waiting for transfers between devices, on_device(): lax.all_to_all(by_depth.astype(jnp.bfloat16), 'slab', split_axis=0, conca...  6.35 us
    all_to_all x1, waiting for transfers between devices, on_device(): lax.all_to_all(slab_slices(image), 'slab', split_axis=2, concat_axis=0, t...  5.89 us
    ppermute x1, starting transfers between devices, with_halo(): before = lax.ppermute(last, axis, up)  4.94 us
  transfers between devices with their start and end apart: 5, of which 2 were waited for; matrix products, arithmetic and copies ran while one was open for 17% of the time, Pallas kernels for 14%

profile of v3, /device:TPU:1, one launch (start us, length us, event | category | flops | bytes accessed | tf_op | source)
XLA Modules:
  0.0 119.1 jit_solution(2258254819319317701)
XLA Ops:
  6.6 1.0 convert_element_type.65
  7.6 4.9 %collective-permute-start = (bf16[2,2,32,384]{3,2,1,0:T(8,128)(2,1)S(1)}, bf16[2,2,32,384]{3,2,1,0:T(8,128)(2,1)S(1)}, u32[]{:S(2)}, u32[]{:S(2)}) collective-permute-start(bf16[2,2,32,384]{3,2,1,0:T(8,128)(2,1)S(1)} %convert_element_type.65), channel_id=1, source_target_pairs={{0,1},{1,2},{2,3},{3,4},{4,5},{5,6},{6,7},{7,8},{8,9},{9,10},{10,1... | collective-permute-start | bytes 294920 | tf_op jit(solution)/shard_map/ppermute | solution.py:18
  12.6 1.9 %collective-permute-start.1 = (bf16[2,2,32,384]{3,2,1,0:T(8,128)(2,1)S(1)}, bf16[2,2,32,384]{3,2,1,0:T(8,128)(2,1)S(1)}, u32[]{:S(2)}, u32[]{:S(2)}) collective-permute-start(bf16[2,2,32,384]{3,2,1,0:T(8,128)(2,1)S(1)} %convert_element_type.65), channel_id=1, source_target_pairs={{1,0},{2,1},{3,2},{4,3},{5,4},{6,5},{7,6},{8,7},{9,8},{10,9},{11,1... | collective-permute-start | bytes 294920 | tf_op jit(solution)/shard_map/ppermute | solution.py:19
  14.5 9.6 %all_gather.3 = f32[8,2,32,384]{3,2,1,0:T(8,128)S(1)} all-gather(f32[2,2,32,384]{3,2,1,0:T(8,128)} %param.12), channel_id=1, replica_groups=mesh['slab'=32,'coil'=4] {'coil'}, dimensions={0}, use_global_device_ids=true | all-gather | bytes 983040 | tf_op jit(solution)/shard_map/all_gather | solution.py:193
  24.1 1.4 %copy.73 = f32[8,2,32,384]{3,0,1,2:T(8,128)} copy(f32[8,2,32,384]{3,2,1,0:T(8,128)S(1)} %all_gather.3) | data formatting | bytes 1572864 | tf_op jit(solution)/shard_map/all_gather | solution.py:193
  25.5 10.1 %all-to-all-start = ((f32[8,2,32,384]{3,0,1,2:T(8,128)}), f32[8,2,32,384]{3,0,1,2:T(8,128)S(1)}, u32[]{:S(2)}, u32[]{:S(2)}) async-start(f32[8,2,32,384]{3,0,1,2:T(8,128)} %copy.73), calls=%async_computation | async-start | bytes 1572864 | tf_op jit(solution)/shard_map/all_to_all | solution.py:212
  35.6 2.6 %multiply_convert_fusion = (bf16[384,384]{1,0:T(8,128)(2,1)S(1)}, bf16[384,384]{1,0:T(8,128)(2,1)S(1)}) fusion(), kind=kLoop, calls=%fused_computation.21 | loop fusion | flops 1916928 | bytes 589824 | tf_op jit(solution)/shard_map/convert_element_type | solution.py:31
  38.2 1.1 multiply_convert_fusion.2
  39.9 0.9 pad_maximum_fusion.ty_ref
  40.8 0.7 fusion.13.p_ref
  41.6 0.7 pad_maximum_fusion.1.tz_ref
  42.4 1.1 fusion.5
  43.5 0.9 fusion.6
  44.4 5.9 %all-to-all-done = f32[8,2,32,384]{3,0,1,2:T(8,128)S(1)} async-done(((f32[8,2,32,384]{3,0,1,2:T(8,128)}), f32[8,2,32,384]{3,0,1,2:T(8,128)S(1)}, u32[]{:S(2)}, u32[]{:S(2)}) %all-to-all-start) | async-done | bytes 786464 | tf_op jit(solution)/shard_map/all_to_all | solution.py:212
  50.4 1.2 copy.75
  51.5 13.9 %shard_map.119 = f32[2,1,384,256]{3,2,1,0:T(8,128)} custom-call(f32[2,1,384,256]{3,2,1,0:T(8,128)} %bitcast.34, bf16[4,2,1,384,256]{4,3,2,1,0:T(8,128)(2,1)} %sens_ref.1, bf16[4,2,1,384,256]{4,3,2,1,0:T(8,128)(2,1)} %meas_ref.1, s32[384,256]{1,0:T(8,128)} %mask_ref.1, bf16[768,384]{1,0:T(8,128)(2,1)} %pad_maximum_fusion.ty_ref, ...), custom_call_target="tpu_custom_call" | custom-call | tf_op jit(solution)/shard_map/pallas_call | solution.py:95
  65.4 1.2 convert_bitcast_fusion
  66.6 1.1 copy.76
  67.7 4.4 %all-to-all-start.1 = ((bf16[256,2,1,384]{3,1,2,0:T(2,128)(2,1)}), bf16[256,2,1,384]{3,1,2,0:T(2,128)(2,1)S(1)}, u32[]{:S(2)}, u32[]{:S(2)}) async-start(bf16[256,2,1,384]{3,1,2,0:T(2,128)(2,1)} %copy.76), calls=%async_computation.1 | async-start | bytes 786432 | tf_op jit(solution)/shard_map/all_to_all | solution.py:216
  72.4 1.2 fusion.7
  73.5 1.0 fusion.8
  75.9 6.3 %all-to-all-done.1 = bf16[256,2,1,384]{3,1,2,0:T(2,128)(2,1)S(1)} async-done(((bf16[256,2,1,384]{3,1,2,0:T(2,128)(2,1)}), bf16[256,2,1,384]{3,1,2,0:T(2,128)(2,1)S(1)}, u32[]{:S(2)}, u32[]{:S(2)}) %all-to-all-start.1) | async-done | bytes 393248 | tf_op jit(solution)/shard_map/all_to_all | solution.py:216
  82.3 0.8 copy.78
  83.1 0.7 constant_dynamic-update-slice_fusion.7
  85.1 1.0 fusion.9
  86.1 1.2 fusion.10
  87.2 0.9 fusion.11
  88.1 1.2 fusion.12.x_ref
  89.3 16.4 %shard_map.118 = f32[2,32,18,384]{3,2,1,0:T(8,128)} custom-call(bf16[2,90,32,384]{3,2,1,0:T(8,128)(2,1)} %fusion.12.x_ref, f32[152,512]{1,0:T(8,128)} %fusion.13.p_ref), custom_call_target="tpu_custom_call" | custom-call | tf_op jit(solution)/shard_map/pallas_call | solution.py:171
  105.7 0.9 convert_element_type.80
  106.6 4.9 %fusion.31 = f32[2,2,32,384]{3,1,2,0:T(2,128)S(1)} fusion(f32[2,2,32,384]{3,2,1,0:T(8,128)S(1)} %copy-done.1, f32[2,2,32,384]{3,2,1,0:T(8,128)S(1)} %copy-done, f32[2,2,32,384]{3,2,1,0:T(8,128)S(1)} %convert_element_type.80, f32[2,32,18,384]{3,2,1,0:T(8,128)} %shard_map.118), kind=kLoop, calls=%fused_computation.65 | loop fusion | flops 589824 | bytes 3342336 | tf_op jit(solution)/shard_map/add | solution.py:222
  111.6 0.7 copy.82
  (45 shorter events, 3.6 us)
Async XLA Ops:
  6.5 35.8 %copy-start = (f32[2,2,32,384]{3,2,1,0:T(8,128)S(1)}, f32[2,2,32,384]{3,2,1,0:T(8,128)}, u32[]{:S(2)}) copy-start(f32[2,2,32,384]{3,2,1,0:T(8,128)} %param.12) | copy-start | bytes 589828
  6.5 32.8 %copy-start.2 = (bf16[128,128]{1,0:T(8,128)(2,1)S(1)}, bf16[128,128]{1,0:T(8,128)(2,1)}, u32[]{:S(2)}) copy-start(bf16[128,128]{1,0:T(8,128)(2,1)} %param.19) | copy-start | bytes 98308
  6.5 32.9 %copy-start.3 = (bf16[128,128]{1,0:T(8,128)(2,1)S(1)}, bf16[128,128]{1,0:T(8,128)(2,1)}, u32[]{:S(2)}) copy-start(bf16[128,128]{1,0:T(8,128)(2,1)} %param.21) | copy-start | bytes 98308
  6.5 33.0 %copy-start.4 = (bf16[3,3,10,128]{3,1,2,0:T(4,128)(2,1)S(1)}, bf16[3,3,10,128]{3,1,2,0:T(4,128)(2,1)}, u32[]{:S(2)}) copy-start(bf16[3,3,10,128]{3,1,2,0:T(4,128)(2,1)} %param.17) | copy-start | bytes 69124
  6.5 33.2 %copy-start.8 = (f32[128]{0:T(128)S(1)}, f32[128]{0:T(128)}, u32[]{:S(2)}) copy-start(f32[128]{0:T(128)} %param.18) | copy-start | bytes 1540
  6.5 33.2 %copy-start.7 = (f32[128]{0:T(128)S(1)}, f32[128]{0:T(128)}, u32[]{:S(2)}) copy-start(f32[128]{0:T(128)} %param.20) | copy-start | bytes 1540
  6.6 33.2 %copy-start.6 = (f32[128]{0:T(128)S(1)}, f32[128]{0:T(128)}, u32[]{:S(2)}) copy-start(f32[128]{0:T(128)} %param.22) | copy-start | bytes 1540
  6.6 33.3 %copy-start.5 = (bf16[3,3,2,128]{3,2,1,0:T(2,128)(2,1)S(1)}, bf16[3,3,2,128]{3,2,1,0:T(2,128)(2,1)}, u32[]{:S(2)}) copy-start(bf16[3,3,2,128]{3,2,1,0:T(2,128)(2,1)} %param.23) | copy-start | bytes 13828
  7.6 34.7 %collective-permute-start = (bf16[2,2,32,384]{3,2,1,0:T(8,128)(2,1)S(1)}, bf16[2,2,32,384]{3,2,1,0:T(8,128)(2,1)S(1)}, u32[]{:S(2)}, u32[]{:S(2)}) collective-permute-start(bf16[2,2,32,384]{3,2,1,0:T(8,128)(2,1)S(1)} %convert_element_type.65), channel_id=1, source_target_pairs={{0,1},{1,2},{2,3},{3,4},{4,5},{5,6},{6,7},{7,8},{8,9},{9,10},{10,1... | collective-permute-start | bytes 294920 | tf_op jit(solution)/shard_map/ppermute | solution.py:18
  12.6 29.8 %collective-permute-start.1 = (bf16[2,2,32,384]{3,2,1,0:T(8,128)(2,1)S(1)}, bf16[2,2,32,384]{3,2,1,0:T(8,128)(2,1)S(1)}, u32[]{:S(2)}, u32[]{:S(2)}) collective-permute-start(bf16[2,2,32,384]{3,2,1,0:T(8,128)(2,1)S(1)} %convert_element_type.65), channel_id=1, source_target_pairs={{1,0},{2,1},{3,2},{4,3},{5,4},{6,5},{7,6},{8,7},{9,8},{10,9},{11,1... | collective-permute-start | bytes 294920 | tf_op jit(solution)/shard_map/ppermute | solution.py:19
  25.5 24.8 %all-to-all-start = ((f32[8,2,32,384]{3,0,1,2:T(8,128)}), f32[8,2,32,384]{3,0,1,2:T(8,128)S(1)}, u32[]{:S(2)}, u32[]{:S(2)}) async-start(f32[8,2,32,384]{3,0,1,2:T(8,128)} %copy.73), calls=%async_computation | async-start | bytes 1572864 | tf_op jit(solution)/shard_map/all_to_all | solution.py:212
  67.7 14.5 %all-to-all-start.1 = ((bf16[256,2,1,384]{3,1,2,0:T(2,128)(2,1)}), bf16[256,2,1,384]{3,1,2,0:T(2,128)(2,1)S(1)}, u32[]{:S(2)}, u32[]{:S(2)}) async-start(bf16[256,2,1,384]{3,1,2,0:T(2,128)(2,1)} %copy.76), calls=%async_computation.1 | async-start | bytes 786432 | tf_op jit(solution)/shard_map/all_to_all | solution.py:216
  72.1 33.6 %reduce-scatter.2.cloned.1.call-start = ((), (), s32[]{:S(2)}) async-start(), calls=%async_computation.3 | async-start | bytes 491520 | tf_op jit(solution)/shard_map/reduce_scatter | solution.py:219
  88.1 18.5 %copy-start.1 = (f32[2,2,32,384]{3,2,1,0:T(8,128)S(1)}, f32[2,2,32,384]{3,2,1,0:T(8,128)}, u32[]{:S(2)}) copy-start(f32[2,2,32,384]{3,2,1,0:T(8,128)} %param.13) | copy-start | bytes 589828
Sparse Core Ops, SparseCore 0:
  83.3 16.5 reduce-scatter.1

commit v4 on v3

--- a/solution.py
+++ b/solution.py
@@ -108,6 +108,10 @@
     )(planes, sens, measured, mask, ty, tz)
 
 
+def silu(h):
+    return h * (0.5 + 0.5 * jnp.tanh(0.5 * h))
+
+
 def net_kernel(x_ref, p_ref, q_ref):
     width = p_ref.shape[1] // 4
     taps_in = x_ref.shape[1]
@@ -123,11 +127,11 @@
     b2 = p_ref[:width, 3 * width + 1 : 3 * width + 2]
     b3 = p_ref[:width, 3 * width + 2 : 3 * width + 3]
     h = jnp.dot(w1, x, preferred_element_type=jnp.float32) + b1
-    h = jax.nn.silu(h).astype(jnp.bfloat16)
+    h = silu(h).astype(jnp.bfloat16)
     h = jnp.dot(w2, h, preferred_element_type=jnp.float32) + b2
-    h = jax.nn.silu(h).astype(jnp.bfloat16)
+    h = silu(h).astype(jnp.bfloat16)
     h = jnp.dot(w3, h, preferred_element_type=jnp.float32) + b3
-    h = jax.nn.silu(h).astype(jnp.bfloat16)
+    h = silu(h).astype(jnp.bfloat16)
     q = jnp.dot(wl, h, preferred_element_type=jnp.float32)
     for row in range(rows):
         q_ref[0, row] = q[:, row * cols : (row + 1) * cols]

time: 121 us -> 125 us (1.033)
  Pallas kernels: 30.3 us -> 33.8 us
    pallas_call x1, Pallas kernels: 16.4 us -> 19.9 us  [score_net(): pl.pallas_call(net_kernel, grid=(slice_count, row_count // rows), in_spec...]
  transfers between devices with their start and end apart: 5 -> 5, of which waited for: 2 -> 2; matrix products, arithmetic and copies ran while one was open for 17% -> 16% of each run, Pallas kernels for 14% -> 16%
where the time goes in v4:
time: 125 us; the launch traced here: 123 us
  Pallas kernels  33.8 us (27%)
  starting transfers between devices  21.5 us (17%)
  other arithmetic  16.1 us (13%)
  local copies, waits for them, and re-layouts  15.5 us (12%)
  between operations  13.7 us (11%)
  waiting for transfers between devices  12.3 us (10%)
  blocking collectives  9.63 us (8%)
    pallas_call x1, Pallas kernels, score_net(): pl.pallas_call(net_kernel, grid=(slice_count, row_count // rows), in_spec...  19.9 us
    pallas_call x1, Pallas kernels, coil_adjoint(): pl.pallas_call(adjoint_kernel, grid=(coils,), in_specs=[pl.BlockSpec((2,...  13.9 us
    all_to_all x1, starting transfers between devices, on_device(): lax.all_to_all(slab_slices(image), 'slab', split_axis=2, concat_axis=0, t...  10.1 us
    all_gather x1, blocking collectives, slab_slices(): return lax.all_gather(image, 'coil', axis=0, tiled=True)  9.63 us
    unnamed x31, local copies, waits for them, and re-layouts  8.82 us
    all_to_all x1, waiting for transfers between devices, on_device(): lax.all_to_all(by_depth.astype(jnp.bfloat16), 'slab', split_axis=0, conca...  6.35 us
    all_to_all x1, waiting for transfers between devices, on_device(): lax.all_to_all(slab_slices(image), 'slab', split_axis=2, concat_axis=0, t...  5.89 us
    ppermute x1, starting transfers between devices, with_halo(): before = lax.ppermute(last, axis, up)  4.94 us
  transfers between devices with their start and end apart: 5, of which 2 were waited for; matrix products, arithmetic and copies ran while one was open for 16% of the time, Pallas kernels for 16%

profile of v4, /device:TPU:1, one launch (start us, length us, event | category | flops | bytes accessed | tf_op | source)
XLA Modules:
  0.0 122.6 jit_solution(13638156470929138298)
XLA Ops:
  6.6 1.0 convert_element_type.65
  7.6 4.9 %collective-permute-start = (bf16[2,2,32,384]{3,2,1,0:T(8,128)(2,1)S(1)}, bf16[2,2,32,384]{3,2,1,0:T(8,128)(2,1)S(1)}, u32[]{:S(2)}, u32[]{:S(2)}) collective-permute-start(bf16[2,2,32,384]{3,2,1,0:T(8,128)(2,1)S(1)} %convert_element_type.65), channel_id=1, source_target_pairs={{0,1},{1,2},{2,3},{3,4},{4,5},{5,6},{6,7},{7,8},{8,9},{9,10},{10,1... | collective-permute-start | bytes 294920 | tf_op jit(solution)/shard_map/ppermute | solution.py:18
  12.6 1.9 %collective-permute-start.1 = (bf16[2,2,32,384]{3,2,1,0:T(8,128)(2,1)S(1)}, bf16[2,2,32,384]{3,2,1,0:T(8,128)(2,1)S(1)}, u32[]{:S(2)}, u32[]{:S(2)}) collective-permute-start(bf16[2,2,32,384]{3,2,1,0:T(8,128)(2,1)S(1)} %convert_element_type.65), channel_id=1, source_target_pairs={{1,0},{2,1},{3,2},{4,3},{5,4},{6,5},{7,6},{8,7},{9,8},{10,9},{11,1... | collective-permute-start | bytes 294920 | tf_op jit(solution)/shard_map/ppermute | solution.py:19
  14.5 9.6 %all_gather.3 = f32[8,2,32,384]{3,2,1,0:T(8,128)S(1)} all-gather(f32[2,2,32,384]{3,2,1,0:T(8,128)} %param.12), channel_id=1, replica_groups=mesh['slab'=32,'coil'=4] {'coil'}, dimensions={0}, use_global_device_ids=true | all-gather | bytes 983040 | tf_op jit(solution)/shard_map/all_gather | solution.py:197
  24.1 1.4 %copy.73 = f32[8,2,32,384]{3,0,1,2:T(8,128)} copy(f32[8,2,32,384]{3,2,1,0:T(8,128)S(1)} %all_gather.3) | data formatting | bytes 1572864 | tf_op jit(solution)/shard_map/all_gather | solution.py:197
  25.5 10.1 %all-to-all-start = ((f32[8,2,32,384]{3,0,1,2:T(8,128)}), f32[8,2,32,384]{3,0,1,2:T(8,128)S(1)}, u32[]{:S(2)}, u32[]{:S(2)}) async-start(f32[8,2,32,384]{3,0,1,2:T(8,128)} %copy.73), calls=%async_computation | async-start | bytes 1572864 | tf_op jit(solution)/shard_map/all_to_all | solution.py:216
  35.6 2.6 %multiply_convert_fusion = (bf16[384,384]{1,0:T(8,128)(2,1)S(1)}, bf16[384,384]{1,0:T(8,128)(2,1)S(1)}) fusion(), kind=kLoop, calls=%fused_computation.21 | loop fusion | flops 1916928 | bytes 589824 | tf_op jit(solution)/shard_map/convert_element_type | solution.py:31
  38.2 1.1 multiply_convert_fusion.2
  39.9 0.9 pad_maximum_fusion.ty_ref
  40.8 0.7 fusion.13.p_ref
  41.6 0.7 pad_maximum_fusion.1.tz_ref
  42.4 1.1 fusion.5
  43.5 0.9 fusion.6
  44.4 5.9 %all-to-all-done = f32[8,2,32,384]{3,0,1,2:T(8,128)S(1)} async-done(((f32[8,2,32,384]{3,0,1,2:T(8,128)}), f32[8,2,32,384]{3,0,1,2:T(8,128)S(1)}, u32[]{:S(2)}, u32[]{:S(2)}) %all-to-all-start) | async-done | bytes 786464 | tf_op jit(solution)/shard_map/all_to_all | solution.py:216
  50.4 1.2 copy.75
  51.5 13.9 %shard_map.119 = f32[2,1,384,256]{3,2,1,0:T(8,128)} custom-call(f32[2,1,384,256]{3,2,1,0:T(8,128)} %bitcast.34, bf16[4,2,1,384,256]{4,3,2,1,0:T(8,128)(2,1)} %sens_ref.1, bf16[4,2,1,384,256]{4,3,2,1,0:T(8,128)(2,1)} %meas_ref.1, s32[384,256]{1,0:T(8,128)} %mask_ref.1, bf16[768,384]{1,0:T(8,128)(2,1)} %pad_maximum_fusion.ty_ref, ...), custom_call_target="tpu_custom_call" | custom-call | tf_op jit(solution)/shard_map/pallas_call | solution.py:95
  65.4 1.2 convert_bitcast_fusion
  66.6 1.1 copy.76
  67.7 4.4 %all-to-all-start.1 = ((bf16[256,2,1,384]{3,1,2,0:T(2,128)(2,1)}), bf16[256,2,1,384]{3,1,2,0:T(2,128)(2,1)S(1)}, u32[]{:S(2)}, u32[]{:S(2)}) async-start(bf16[256,2,1,384]{3,1,2,0:T(2,128)(2,1)} %copy.76), calls=%async_computation.1 | async-start | bytes 786432 | tf_op jit(solution)/shard_map/all_to_all | solution.py:220
  72.4 1.2 fusion.7
  73.5 1.0 fusion.8
  75.9 6.3 %all-to-all-done.1 = bf16[256,2,1,384]{3,1,2,0:T(2,128)(2,1)S(1)} async-done(((bf16[256,2,1,384]{3,1,2,0:T(2,128)(2,1)}), bf16[256,2,1,384]{3,1,2,0:T(2,128)(2,1)S(1)}, u32[]{:S(2)}, u32[]{:S(2)}) %all-to-all-start.1) | async-done | bytes 393248 | tf_op jit(solution)/shard_map/all_to_all | solution.py:220
  82.3 0.8 copy.78
  83.1 0.7 constant_dynamic-update-slice_fusion.7
  85.1 1.0 fusion.9
  86.1 1.2 fusion.10
  87.2 0.9 fusion.11
  88.1 1.2 fusion.12.x_ref
  89.3 19.9 %shard_map.118 = f32[2,32,18,384]{3,2,1,0:T(8,128)} custom-call(bf16[2,90,32,384]{3,2,1,0:T(8,128)(2,1)} %fusion.12.x_ref, f32[152,512]{1,0:T(8,128)} %fusion.13.p_ref), custom_call_target="tpu_custom_call" | custom-call | tf_op jit(solution)/shard_map/pallas_call | solution.py:175
  109.2 0.9 convert_element_type.80
  110.2 4.9 %fusion.31 = f32[2,2,32,384]{3,1,2,0:T(2,128)S(1)} fusion(f32[2,2,32,384]{3,2,1,0:T(8,128)S(1)} %copy-done.1, f32[2,2,32,384]{3,2,1,0:T(8,128)S(1)} %copy-done, f32[2,2,32,384]{3,2,1,0:T(8,128)S(1)} %convert_element_type.80, f32[2,32,18,384]{3,2,1,0:T(8,128)} %shard_map.118), kind=kLoop, calls=%fused_computation.65 | loop fusion | flops 589824 | bytes 3342336 | tf_op jit(solution)/shard_map/add | solution.py:226
  115.1 0.7 copy.82
  (45 shorter events, 3.6 us)
Async XLA Ops:
  6.5 35.8 %copy-start = (f32[2,2,32,384]{3,2,1,0:T(8,128)S(1)}, f32[2,2,32,384]{3,2,1,0:T(8,128)}, u32[]{:S(2)}) copy-start(f32[2,2,32,384]{3,2,1,0:T(8,128)} %param.12) | copy-start | bytes 589828
  6.5 32.8 %copy-start.2 = (bf16[128,128]{1,0:T(8,128)(2,1)S(1)}, bf16[128,128]{1,0:T(8,128)(2,1)}, u32[]{:S(2)}) copy-start(bf16[128,128]{1,0:T(8,128)(2,1)} %param.19) | copy-start | bytes 98308
  6.5 32.9 %copy-start.3 = (bf16[128,128]{1,0:T(8,128)(2,1)S(1)}, bf16[128,128]{1,0:T(8,128)(2,1)}, u32[]{:S(2)}) copy-start(bf16[128,128]{1,0:T(8,128)(2,1)} %param.21) | copy-start | bytes 98308
  6.5 33.0 %copy-start.4 = (bf16[3,3,10,128]{3,1,2,0:T(4,128)(2,1)S(1)}, bf16[3,3,10,128]{3,1,2,0:T(4,128)(2,1)}, u32[]{:S(2)}) copy-start(bf16[3,3,10,128]{3,1,2,0:T(4,128)(2,1)} %param.17) | copy-start | bytes 69124
  6.5 33.2 %copy-start.8 = (f32[128]{0:T(128)S(1)}, f32[128]{0:T(128)}, u32[]{:S(2)}) copy-start(f32[128]{0:T(128)} %param.18) | copy-start | bytes 1540
  6.5 33.2 %copy-start.7 = (f32[128]{0:T(128)S(1)}, f32[128]{0:T(128)}, u32[]{:S(2)}) copy-start(f32[128]{0:T(128)} %param.20) | copy-start | bytes 1540
  6.6 33.2 %copy-start.6 = (f32[128]{0:T(128)S(1)}, f32[128]{0:T(128)}, u32[]{:S(2)}) copy-start(f32[128]{0:T(128)} %param.22) | copy-start | bytes 1540
  6.6 33.3 %copy-start.5 = (bf16[3,3,2,128]{3,2,1,0:T(2,128)(2,1)S(1)}, bf16[3,3,2,128]{3,2,1,0:T(2,128)(2,1)}, u32[]{:S(2)}) copy-start(bf16[3,3,2,128]{3,2,1,0:T(2,128)(2,1)} %param.23) | copy-start | bytes 13828
  7.6 34.7 %collective-permute-start = (bf16[2,2,32,384]{3,2,1,0:T(8,128)(2,1)S(1)}, bf16[2,2,32,384]{3,2,1,0:T(8,128)(2,1)S(1)}, u32[]{:S(2)}, u32[]{:S(2)}) collective-permute-start(bf16[2,2,32,384]{3,2,1,0:T(8,128)(2,1)S(1)} %convert_element_type.65), channel_id=1, source_target_pairs={{0,1},{1,2},{2,3},{3,4},{4,5},{5,6},{6,7},{7,8},{8,9},{9,10},{10,1... | collective-permute-start | bytes 294920 | tf_op jit(solution)/shard_map/ppermute | solution.py:18
  12.6 29.8 %collective-permute-start.1 = (bf16[2,2,32,384]{3,2,1,0:T(8,128)(2,1)S(1)}, bf16[2,2,32,384]{3,2,1,0:T(8,128)(2,1)S(1)}, u32[]{:S(2)}, u32[]{:S(2)}) collective-permute-start(bf16[2,2,32,384]{3,2,1,0:T(8,128)(2,1)S(1)} %convert_element_type.65), channel_id=1, source_target_pairs={{1,0},{2,1},{3,2},{4,3},{5,4},{6,5},{7,6},{8,7},{9,8},{10,9},{11,1... | collective-permute-start | bytes 294920 | tf_op jit(solution)/shard_map/ppermute | solution.py:19
  25.5 24.8 %all-to-all-start = ((f32[8,2,32,384]{3,0,1,2:T(8,128)}), f32[8,2,32,384]{3,0,1,2:T(8,128)S(1)}, u32[]{:S(2)}, u32[]{:S(2)}) async-start(f32[8,2,32,384]{3,0,1,2:T(8,128)} %copy.73), calls=%async_computation | async-start | bytes 1572864 | tf_op jit(solution)/shard_map/all_to_all | solution.py:216
  67.7 14.5 %all-to-all-start.1 = ((bf16[256,2,1,384]{3,1,2,0:T(2,128)(2,1)}), bf16[256,2,1,384]{3,1,2,0:T(2,128)(2,1)S(1)}, u32[]{:S(2)}, u32[]{:S(2)}) async-start(bf16[256,2,1,384]{3,1,2,0:T(2,128)(2,1)} %copy.76), calls=%async_computation.1 | async-start | bytes 786432 | tf_op jit(solution)/shard_map/all_to_all | solution.py:220
  72.1 37.1 %reduce-scatter.2.cloned.1.call-start = ((), (), s32[]{:S(2)}) async-start(), calls=%async_computation.3 | async-start | bytes 491520 | tf_op jit(solution)/shard_map/reduce_scatter | solution.py:223
  88.1 22.0 %copy-start.1 = (f32[2,2,32,384]{3,2,1,0:T(8,128)S(1)}, f32[2,2,32,384]{3,2,1,0:T(8,128)}, u32[]{:S(2)}) copy-start(f32[2,2,32,384]{3,2,1,0:T(8,128)} %param.13) | copy-start | bytes 589828
Sparse Core Ops, SparseCore 0:
  83.3 16.5 reduce-scatter.1

commit v5 on v3

--- a/solution.py
+++ b/solution.py
@@ -105,6 +105,11 @@
         ],
         out_specs=pl.BlockSpec((2, None, ny, nz), lambda c: (0, 0, 0, 0)),
         out_shape=jax.ShapeDtypeStruct(planes.shape, jnp.float32),
+        cost_estimate=pl.CostEstimate(
+            flops=coils * 8 * ny * nz * (ny + nz) * 2,
+            transcendentals=0,
+            bytes_accessed=(sens.size + measured.size) * 2 + planes.size * 8,
+        ),
     )(planes, sens, measured, mask, ty, tz)
 
 
@@ -177,6 +182,11 @@
         ],
         out_specs=pl.BlockSpec((1, rows, outs, col_count), lambda z, n: (z, n, 0, 0)),
         out_shape=jax.ShapeDtypeStruct((slice_count, row_count, outs, col_count), jnp.float32),
+        cost_estimate=pl.CostEstimate(
+            flops=2 * slice_count * row_count * col_count * width * (taps_in + 2 * width + outs),
+            transcendentals=3 * slice_count * row_count * col_count * width,
+            bytes_accessed=columns.size * 2 + slice_count * row_count * outs * col_count * 4,
+        ),
     )(columns, packed)
     q = jnp.pad(q, ((0, 0), (1, 1), (0, 0), (1, 1)))
     score_field = jnp.zeros((slice_count, row_count, 2, col_count), jnp.float32)
@@ -190,7 +200,13 @@
 
 
 def slab_slices(image):
-    return lax.all_gather(image, "coil", axis=0, tiled=True)
+    groups = lax.axis_size("coil")
+    received = [image] + [
+        lax.ppermute(image, "coil", [(i, (i + shift) % groups) for i in range(groups)])
+        for shift in range(1, groups)
+    ]
+    order = (lax.axis_index("coil") - jnp.arange(groups)) % groups
+    return jnp.take(jnp.stack(received), order, axis=0).reshape((-1,) + image.shape[1:])
 
 
 def on_device(

time: 121 us -> 125 us (1.033)
  blocking collectives: 9.63 us -> 0 us
  waiting for transfers between devices: 12.3 us -> 18.2 us
  starting transfers between devices: 21.5 us -> 24.5 us
  local copies, waits for them, and re-layouts: 15.5 us -> 17.9 us
  other arithmetic: 16.1 us -> 18.2 us
    all_gather x1 -> x0, blocking collectives: 9.63 us -> none  [slab_slices(): return lax.all_gather(image, 'coil', axis=0, tiled=True)]
    all_to_all x1, waiting for transfers between devices: 5.89 us -> 10.2 us  [on_device(): lax.all_to_all(slab_slices(image), 'slab', split_axis=2, concat_axis=0, t...]
    ppermute x0 -> x3, starting transfers between devices: none -> 2.56 us  [slab_slices(): lax.ppermute(image, 'coil', [(i, (i + shift) % groups) for i in range(gro...]
    unnamed x31 -> x17, local copies, waits for them, and re-layouts: 8.82 us -> 11.1 us
    all_to_all x1, waiting for transfers between devices: 6.35 us -> 7.96 us  [on_device(): lax.all_to_all(by_depth.astype(jnp.bfloat16), 'slab', split_axis=0, conca...]
    select_n x0 -> x2, other arithmetic: none -> 1.4 us  [slab_slices(): jnp.take(jnp.stack(received), order, axis=0)]
    all_gather x1 -> x0, local copies, waits for them, and re-layouts: 1.37 us -> none  [slab_slices(): return lax.all_gather(image, 'coil', axis=0, tiled=True)]
  transfers between devices with their start and end apart: 5 -> 8, of which waited for: 2 -> 2; matrix products, arithmetic and copies ran while one was open for 17% -> 20% of each run, Pallas kernels for 14% -> 13%
where the time goes in v5:
time: 125 us; the launch traced here: 123 us
  Pallas kernels  30.4 us (24%)
  starting transfers between devices  24.5 us (20%)
  other arithmetic  18.2 us (15%)
  waiting for transfers between devices  18.2 us (15%)
  local copies, waits for them, and re-layouts  17.9 us (14%)
  between operations  13.6 us (11%)
    pallas_call x1, Pallas kernels, score_net(): pl.pallas_call(net_kernel, grid=(slice_count, row_count // rows), in_spec...  16.5 us
    pallas_call x1, Pallas kernels, coil_adjoint(): pl.pallas_call(adjoint_kernel, grid=(coils,), in_specs=[pl.BlockSpec((2,...  13.9 us
    unnamed x17, local copies, waits for them, and re-layouts  11.1 us
    all_to_all x1, starting transfers between devices, on_device(): lax.all_to_all(slab_slices(image), 'slab', split_axis=2, concat_axis=0, t...  10.4 us
    all_to_all x1, waiting for transfers between devices, on_device(): lax.all_to_all(slab_slices(image), 'slab', split_axis=2, concat_axis=0, t...  10.2 us
    all_to_all x1, waiting for transfers between devices, on_device(): lax.all_to_all(by_depth.astype(jnp.bfloat16), 'slab', split_axis=0, conca...  7.96 us
    ppermute x1, starting transfers between devices, with_halo(): before = lax.ppermute(last, axis, up)  4.94 us
    add x1, other arithmetic, on_device(): return image + STEP_SIZE * (score_field - gradient) + noise  4.77 us
  transfers between devices with their start and end apart: 8, of which 2 were waited for; matrix products, arithmetic and copies ran while one was open for 20% of the time, Pallas kernels for 13%

profile of v5, /device:TPU:1, one launch (start us, length us, event | category | flops | bytes accessed | tf_op | source)
XLA Modules:
  0.0 122.7 jit_solution(12202215651406159527)
XLA Ops:
  6.5 1.0 convert_element_type.65
  7.6 4.9 %collective-permute-start = (bf16[2,2,32,384]{3,2,1,0:T(8,128)(2,1)S(1)}, bf16[2,2,32,384]{3,2,1,0:T(8,128)(2,1)S(1)}, u32[]{:S(2)}, u32[]{:S(2)}) collective-permute-start(bf16[2,2,32,384]{3,2,1,0:T(8,128)(2,1)S(1)} %convert_element_type.65), channel_id=1, source_target_pairs={{0,1},{1,2},{2,3},{3,4},{4,5},{5,6},{6,7},{7,8},{8,9},{9,10},{10,1... | collective-permute-start | bytes 294920 | tf_op jit(solution)/shard_map/ppermute | solution.py:18
  12.5 1.9 %collective-permute-start.1 = (bf16[2,2,32,384]{3,2,1,0:T(8,128)(2,1)S(1)}, bf16[2,2,32,384]{3,2,1,0:T(8,128)(2,1)S(1)}, u32[]{:S(2)}, u32[]{:S(2)}) collective-permute-start(bf16[2,2,32,384]{3,2,1,0:T(8,128)(2,1)S(1)} %convert_element_type.65), channel_id=1, source_target_pairs={{1,0},{2,1},{3,2},{4,3},{5,4},{6,5},{7,6},{8,7},{9,8},{10,9},{11,1... | collective-permute-start | bytes 294920 | tf_op jit(solution)/shard_map/ppermute | solution.py:19
  14.5 1.8 %collective-permute-start.2 = (f32[2,2,32,384]{3,2,1,0:T(8,128)}, f32[2,2,32,384]{3,2,1,0:T(8,128)S(1)}, u32[]{:S(2)}, u32[]{:S(2)}) collective-permute-start(f32[2,2,32,384]{3,2,1,0:T(8,128)} %param.12), channel_id=1, source_target_pairs={{0,1},{1,2},{2,3},{3,0},{4,5},{5,6},{6,7},{7,4},{8,9},{9,10},{10,1... | collective-permute-start | bytes 589832 | tf_op jit(solution)/shard_map/ppermute | solution.py:205
  17.0 2.6 %multiply_convert_fusion = (bf16[384,384]{1,0:T(8,128)(2,1)S(1)}, bf16[384,384]{1,0:T(8,128)(2,1)S(1)}) fusion(), kind=kLoop, calls=%fused_computation.24 | loop fusion | flops 1916928 | bytes 589824 | tf_op jit(solution)/shard_map/convert_element_type | solution.py:31
  19.6 1.1 multiply_convert_fusion.2
  20.7 0.9 copy.70
  21.6 0.9 copy.71
  22.5 0.8 copy.68
  25.1 0.9 pad_maximum_fusion.1.ty_ref
  26.0 0.7 pad_maximum_fusion.2.tz_ref
  28.3 1.4 %copy_select_fusion = f32[8,2,32,384]{3,0,1,2:T(8,128)} fusion(f32[8,2,32,384]{3,2,1,0:T(8,128)S(1)} %bitcast.41, pred[8]{0:T(512)(128)(4,1)S(1)} %broadcast_in_dim.19), kind=kLoop, calls=%fused_computation.19 | loop fusion | flops 196608 | bytes 1572872 | tf_op jit(solution)/shard_map/jit(_take)/select_n | solution.py:209
  29.7 10.4 %all-to-all-start = ((f32[8,2,32,384]{3,0,1,2:T(8,128)}), f32[8,2,32,384]{3,0,1,2:T(8,128)S(1)}, u32[]{:S(2)}, u32[]{:S(2)}) async-start(f32[8,2,32,384]{3,0,1,2:T(8,128)} %copy_select_fusion), calls=%async_computation | async-start | bytes 1572864 | tf_op jit(solution)/shard_map/all_to_all | solution.py:228
  40.1 1.1 fusion.5
  41.2 0.9 fusion.6
  42.1 1.2 fusion.7
  43.3 1.1 fusion.8
  45.0 10.2 %all-to-all-done = f32[8,2,32,384]{3,0,1,2:T(8,128)S(1)} async-done(((f32[8,2,32,384]{3,0,1,2:T(8,128)}), f32[8,2,32,384]{3,0,1,2:T(8,128)S(1)}, u32[]{:S(2)}, u32[]{:S(2)}) %all-to-all-start) | async-done | bytes 786464 | tf_op jit(solution)/shard_map/all_to_all | solution.py:228
  55.3 1.2 copy.75
  56.5 13.9 %shard_map.119 = f32[2,1,384,256]{3,2,1,0:T(8,128)} custom-call(f32[2,1,384,256]{3,2,1,0:T(8,128)} %bitcast.44, bf16[4,2,1,384,256]{4,3,2,1,0:T(8,128)(2,1)} %sens_ref.1, bf16[4,2,1,384,256]{4,3,2,1,0:T(8,128)(2,1)} %meas_ref.1, s32[384,256]{1,0:T(8,128)} %mask_ref.1, bf16[768,384]{1,0:T(8,128)(2,1)} %pad_maximum_fusion.1.ty_ref, ...), custom_call_target="tpu_custom_call" | custom-call | flops 4026531840 | bytes 4718592 | tf_op jit(solution)/shard_map/pallas_call | solution.py:95
  70.4 1.2 convert_bitcast_fusion
  71.6 1.1 copy.76
  72.7 4.5 %all-to-all-start.1 = ((bf16[256,2,1,384]{3,1,2,0:T(2,128)(2,1)}), bf16[256,2,1,384]{3,1,2,0:T(2,128)(2,1)S(1)}, u32[]{:S(2)}, u32[]{:S(2)}) async-start(bf16[256,2,1,384]{3,1,2,0:T(2,128)(2,1)} %copy.76), calls=%async_computation.1 | async-start | bytes 786432 | tf_op jit(solution)/shard_map/all_to_all | solution.py:232
  79.3 8.0 %all-to-all-done.1 = bf16[256,2,1,384]{3,1,2,0:T(2,128)(2,1)S(1)} async-done(((bf16[256,2,1,384]{3,1,2,0:T(2,128)(2,1)}), bf16[256,2,1,384]{3,1,2,0:T(2,128)(2,1)S(1)}, u32[]{:S(2)}, u32[]{:S(2)}) %all-to-all-start.1) | async-done | bytes 393248 | tf_op jit(solution)/shard_map/all_to_all | solution.py:232
  87.4 0.8 copy.78
  88.8 1.0 fusion.9
  89.9 1.1 fusion.10
  91.0 0.9 fusion.11
  91.9 1.1 fusion.12.x_ref
  93.0 16.5 %shard_map.118 = f32[2,32,18,384]{3,2,1,0:T(8,128)} custom-call(bf16[2,90,32,384]{3,2,1,0:T(8,128)(2,1)} %fusion.12.x_ref, f32[152,512]{1,0:T(8,128)} %fusion.13.p_ref), custom_call_target="tpu_custom_call" | custom-call | flops 2290089984 | bytes 6193152 | tf_op jit(solution)/shard_map/pallas_call | solution.py:176
  109.5 0.9 convert_element_type.80
  110.4 4.8 %fusion.31 = f32[2,2,32,384]{3,1,2,0:T(2,128)S(1)} fusion(f32[2,2,32,384]{3,2,1,0:T(8,128)S(1)} %copy-done.1, f32[2,2,32,384]{3,2,1,0:T(8,128)S(1)} %copy-done, f32[2,2,32,384]{3,2,1,0:T(8,128)S(1)} %convert_element_type.80, f32[2,32,18,384]{3,2,1,0:T(8,128)} %shard_map.118), kind=kLoop, calls=%fused_computation.68 | loop fusion | flops 589824 | bytes 3342336 | tf_op jit(solution)/shard_map/add | solution.py:238
  (43 shorter events, 8.4 us)
Async XLA Ops:
  6.5 21.0 %copy-start = (f32[2,2,32,384]{3,2,1,0:T(8,128)S(1)}, f32[2,2,32,384]{3,2,1,0:T(8,128)}, u32[]{:S(2)}) copy-start(f32[2,2,32,384]{3,2,1,0:T(8,128)} %param.12) | copy-start | bytes 589828
  7.6 20.0 %collective-permute-start = (bf16[2,2,32,384]{3,2,1,0:T(8,128)(2,1)S(1)}, bf16[2,2,32,384]{3,2,1,0:T(8,128)(2,1)S(1)}, u32[]{:S(2)}, u32[]{:S(2)}) collective-permute-start(bf16[2,2,32,384]{3,2,1,0:T(8,128)(2,1)S(1)} %convert_element_type.65), channel_id=1, source_target_pairs={{0,1},{1,2},{2,3},{3,4},{4,5},{5,6},{6,7},{7,8},{8,9},{9,10},{10,1... | collective-permute-start | bytes 294920 | tf_op jit(solution)/shard_map/ppermute | solution.py:18
  12.5 27.6 %collective-permute-start.1 = (bf16[2,2,32,384]{3,2,1,0:T(8,128)(2,1)S(1)}, bf16[2,2,32,384]{3,2,1,0:T(8,128)(2,1)S(1)}, u32[]{:S(2)}, u32[]{:S(2)}) collective-permute-start(bf16[2,2,32,384]{3,2,1,0:T(8,128)(2,1)S(1)} %convert_element_type.65), channel_id=1, source_target_pairs={{1,0},{2,1},{3,2},{4,3},{5,4},{6,5},{7,6},{8,7},{9,8},{10,9},{11,1... | collective-permute-start | bytes 294920 | tf_op jit(solution)/shard_map/ppermute | solution.py:19
  14.4 13.2 %collective-permute-start.4 = (f32[2,2,32,384]{3,2,1,0:T(8,128)}, f32[2,2,32,384]{3,2,1,0:T(8,128)S(1)}, u32[]{:S(2)}, u32[]{:S(2)}) collective-permute-start(f32[2,2,32,384]{3,2,1,0:T(8,128)} %param.12), channel_id=1, source_target_pairs={{0,3},{1,0},{2,1},{3,2},{4,7},{5,4},{6,5},{7,6},{8,11},{9,8},{10,9... | collective-permute-start | bytes 589832 | tf_op jit(solution)/shard_map/ppermute | solution.py:205
  14.5 13.1 %collective-permute-start.2 = (f32[2,2,32,384]{3,2,1,0:T(8,128)}, f32[2,2,32,384]{3,2,1,0:T(8,128)S(1)}, u32[]{:S(2)}, u32[]{:S(2)}) collective-permute-start(f32[2,2,32,384]{3,2,1,0:T(8,128)} %param.12), channel_id=1, source_target_pairs={{0,1},{1,2},{2,3},{3,0},{4,5},{5,6},{6,7},{7,4},{8,9},{9,10},{10,1... | collective-permute-start | bytes 589832 | tf_op jit(solution)/shard_map/ppermute | solution.py:205
  16.3 11.3 %collective-permute-start.3 = (f32[2,2,32,384]{3,2,1,0:T(8,128)}, f32[2,2,32,384]{3,2,1,0:T(8,128)S(1)}, u32[]{:S(2)}, u32[]{:S(2)}) collective-permute-start(f32[2,2,32,384]{3,2,1,0:T(8,128)} %param.12), channel_id=1, source_target_pairs={{0,2},{1,3},{2,0},{3,1},{4,6},{5,7},{6,4},{7,5},{8,10},{9,11},{10,... | collective-permute-start | bytes 589832 | tf_op jit(solution)/shard_map/ppermute | solution.py:205
  29.7 25.6 %all-to-all-start = ((f32[8,2,32,384]{3,0,1,2:T(8,128)}), f32[8,2,32,384]{3,0,1,2:T(8,128)S(1)}, u32[]{:S(2)}, u32[]{:S(2)}) async-start(f32[8,2,32,384]{3,0,1,2:T(8,128)} %copy_select_fusion), calls=%async_computation | async-start | bytes 1572864 | tf_op jit(solution)/shard_map/all_to_all | solution.py:228
  72.7 14.6 %all-to-all-start.1 = ((bf16[256,2,1,384]{3,1,2,0:T(2,128)(2,1)}), bf16[256,2,1,384]{3,1,2,0:T(2,128)(2,1)S(1)}, u32[]{:S(2)}, u32[]{:S(2)}) async-start(bf16[256,2,1,384]{3,1,2,0:T(2,128)(2,1)} %copy.76), calls=%async_computation.1 | async-start | bytes 786432 | tf_op jit(solution)/shard_map/all_to_all | solution.py:232
  77.1 32.4 %reduce-scatter.2.cloned.1.call-start = ((), (), s32[]{:S(2)}) async-start(), calls=%async_computation.3 | async-start | bytes 491520 | tf_op jit(solution)/shard_map/reduce_scatter | solution.py:235
  93.0 17.4 %copy-start.1 = (f32[2,2,32,384]{3,2,1,0:T(8,128)S(1)}, f32[2,2,32,384]{3,2,1,0:T(8,128)}, u32[]{:S(2)}) copy-start(f32[2,2,32,384]{3,2,1,0:T(8,128)} %param.13) | copy-start | bytes 589828
Sparse Core Ops, SparseCore 0:
  88.3 15.7 reduce-scatter.1

commit v6 on v3

--- a/solution.py
+++ b/solution.py
@@ -209,16 +209,17 @@
 ):
     window = with_halo(image.astype(jnp.bfloat16), ((("slab", "coil"), 0),), 2)
     score_field = score_net(window, w_first, b_first, w_second, b_second, w_third, b_third, w_last)
-    planes_in = lax.all_to_all(slab_slices(image), "slab", split_axis=2, concat_axis=0, tiled=True)
+    groups = lax.axis_size("coil")
+    depth, parts, rows, lines = image.shape
+    copies = jnp.broadcast_to(image[:, :, :, None], (depth, parts, rows, groups, lines))
+    copies = copies.reshape(depth, parts, rows * groups, lines)
+    planes_in = lax.all_to_all(copies, ("slab", "coil"), split_axis=2, concat_axis=0, tiled=True)
     planes = jnp.transpose(planes_in, (1, 2, 3, 0))
     partial_sum = coil_adjoint(planes, sens, measured, mask)
-    by_depth = jnp.transpose(partial_sum, (3, 0, 1, 2))
-    slab_part = lax.all_to_all(
-        by_depth.astype(jnp.bfloat16), "slab", split_axis=0, concat_axis=2, tiled=True
-    ).astype(by_depth.dtype)
-    gradient = lax.psum_scatter(
-        slab_part.astype(jnp.bfloat16), "coil", scatter_dimension=0, tiled=True
-    ).astype(jnp.float32)
+    by_depth = jnp.transpose(partial_sum, (3, 0, 1, 2)).astype(jnp.bfloat16)
+    by_device = lax.all_to_all(by_depth, ("slab", "coil"), split_axis=0, concat_axis=2, tiled=True)
+    by_device = by_device.astype(jnp.float32).reshape(depth, parts, rows, groups, lines)
+    gradient = jnp.sum(by_device, axis=3)
     return image + STEP_SIZE * (score_field - gradient) + noise
 
 

time: 121 us -> 92.3 us (0.76); the launches traced: 119 us -> 91.8 us
  between operations: 13.7 us -> 0.23 us
  waiting for transfers between devices: 12.3 us -> 0.01 us
  blocking collectives: 9.63 us -> 0 us
  starting transfers between devices: 21.5 us -> 27.6 us
  local copies, waits for them, and re-layouts: 15.5 us -> 17.8 us
    all_to_all x2, waiting for transfers between devices: 12.2 us -> 0.01 us  [the longest x1 0.01 us: on_device(): lax.all_to_all(copies, ('slab', 'coil'), split_axis=2, concat_axis=0, til...]
    all_gather x1 -> x0, blocking collectives: 9.63 us -> none  [slab_slices(): return lax.all_gather(image, 'coil', axis=0, tiled=True)]
    all_to_all x2, starting transfers between devices: 14.5 us -> 20.7 us  [the longest x1 10.9 us: on_device(): lax.all_to_all(copies, ('slab', 'coil'), split_axis=2, concat_axis=0, til...]
    unnamed x31 -> x26, local copies, waits for them, and re-layouts: 8.82 us -> 12.3 us
    all_gather x1 -> x0, local copies, waits for them, and re-layouts: 1.37 us -> none  [slab_slices(): return lax.all_gather(image, 'coil', axis=0, tiled=True)]
  transfers between devices with their start and end apart: 5 -> 4, of which waited for: 2 -> 0; matrix products, arithmetic and copies ran while one was open for 17% -> 25% of each run, Pallas kernels for 14% -> 18%
where the time goes in v6:
time: 92.3 us; the launch traced here: 91.8 us
  Pallas kernels  30.3 us (33%)
  starting transfers between devices  27.6 us (30%)
  local copies, waits for them, and re-layouts  17.8 us (19%)
  other arithmetic  15.8 us (17%)
    pallas_call x1, Pallas kernels, score_net(): pl.pallas_call(net_kernel, grid=(slice_count, row_count // rows), in_spec...  16.5 us
    pallas_call x1, Pallas kernels, coil_adjoint(): pl.pallas_call(adjoint_kernel, grid=(coils,), in_specs=[pl.BlockSpec((2,...  13.9 us
    unnamed x26, local copies, waits for them, and re-layouts  12.3 us
    all_to_all x1, starting transfers between devices, on_device(): lax.all_to_all(copies, ('slab', 'coil'), split_axis=2, concat_axis=0, til...  10.9 us
    all_to_all x1, starting transfers between devices, on_device(): lax.all_to_all(by_depth, ('slab', 'coil'), split_axis=0, concat_axis=2, t...  9.76 us
    ppermute x1, starting transfers between devices, with_halo(): before = lax.ppermute(last, axis, up)  4.94 us
    add x1, other arithmetic, on_device(): return image + STEP_SIZE * (score_field - gradient) + noise  4.74 us
    convert_element_type x2, other arithmetic, dft_tables(): (jnp.sin(phase_angle) * norm_scale).astype(jnp.bfloat16)  3.7 us
  transfers between devices with their start and end apart: 4, of which 0 were waited for; matrix products, arithmetic and copies ran while one was open for 25% of the time, Pallas kernels for 18%

profile of v6, /device:TPU:1, one launch (start us, length us, event | category | flops | bytes accessed | tf_op | source)
XLA Modules:
  0.0 91.8 jit_solution(5570357194307101826)
XLA Ops:
  0.0 1.0 %convert_element_type.77 = bf16[2,2,32,384]{3,2,1,0:T(8,128)(2,1)S(1)} convert(f32[2,2,32,384]{3,2,1,0:T(8,128)} %param.12) | non-fusion elementwise | flops 49152 | bytes 294912 | tf_op jit(solution)/shard_map/convert_element_type | solution.py:210
  1.0 4.9 %collective-permute-start = (bf16[2,2,32,384]{3,2,1,0:T(8,128)(2,1)S(1)}, bf16[2,2,32,384]{3,2,1,0:T(8,128)(2,1)S(1)}, u32[]{:S(2)}, u32[]{:S(2)}) collective-permute-start(bf16[2,2,32,384]{3,2,1,0:T(8,128)(2,1)S(1)} %convert_element_type.77), channel_id=1, source_target_pairs={{0,1},{1,2},{2,3},{3,4},{4,5},{5,6},{6,7},{7,8},{8,9},{9,10},{10,1... | collective-permute-start | bytes 294920 | tf_op jit(solution)/shard_map/ppermute | solution.py:18
  6.0 1.9 %collective-permute-start.1 = (bf16[2,2,32,384]{3,2,1,0:T(8,128)(2,1)S(1)}, bf16[2,2,32,384]{3,2,1,0:T(8,128)(2,1)S(1)}, u32[]{:S(2)}, u32[]{:S(2)}) collective-permute-start(bf16[2,2,32,384]{3,2,1,0:T(8,128)(2,1)S(1)} %convert_element_type.77), channel_id=1, source_target_pairs={{1,0},{2,1},{3,2},{4,3},{5,4},{6,5},{7,6},{8,7},{9,8},{10,9},{11,1... | collective-permute-start | bytes 294920 | tf_op jit(solution)/shard_map/ppermute | solution.py:19
  7.9 1.1 %copy.65 = f32[2,2,32,384]{3,1,0,2:T(2,128)S(1)} copy(f32[2,2,32,384]{3,2,1,0:T(8,128)} %param.12) | data formatting | bytes 393216 | tf_op args[0]
  9.0 1.1 %broadcast_in_dim.2 = f32[2,2,32,4,384]{4,1,0,3,2:T(2,128)} broadcast(f32[2,2,32,384]{3,1,0,2:T(2,128)S(1)} %copy.65), dimensions={0,1,2,4} | broadcast | bytes 983040 | tf_op jit(solution)/shard_map/broadcast_in_dim | solution.py:214
  10.1 10.9 %all-to-all-start = ((f32[2,2,128,384]{3,1,0,2:T(2,128)}), f32[2,2,128,384]{3,1,0,2:T(2,128)S(1)}, u32[]{:S(2)}, u32[]{:S(2)}) async-start(f32[2,2,128,384]{3,1,0,2:T(2,128)} %bitcast.7), calls=%async_computation | async-start | bytes 1572864 | tf_op jit(solution)/shard_map/all_to_all | solution.py:216
  21.0 2.6 %multiply_convert_fusion = (bf16[384,384]{1,0:T(8,128)(2,1)S(1)}, bf16[384,384]{1,0:T(8,128)(2,1)S(1)}) fusion(), kind=kLoop, calls=%fused_computation.20 | loop fusion | flops 1916928 | bytes 589824 | tf_op jit(solution)/shard_map/convert_element_type | solution.py:31
  23.6 1.1 %multiply_convert_fusion.2 = (bf16[256,256]{1,0:T(8,128)(2,1)S(1)}, bf16[256,256]{1,0:T(8,128)(2,1)S(1)}) fusion(), kind=kLoop, calls=%fused_computation.47 | loop fusion | flops 1179648 | bytes 262144 | tf_op jit(solution)/shard_map/convert_element_type | solution.py:31
  24.7 0.9 copy.62
  25.6 0.9 copy.63
  26.5 0.8 copy.60
  27.6 0.9 pad_maximum_fusion.ty_ref
  28.5 0.7 fusion.13.p_ref
  29.3 0.7 pad_maximum_fusion.1.tz_ref
  30.1 1.1 %fusion.5 = bf16[2,90,32,384]{3,2,1,0:T(8,128)(2,1)} fusion(bf16[2,10,32,384]{3,2,1,0:T(8,128)(2,1)S(1)} %constant_dynamic-update-slice_fusion), kind=kLoop, calls=%fused_computation.26 | loop fusion | bytes 983040
  31.2 1.0 %fusion.6 = bf16[2,90,32,384]{3,2,1,0:T(8,128)(2,1)} fusion(bf16[2,90,32,384]{3,2,1,0:T(8,128)(2,1)} %fusion.5, bf16[2,10,32,384]{3,2,1,0:T(8,128)(2,1)S(1)} %constant_dynamic-update-slice_fusion), kind=kLoop, calls=%fused_computation.27 | loop fusion | bytes 983040
  32.2 1.2 %fusion.7 = bf16[2,90,32,384]{3,2,1,0:T(8,128)(2,1)} fusion(bf16[2,90,32,384]{3,2,1,0:T(8,128)(2,1)} %fusion.6, bf16[2,10,32,384]{3,2,1,0:T(8,128)(2,1)S(1)} %constant_dynamic-update-slice_fusion), kind=kLoop, calls=%fused_computation.28 | loop fusion | bytes 983040
  33.3 1.1 %fusion.8 = bf16[2,90,32,384]{3,2,1,0:T(8,128)(2,1)} fusion(bf16[2,90,32,384]{3,2,1,0:T(8,128)(2,1)} %fusion.7, bf16[2,10,32,384]{3,2,1,0:T(8,128)(2,1)S(1)} %constant_dynamic-update-slice_fusion), kind=kLoop, calls=%fused_computation.29 | loop fusion | bytes 983040
  35.1 0.7 constant_dynamic-update-slice_fusion.8
  37.0 0.7 constant_dynamic-update-slice_fusion.5
  37.7 1.2 %copy.66 = f32[256,2,1,384]{0,3,2,1:T(8,128)} copy(f32[256,2,1,384]{3,1,0,2:T(2,128)S(1)} %bitcast.30) | data formatting | bytes 1572864 | tf_op jit(solution)/shard_map/all_to_all | solution.py:216
  38.9 13.9 %shard_map.119 = f32[2,1,384,256]{3,2,1,0:T(8,128)} custom-call(f32[2,1,384,256]{3,2,1,0:T(8,128)} %bitcast.32, bf16[4,2,1,384,256]{4,3,2,1,0:T(8,128)(2,1)} %sens_ref.1, bf16[4,2,1,384,256]{4,3,2,1,0:T(8,128)(2,1)} %meas_ref.1, s32[384,256]{1,0:T(8,128)} %mask_ref.1, bf16[768,384]{1,0:T(8,128)(2,1)} %pad_maximum_fusion.ty_ref, ...), custom_call_target="tpu_custom_call" | custom-call | tf_op jit(solution)/shard_map/pallas_call | solution.py:95
  52.8 1.2 %convert_bitcast_fusion = bf16[256,2,1,384]{0,3,2,1:T(8,128)(2,1)S(1)} fusion(f32[2,1,384,256]{3,2,1,0:T(8,128)} %shard_map.119), kind=kLoop, calls=%fused_computation.34 | loop fusion | flops 196608 | bytes 1179648 | tf_op jit(solution)/shard_map/convert_element_type | solution.py:219
  54.0 1.1 %copy.67 = bf16[256,2,1,384]{3,1,2,0:T(2,128)(2,1)} copy(bf16[256,2,1,384]{0,3,2,1:T(8,128)(2,1)S(1)} %convert_bitcast_fusion) | data formatting | bytes 786432 | tf_op jit(solution)/shard_map/convert_element_type | solution.py:219
  55.1 9.8 %all-to-all-start.1 = ((bf16[256,2,1,384]{3,1,2,0:T(2,128)(2,1)}), bf16[256,2,1,384]{3,1,2,0:T(2,128)(2,1)S(1)}, u32[]{:S(2)}, u32[]{:S(2)}) async-start(bf16[256,2,1,384]{3,1,2,0:T(2,128)(2,1)} %copy.67), calls=%async_computation.1 | async-start | bytes 786432 | tf_op jit(solution)/shard_map/all_to_all | solution.py:220
  64.8 1.0 %fusion.9 = bf16[2,90,32,384]{3,2,1,0:T(8,128)(2,1)} fusion(bf16[2,90,32,384]{3,2,1,0:T(8,128)(2,1)} %constant_dynamic-update-slice_fusion.5, bf16[2,10,32,384]{3,2,1,0:T(8,128)(2,1)S(1)} %constant_dynamic-update-slice_fusion), kind=kLoop, calls=%fused_computation.30 | loop fusion | bytes 983040
  65.9 1.1 %fusion.10 = bf16[2,90,32,384]{3,2,1,0:T(8,128)(2,1)} fusion(bf16[2,90,32,384]{3,2,1,0:T(8,128)(2,1)} %fusion.9, bf16[2,10,32,384]{3,2,1,0:T(8,128)(2,1)S(1)} %constant_dynamic-update-slice_fusion), kind=kLoop, calls=%fused_computation.31 | loop fusion | bytes 983040
  67.0 0.9 fusion.11
  67.9 1.1 %fusion.12.x_ref = bf16[2,90,32,384]{3,2,1,0:T(8,128)(2,1)} fusion(bf16[2,90,32,384]{3,2,1,0:T(8,128)(2,1)} %fusion.11, bf16[2,10,32,384]{3,2,1,0:T(8,128)(2,1)S(1)} %constant_dynamic-update-slice_fusion), kind=kLoop, calls=%fused_computation.33 | loop fusion | bytes 983040 | tf_op jit(solution)/shard_map/concatenate | solution.py:145
  69.1 16.5 %shard_map.118 = f32[2,32,18,384]{3,2,1,0:T(8,128)} custom-call(bf16[2,90,32,384]{3,2,1,0:T(8,128)(2,1)} %fusion.12.x_ref, f32[152,512]{1,0:T(8,128)} %fusion.13.p_ref), custom_call_target="tpu_custom_call" | custom-call | tf_op jit(solution)/shard_map/pallas_call | solution.py:171
  86.3 4.7 %fusion.31 = f32[2,2,32,384]{3,1,2,0:T(2,128)S(1)} fusion(f32[2,2,32,384]{3,2,1,0:T(8,128)S(1)} %copy-done.1, f32[2,2,32,384]{3,2,1,0:T(8,128)S(1)} %copy-done, f32[2,2,32,384]{3,1,0,2:T(2,128)S(1)} %reduce_sum.9, f32[2,32,18,384]{3,2,1,0:T(8,128)} %shard_map.118), kind=kLoop, calls=%fused_computation.63 | loop fusion | flops 589824 | bytes 3342336 | tf_op jit(solution)/shard_map/add | solution.py:223
  91.1 0.7 copy.71
  (34 shorter events, 3.1 us)
Async XLA Ops:
  0.0 30.0 %copy-start = (f32[2,2,32,384]{3,2,1,0:T(8,128)S(1)}, f32[2,2,32,384]{3,2,1,0:T(8,128)}, u32[]{:S(2)}) copy-start(f32[2,2,32,384]{3,2,1,0:T(8,128)} %param.12) | copy-start | bytes 589828
  0.0 27.4 %copy-start.5 = (f32[128]{0:T(128)S(1)}, f32[128]{0:T(128)}, u32[]{:S(2)}) copy-start(f32[128]{0:T(128)} %param.18) | copy-start | bytes 1540
  0.0 27.4 %copy-start.4 = (f32[128]{0:T(128)S(1)}, f32[128]{0:T(128)}, u32[]{:S(2)}) copy-start(f32[128]{0:T(128)} %param.20) | copy-start | bytes 1540
  0.0 27.4 %copy-start.3 = (f32[128]{0:T(128)S(1)}, f32[128]{0:T(128)}, u32[]{:S(2)}) copy-start(f32[128]{0:T(128)} %param.22) | copy-start | bytes 1540
  0.0 27.5 %copy-start.2 = (bf16[3,3,2,128]{3,2,1,0:T(2,128)(2,1)S(1)}, bf16[3,3,2,128]{3,2,1,0:T(2,128)(2,1)}, u32[]{:S(2)}) copy-start(bf16[3,3,2,128]{3,2,1,0:T(2,128)(2,1)} %param.23) | copy-start | bytes 13828
  1.0 29.0 %collective-permute-start = (bf16[2,2,32,384]{3,2,1,0:T(8,128)(2,1)S(1)}, bf16[2,2,32,384]{3,2,1,0:T(8,128)(2,1)S(1)}, u32[]{:S(2)}, u32[]{:S(2)}) collective-permute-start(bf16[2,2,32,384]{3,2,1,0:T(8,128)(2,1)S(1)} %convert_element_type.77), channel_id=1, source_target_pairs={{0,1},{1,2},{2,3},{3,4},{4,5},{5,6},{6,7},{7,8},{8,9},{9,10},{10,1... | collective-permute-start | bytes 294920 | tf_op jit(solution)/shard_map/ppermute | solution.py:18
  6.0 24.1 %collective-permute-start.1 = (bf16[2,2,32,384]{3,2,1,0:T(8,128)(2,1)S(1)}, bf16[2,2,32,384]{3,2,1,0:T(8,128)(2,1)S(1)}, u32[]{:S(2)}, u32[]{:S(2)}) collective-permute-start(bf16[2,2,32,384]{3,2,1,0:T(8,128)(2,1)S(1)} %convert_element_type.77), channel_id=1, source_target_pairs={{1,0},{2,1},{3,2},{4,3},{5,4},{6,5},{7,6},{8,7},{9,8},{10,9},{11,1... | collective-permute-start | bytes 294920 | tf_op jit(solution)/shard_map/ppermute | solution.py:19
  10.1 27.6 %all-to-all-start = ((f32[2,2,128,384]{3,1,0,2:T(2,128)}), f32[2,2,128,384]{3,1,0,2:T(2,128)S(1)}, u32[]{:S(2)}, u32[]{:S(2)}) async-start(f32[2,2,128,384]{3,1,0,2:T(2,128)} %bitcast.7), calls=%async_computation | async-start | bytes 1572864 | tf_op jit(solution)/shard_map/all_to_all | solution.py:216
  55.1 30.5 %all-to-all-start.1 = ((bf16[256,2,1,384]{3,1,2,0:T(2,128)(2,1)}), bf16[256,2,1,384]{3,1,2,0:T(2,128)(2,1)S(1)}, u32[]{:S(2)}, u32[]{:S(2)}) async-start(bf16[256,2,1,384]{3,1,2,0:T(2,128)(2,1)} %copy.67), calls=%async_computation.1 | async-start | bytes 786432 | tf_op jit(solution)/shard_map/all_to_all | solution.py:220
  69.1 17.3 %copy-start.1 = (f32[2,2,32,384]{3,2,1,0:T(8,128)S(1)}, f32[2,2,32,384]{3,2,1,0:T(8,128)}, u32[]{:S(2)}) copy-start(f32[2,2,32,384]{3,2,1,0:T(8,128)} %param.13) | copy-start | bytes 589828

commit v7 on v6

--- a/solution.py
+++ b/solution.py
@@ -211,10 +211,10 @@
     score_field = score_net(window, w_first, b_first, w_second, b_second, w_third, b_third, w_last)
     groups = lax.axis_size("coil")
     depth, parts, rows, lines = image.shape
-    copies = jnp.broadcast_to(image[:, :, :, None], (depth, parts, rows, groups, lines))
+    copies = jnp.broadcast_to(image.astype(jnp.bfloat16)[:, :, :, None], (depth, parts, rows, groups, lines))
     copies = copies.reshape(depth, parts, rows * groups, lines)
     planes_in = lax.all_to_all(copies, ("slab", "coil"), split_axis=2, concat_axis=0, tiled=True)
-    planes = jnp.transpose(planes_in, (1, 2, 3, 0))
+    planes = jnp.transpose(planes_in, (1, 2, 3, 0)).astype(jnp.float32)
     partial_sum = coil_adjoint(planes, sens, measured, mask)
     by_depth = jnp.transpose(partial_sum, (3, 0, 1, 2)).astype(jnp.bfloat16)
     by_device = lax.all_to_all(by_depth, ("slab", "coil"), split_axis=0, concat_axis=2, tiled=True)

time: 92.3 us -> 93.1 us (level)
  other arithmetic: 15.8 us -> 17.1 us
    convert_element_type x0 -> x2, local copies, waits for them, and re-layouts: none -> 1.3 us  [the longest x1 1.23 us: on_device(): planes = jnp.transpose(planes_in, (1, 2, 3, 0)).astype(jnp.float32)]
    all_to_all x1 -> x0, local copies, waits for them, and re-layouts: 1.22 us -> none  [on_device(): lax.all_to_all(copies, ('slab', 'coil'), split_axis=2, concat_axis=0, til...]
    unnamed x26 -> x17, local copies, waits for them, and re-layouts: 12.3 us -> 11.1 us
where the time goes in v7:
time: 93.1 us; the launch traced here: 92.5 us
  Pallas kernels  30.3 us (33%)
  starting transfers between devices  27.6 us (30%)
  local copies, waits for them, and re-layouts  17.4 us (19%)
  other arithmetic  17.1 us (18%)
    pallas_call x1, Pallas kernels, score_net(): pl.pallas_call(net_kernel, grid=(slice_count, row_count // rows), in_spec...  16.5 us
    pallas_call x1, Pallas kernels, coil_adjoint(): pl.pallas_call(adjoint_kernel, grid=(coils,), in_specs=[pl.BlockSpec((2,...  13.9 us
    unnamed x17, local copies, waits for them, and re-layouts  11.1 us
    all_to_all x1, starting transfers between devices, on_device(): lax.all_to_all(copies, ('slab', 'coil'), split_axis=2, concat_axis=0, til...  10.9 us
    all_to_all x1, starting transfers between devices, on_device(): lax.all_to_all(by_depth, ('slab', 'coil'), split_axis=0, concat_axis=2, t...  9.77 us
    add x1, other arithmetic, on_device(): return image + STEP_SIZE * (score_field - gradient) + noise  5 us
    ppermute x1, starting transfers between devices, with_halo(): before = lax.ppermute(last, axis, up)  4.94 us
    convert_element_type x2, other arithmetic, dft_tables(): (jnp.sin(phase_angle) * norm_scale).astype(jnp.bfloat16)  3.7 us
  transfers between devices with their start and end apart: 4, of which 0 were waited for; matrix products, arithmetic and copies ran while one was open for 25% of the time, Pallas kernels for 18%

profile of v7, /device:TPU:1, one launch (start us, length us, event | category | flops | bytes accessed | tf_op | source)
XLA Modules:
  0.0 92.5 jit_solution(9732714494262794171)
XLA Ops:
  0.0 1.0 %convert_element_type.89 = bf16[2,2,32,384]{3,2,1,0:T(8,128)(2,1)S(1)} convert(f32[2,2,32,384]{3,2,1,0:T(8,128)} %param.12) | non-fusion elementwise | flops 49152 | bytes 294912 | tf_op jit(solution)/shard_map/convert_element_type | solution.py:210
  1.0 4.9 %collective-permute-start = (bf16[2,2,32,384]{3,2,1,0:T(8,128)(2,1)S(1)}, bf16[2,2,32,384]{3,2,1,0:T(8,128)(2,1)S(1)}, u32[]{:S(2)}, u32[]{:S(2)}) collective-permute-start(bf16[2,2,32,384]{3,2,1,0:T(8,128)(2,1)S(1)} %convert_element_type.89), channel_id=1, source_target_pairs={{0,1},{1,2},{2,3},{3,4},{4,5},{5,6},{6,7},{7,8},{8,9},{9,10},{10,1... | collective-permute-start | bytes 294920 | tf_op jit(solution)/shard_map/ppermute | solution.py:18
  6.0 1.9 %collective-permute-start.1 = (bf16[2,2,32,384]{3,2,1,0:T(8,128)(2,1)S(1)}, bf16[2,2,32,384]{3,2,1,0:T(8,128)(2,1)S(1)}, u32[]{:S(2)}, u32[]{:S(2)}) collective-permute-start(bf16[2,2,32,384]{3,2,1,0:T(8,128)(2,1)S(1)} %convert_element_type.89), channel_id=1, source_target_pairs={{1,0},{2,1},{3,2},{4,3},{5,4},{6,5},{7,6},{8,7},{9,8},{10,9},{11,1... | collective-permute-start | bytes 294920 | tf_op jit(solution)/shard_map/ppermute | solution.py:19
  8.0 1.0 %broadcast_in_dim.2 = bf16[2,2,32,4,384]{4,1,0,3,2:T(2,128)(2,1)} broadcast(bf16[2,2,32,384]{3,1,0,2:T(2,128)(2,1)S(1)} %copy.65), dimensions={0,1,2,4} | broadcast | bytes 491520 | tf_op jit(solution)/shard_map/broadcast_in_dim | solution.py:214
  8.9 10.9 %all-to-all-start = ((bf16[2,2,128,384]{3,1,0,2:T(2,128)(2,1)}), bf16[2,2,128,384]{3,1,0,2:T(2,128)(2,1)S(1)}, u32[]{:S(2)}, u32[]{:S(2)}) async-start(bf16[2,2,128,384]{3,1,0,2:T(2,128)(2,1)} %bitcast.7), calls=%async_computation | async-start | bytes 786432 | tf_op jit(solution)/shard_map/all_to_all | solution.py:216
  19.9 2.6 %multiply_convert_fusion = (bf16[384,384]{1,0:T(8,128)(2,1)S(1)}, bf16[384,384]{1,0:T(8,128)(2,1)S(1)}) fusion(), kind=kLoop, calls=%fused_computation.20 | loop fusion | flops 1916928 | bytes 589824 | tf_op jit(solution)/shard_map/convert_element_type | solution.py:31
  22.5 1.1 %multiply_convert_fusion.2 = (bf16[256,256]{1,0:T(8,128)(2,1)S(1)}, bf16[256,256]{1,0:T(8,128)(2,1)S(1)}) fusion(), kind=kLoop, calls=%fused_computation.48 | loop fusion | flops 1179648 | bytes 262144 | tf_op jit(solution)/shard_map/convert_element_type | solution.py:31
  23.6 0.9 copy.62
  24.5 0.9 copy.63
  25.3 0.8 copy.60
  26.3 0.7 pad_maximum_fusion.4
  27.1 0.7 convert_element_type.95
  27.8 0.9 pad_maximum_fusion.ty_ref
  28.7 0.7 fusion.13.p_ref
  29.4 0.7 pad_maximum_fusion.1.tz_ref
  30.3 1.1 %fusion.5 = bf16[2,90,32,384]{3,2,1,0:T(8,128)(2,1)} fusion(bf16[2,10,32,384]{3,2,1,0:T(8,128)(2,1)S(1)} %constant_dynamic-update-slice_fusion), kind=kLoop, calls=%fused_computation.26 | loop fusion | bytes 983040
  31.4 0.9 %fusion.6 = bf16[2,90,32,384]{3,2,1,0:T(8,128)(2,1)} fusion(bf16[2,90,32,384]{3,2,1,0:T(8,128)(2,1)} %fusion.5, bf16[2,10,32,384]{3,2,1,0:T(8,128)(2,1)S(1)} %constant_dynamic-update-slice_fusion), kind=kLoop, calls=%fused_computation.27 | loop fusion | bytes 983040
  32.3 1.2 %fusion.7 = bf16[2,90,32,384]{3,2,1,0:T(8,128)(2,1)} fusion(bf16[2,90,32,384]{3,2,1,0:T(8,128)(2,1)} %fusion.6, bf16[2,10,32,384]{3,2,1,0:T(8,128)(2,1)S(1)} %constant_dynamic-update-slice_fusion), kind=kLoop, calls=%fused_computation.28 | loop fusion | bytes 983040
  33.5 1.1 %fusion.8 = bf16[2,90,32,384]{3,2,1,0:T(8,128)(2,1)} fusion(bf16[2,90,32,384]{3,2,1,0:T(8,128)(2,1)} %fusion.7, bf16[2,10,32,384]{3,2,1,0:T(8,128)(2,1)S(1)} %constant_dynamic-update-slice_fusion), kind=kLoop, calls=%fused_computation.29 | loop fusion | bytes 983040
  36.5 0.7 constant_dynamic-update-slice_fusion.6
  38.1 1.2 %copy.66 = f32[256,2,1,384]{0,3,2,1:T(8,128)} copy(f32[256,2,1,384]{3,1,0,2:T(2,128)S(1)} %bitcast.32) | data formatting | bytes 1572864 | tf_op jit(solution)/shard_map/convert_element_type | solution.py:217
  39.4 13.9 %shard_map.119 = f32[2,1,384,256]{3,2,1,0:T(8,128)} custom-call(f32[2,1,384,256]{3,2,1,0:T(8,128)} %bitcast.33, bf16[4,2,1,384,256]{4,3,2,1,0:T(8,128)(2,1)} %sens_ref.1, bf16[4,2,1,384,256]{4,3,2,1,0:T(8,128)(2,1)} %meas_ref.1, s32[384,256]{1,0:T(8,128)} %mask_ref.1, bf16[768,384]{1,0:T(8,128)(2,1)} %pad_maximum_fusion.ty_ref, ...), custom_call_target="tpu_custom_call" | custom-call | tf_op jit(solution)/shard_map/pallas_call | solution.py:95
  53.2 1.2 %convert_bitcast_fusion = bf16[256,2,1,384]{0,3,2,1:T(8,128)(2,1)S(1)} fusion(f32[2,1,384,256]{3,2,1,0:T(8,128)} %shard_map.119), kind=kLoop, calls=%fused_computation.35 | loop fusion | flops 196608 | bytes 1179648 | tf_op jit(solution)/shard_map/convert_element_type | solution.py:219
  54.4 1.1 %copy.67 = bf16[256,2,1,384]{3,1,2,0:T(2,128)(2,1)} copy(bf16[256,2,1,384]{0,3,2,1:T(8,128)(2,1)S(1)} %convert_bitcast_fusion) | data formatting | bytes 786432 | tf_op jit(solution)/shard_map/convert_element_type | solution.py:219
  55.5 9.8 %all-to-all-start.1 = ((bf16[256,2,1,384]{3,1,2,0:T(2,128)(2,1)}), bf16[256,2,1,384]{3,1,2,0:T(2,128)(2,1)S(1)}, u32[]{:S(2)}, u32[]{:S(2)}) async-start(bf16[256,2,1,384]{3,1,2,0:T(2,128)(2,1)} %copy.67), calls=%async_computation.1 | async-start | bytes 786432 | tf_op jit(solution)/shard_map/all_to_all | solution.py:220
  65.3 1.0 %fusion.9 = bf16[2,90,32,384]{3,2,1,0:T(8,128)(2,1)} fusion(bf16[2,90,32,384]{3,2,1,0:T(8,128)(2,1)} %constant_dynamic-update-slice_fusion.5, bf16[2,10,32,384]{3,2,1,0:T(8,128)(2,1)S(1)} %constant_dynamic-update-slice_fusion), kind=kLoop, calls=%fused_computation.30 | loop fusion | bytes 983040
  66.4 1.1 %fusion.10 = bf16[2,90,32,384]{3,2,1,0:T(8,128)(2,1)} fusion(bf16[2,90,32,384]{3,2,1,0:T(8,128)(2,1)} %fusion.9, bf16[2,10,32,384]{3,2,1,0:T(8,128)(2,1)S(1)} %constant_dynamic-update-slice_fusion), kind=kLoop, calls=%fused_computation.31 | loop fusion | bytes 983040
  67.5 0.9 fusion.11
  68.4 1.2 %fusion.12.x_ref = bf16[2,90,32,384]{3,2,1,0:T(8,128)(2,1)} fusion(bf16[2,90,32,384]{3,2,1,0:T(8,128)(2,1)} %fusion.11, bf16[2,10,32,384]{3,2,1,0:T(8,128)(2,1)S(1)} %constant_dynamic-update-slice_fusion), kind=kLoop, calls=%fused_computation.33 | loop fusion | bytes 983040 | tf_op jit(solution)/shard_map/concatenate | solution.py:145
  69.6 16.5 %shard_map.118 = f32[2,32,18,384]{3,2,1,0:T(8,128)} custom-call(bf16[2,90,32,384]{3,2,1,0:T(8,128)(2,1)} %fusion.12.x_ref, f32[152,512]{1,0:T(8,128)} %fusion.13.p_ref), custom_call_target="tpu_custom_call" | custom-call | tf_op jit(solution)/shard_map/pallas_call | solution.py:171
  86.8 5.0 %fusion.31 = f32[2,2,32,384]{3,1,2,0:T(2,128)S(1)} fusion(f32[2,2,32,384]{3,2,1,0:T(8,128)S(1)} %copy-done.1, f32[2,2,32,384]{3,2,1,0:T(8,128)S(1)} %copy-done, f32[2,2,32,384]{3,1,0,2:T(2,128)S(1)} %reduce_sum.9, f32[2,32,18,384]{3,2,1,0:T(8,128)} %shard_map.118), kind=kLoop, calls=%fused_computation.64 | loop fusion | flops 589824 | bytes 3342336 | tf_op jit(solution)/shard_map/add | solution.py:223
  91.8 0.7 copy.71
  (27 shorter events, 4.1 us)
Async XLA Ops:
  0.0 30.2 %copy-start = (f32[2,2,32,384]{3,2,1,0:T(8,128)S(1)}, f32[2,2,32,384]{3,2,1,0:T(8,128)}, u32[]{:S(2)}) copy-start(f32[2,2,32,384]{3,2,1,0:T(8,128)} %param.12) | copy-start | bytes 589828
  1.0 29.2 %collective-permute-start = (bf16[2,2,32,384]{3,2,1,0:T(8,128)(2,1)S(1)}, bf16[2,2,32,384]{3,2,1,0:T(8,128)(2,1)S(1)}, u32[]{:S(2)}, u32[]{:S(2)}) collective-permute-start(bf16[2,2,32,384]{3,2,1,0:T(8,128)(2,1)S(1)} %convert_element_type.89), channel_id=1, source_target_pairs={{0,1},{1,2},{2,3},{3,4},{4,5},{5,6},{6,7},{7,8},{8,9},{9,10},{10,1... | collective-permute-start | bytes 294920 | tf_op jit(solution)/shard_map/ppermute | solution.py:18
  6.0 24.3 %collective-permute-start.1 = (bf16[2,2,32,384]{3,2,1,0:T(8,128)(2,1)S(1)}, bf16[2,2,32,384]{3,2,1,0:T(8,128)(2,1)S(1)}, u32[]{:S(2)}, u32[]{:S(2)}) collective-permute-start(bf16[2,2,32,384]{3,2,1,0:T(8,128)(2,1)S(1)} %convert_element_type.89), channel_id=1, source_target_pairs={{1,0},{2,1},{3,2},{4,3},{5,4},{6,5},{7,6},{8,7},{9,8},{10,9},{11,1... | collective-permute-start | bytes 294920 | tf_op jit(solution)/shard_map/ppermute | solution.py:19
  8.9 28.9 %all-to-all-start = ((bf16[2,2,128,384]{3,1,0,2:T(2,128)(2,1)}), bf16[2,2,128,384]{3,1,0,2:T(2,128)(2,1)S(1)}, u32[]{:S(2)}, u32[]{:S(2)}) async-start(bf16[2,2,128,384]{3,1,0,2:T(2,128)(2,1)} %bitcast.7), calls=%async_computation | async-start | bytes 786432 | tf_op jit(solution)/shard_map/all_to_all | solution.py:216
  55.5 30.5 %all-to-all-start.1 = ((bf16[256,2,1,384]{3,1,2,0:T(2,128)(2,1)}), bf16[256,2,1,384]{3,1,2,0:T(2,128)(2,1)S(1)}, u32[]{:S(2)}, u32[]{:S(2)}) async-start(bf16[256,2,1,384]{3,1,2,0:T(2,128)(2,1)} %copy.67), calls=%async_computation.1 | async-start | bytes 786432 | tf_op jit(solution)/shard_map/all_to_all | solution.py:220
  69.6 17.3 %copy-start.1 = (f32[2,2,32,384]{3,2,1,0:T(8,128)S(1)}, f32[2,2,32,384]{3,2,1,0:T(8,128)}, u32[]{:S(2)}) copy-start(f32[2,2,32,384]{3,2,1,0:T(8,128)} %param.13) | copy-start | bytes 589828

commit v8 on v6

--- a/solution.py
+++ b/solution.py
@@ -1,3 +1,5 @@
+import ml_dtypes
+import numpy as np
 import jax
 import jax.numpy as jnp
 from jax import lax
@@ -22,13 +24,13 @@
 
 
 def dft_tables(length):
-    line_index = jnp.arange(length, dtype=jnp.int32)
+    line_index = np.arange(length, dtype=np.int64)
     phase_turns = line_index[:, None] * line_index[None, :] % length
-    phase_angle = phase_turns.astype(jnp.float32) * (2.0 * jnp.pi / length)
-    norm_scale = 1.0 / jnp.sqrt(jnp.float32(length))
+    phase_angle = phase_turns.astype(np.float32) * np.float32(2.0 * np.pi / length)
+    norm_scale = np.float32(1.0) / np.sqrt(np.float32(length))
     return (
-        (jnp.cos(phase_angle) * norm_scale).astype(jnp.bfloat16),
-        (jnp.sin(phase_angle) * norm_scale).astype(jnp.bfloat16),
+        (np.cos(phase_angle) * norm_scale).astype(ml_dtypes.bfloat16),
+        (np.sin(phase_angle) * norm_scale).astype(ml_dtypes.bfloat16),
     )
 
 
@@ -89,8 +91,8 @@
     nz = planes.shape[3]
     cos_y, sin_y = dft_tables(ny)
     cos_z, sin_z = dft_tables(nz)
-    ty = jnp.concatenate([cos_y, sin_y], axis=0)
-    tz = jnp.concatenate([cos_z, sin_z], axis=1)
+    ty = jnp.asarray(np.concatenate([cos_y, sin_y], axis=0))
+    tz = jnp.asarray(np.concatenate([cos_z, sin_z], axis=1))
     coils = sens.shape[0]
     return pl.pallas_call(
         adjoint_kernel,

time: 92.3 us -> 88.7 us (0.961)
  other arithmetic: 15.8 us -> 11.5 us
  starting transfers between devices: 27.6 us -> 23.5 us
  waiting for transfers between devices: 0.01 us -> 4.06 us
    all_to_all x1, waiting for transfers between devices: 0.01 us -> 4.05 us  [on_device(): lax.all_to_all(copies, ('slab', 'coil'), split_axis=2, concat_axis=0, til...]
    all_to_all x1, starting transfers between devices: 9.76 us -> 5.72 us  [on_device(): lax.all_to_all(by_depth, ('slab', 'coil'), split_axis=0, concat_axis=2, t...]
    convert_element_type x2 -> x0, other arithmetic: 3.7 us -> none  [dft_tables(): (jnp.sin(phase_angle) * norm_scale).astype(jnp.bfloat16)]
    concatenate x2 -> x0, other arithmetic: 1.62 us -> none  [the longest x1 0.9 us: coil_adjoint(): ty = jnp.concatenate([cos_y, sin_y], axis=0)]
    unnamed x26 -> x18, local copies, waits for them, and re-layouts: 12.3 us -> 12.2 us
  transfers between devices with their start and end apart: 4 -> 4, of which waited for: 0 -> 1; matrix products, arithmetic and copies ran while one was open for 25% -> 21% of each run, Pallas kernels for 18% -> 19%
where the time goes in v8:
time: 88.7 us; the launch traced here: 88.1 us
  Pallas kernels  30.4 us (34%)
  starting transfers between devices  23.5 us (26%)
  local copies, waits for them, and re-layouts  18.5 us (21%)
  other arithmetic  11.5 us (13%)
  waiting for transfers between devices  4.06 us (5%)
    pallas_call x1, Pallas kernels, score_net(): pl.pallas_call(net_kernel, grid=(slice_count, row_count // rows), in_spec...  16.5 us
    pallas_call x1, Pallas kernels, coil_adjoint(): pl.pallas_call(adjoint_kernel, grid=(coils,), in_specs=[pl.BlockSpec((2,...  13.9 us
    unnamed x18, local copies, waits for them, and re-layouts  12.2 us
    all_to_all x1, starting transfers between devices, on_device(): lax.all_to_all(copies, ('slab', 'coil'), split_axis=2, concat_axis=0, til...  10.9 us
    all_to_all x1, starting transfers between devices, on_device(): lax.all_to_all(by_depth, ('slab', 'coil'), split_axis=0, concat_axis=2, t...  5.72 us
    add x1, other arithmetic, on_device(): return image + STEP_SIZE * (score_field - gradient) + noise  5.05 us
    ppermute x1, starting transfers between devices, with_halo(): before = lax.ppermute(last, axis, up)  4.94 us
    all_to_all x1, waiting for transfers between devices, on_device(): lax.all_to_all(copies, ('slab', 'coil'), split_axis=2, concat_axis=0, til...  4.05 us
  transfers between devices with their start and end apart: 4, of which 1 were waited for; matrix products, arithmetic and copies ran while one was open for 21% of the time, Pallas kernels for 19%

profile of v8, /device:TPU:1, one launch (start us, length us, event | category | flops | bytes accessed | tf_op | source)
XLA Modules:
  0.0 88.1 jit_solution(12083597063933079700)
XLA Ops:
  0.0 1.0 %convert_element_type.55 = bf16[2,2,32,384]{3,2,1,0:T(8,128)(2,1)S(1)} convert(f32[2,2,32,384]{3,2,1,0:T(8,128)} %param.14) | non-fusion elementwise | flops 49152 | bytes 294912 | tf_op jit(solution)/shard_map/convert_element_type | solution.py:212
  1.0 4.9 %collective-permute-start = (bf16[2,2,32,384]{3,2,1,0:T(8,128)(2,1)S(1)}, bf16[2,2,32,384]{3,2,1,0:T(8,128)(2,1)S(1)}, u32[]{:S(2)}, u32[]{:S(2)}) collective-permute-start(bf16[2,2,32,384]{3,2,1,0:T(8,128)(2,1)S(1)} %convert_element_type.55), channel_id=1, source_target_pairs={{0,1},{1,2},{2,3},{3,4},{4,5},{5,6},{6,7},{7,8},{8,9},{9,10},{10,1... | collective-permute-start | bytes 294920 | tf_op jit(solution)/shard_map/ppermute | solution.py:20
  6.0 1.9 %collective-permute-start.1 = (bf16[2,2,32,384]{3,2,1,0:T(8,128)(2,1)S(1)}, bf16[2,2,32,384]{3,2,1,0:T(8,128)(2,1)S(1)}, u32[]{:S(2)}, u32[]{:S(2)}) collective-permute-start(bf16[2,2,32,384]{3,2,1,0:T(8,128)(2,1)S(1)} %convert_element_type.55), channel_id=1, source_target_pairs={{1,0},{2,1},{3,2},{4,3},{5,4},{6,5},{7,6},{8,7},{9,8},{10,9},{11,1... | collective-permute-start | bytes 294920 | tf_op jit(solution)/shard_map/ppermute | solution.py:21
  7.9 1.1 %copy.67 = f32[2,2,32,384]{3,1,0,2:T(2,128)S(1)} copy(f32[2,2,32,384]{3,2,1,0:T(8,128)} %param.14) | data formatting | bytes 393216 | tf_op args[0]
  9.0 1.1 %broadcast_in_dim.2 = f32[2,2,32,4,384]{4,1,0,3,2:T(2,128)} broadcast(f32[2,2,32,384]{3,1,0,2:T(2,128)S(1)} %copy.67), dimensions={0,1,2,4} | broadcast | bytes 983040 | tf_op jit(solution)/shard_map/broadcast_in_dim | solution.py:216
  10.1 10.9 %all-to-all-start = ((f32[2,2,128,384]{3,1,0,2:T(2,128)}), f32[2,2,128,384]{3,1,0,2:T(2,128)S(1)}, u32[]{:S(2)}, u32[]{:S(2)}) async-start(f32[2,2,128,384]{3,1,0,2:T(2,128)} %bitcast.7), calls=%async_computation | async-start | bytes 1572864 | tf_op jit(solution)/shard_map/all_to_all | solution.py:218
  21.0 0.9 copy.64
  21.9 0.9 copy.65
  22.8 0.8 copy.62
  23.7 0.7 pad_maximum_fusion.2
  24.5 0.7 convert_element_type.61
  25.2 0.8 fusion.8.p_ref
  26.1 1.1 %fusion = bf16[2,90,32,384]{3,2,1,0:T(8,128)(2,1)} fusion(bf16[2,10,32,384]{3,2,1,0:T(8,128)(2,1)S(1)} %constant_dynamic-update-slice_fusion), kind=kLoop, calls=%fused_computation.16 | loop fusion | bytes 983040
  27.2 0.9 %fusion.1 = bf16[2,90,32,384]{3,2,1,0:T(8,128)(2,1)} fusion(bf16[2,90,32,384]{3,2,1,0:T(8,128)(2,1)} %fusion, bf16[2,10,32,384]{3,2,1,0:T(8,128)(2,1)S(1)} %constant_dynamic-update-slice_fusion), kind=kLoop, calls=%fused_computation.17 | loop fusion | bytes 983040
  28.1 1.2 %fusion.2 = bf16[2,90,32,384]{3,2,1,0:T(8,128)(2,1)} fusion(bf16[2,90,32,384]{3,2,1,0:T(8,128)(2,1)} %fusion.1, bf16[2,10,32,384]{3,2,1,0:T(8,128)(2,1)S(1)} %constant_dynamic-update-slice_fusion), kind=kLoop, calls=%fused_computation.18 | loop fusion | bytes 983040
  29.3 1.1 %fusion.3 = bf16[2,90,32,384]{3,2,1,0:T(8,128)(2,1)} fusion(bf16[2,90,32,384]{3,2,1,0:T(8,128)(2,1)} %fusion.2, bf16[2,10,32,384]{3,2,1,0:T(8,128)(2,1)S(1)} %constant_dynamic-update-slice_fusion), kind=kLoop, calls=%fused_computation.19 | loop fusion | bytes 983040
  31.0 0.7 constant_dynamic-update-slice_fusion.8
  31.6 0.6 constant_dynamic-update-slice_fusion.7
  32.3 0.7 constant_dynamic-update-slice_fusion.6
  33.6 4.1 %all-to-all-done = f32[2,2,128,384]{3,1,0,2:T(2,128)S(1)} async-done(((f32[2,2,128,384]{3,1,0,2:T(2,128)}), f32[2,2,128,384]{3,1,0,2:T(2,128)S(1)}, u32[]{:S(2)}, u32[]{:S(2)}) %all-to-all-start) | async-done | bytes 786464 | tf_op jit(solution)/shard_map/all_to_all | solution.py:218
  37.7 1.2 %copy.68 = f32[256,2,1,384]{0,3,2,1:T(8,128)} copy(f32[256,2,1,384]{3,1,0,2:T(2,128)S(1)} %bitcast.30) | data formatting | bytes 1572864 | tf_op jit(solution)/shard_map/all_to_all | solution.py:218
  38.9 13.9 %shard_map.137 = f32[2,1,384,256]{3,2,1,0:T(8,128)} custom-call(f32[2,1,384,256]{3,2,1,0:T(8,128)} %bitcast.32, bf16[4,2,1,384,256]{4,3,2,1,0:T(8,128)(2,1)} %sens_ref.1, bf16[4,2,1,384,256]{4,3,2,1,0:T(8,128)(2,1)} %meas_ref.1, s32[384,256]{1,0:T(8,128)} %mask_ref.1, bf16[768,384]{1,0:T(8,128)(2,1)} %constant.13.clone.ty_ref, ...), custom_call_target="tpu_custom_call" | custom-call | tf_op jit(solution)/shard_map/pallas_call | solution.py:97
  52.8 1.2 %convert_bitcast_fusion = bf16[256,2,1,384]{0,3,2,1:T(8,128)(2,1)S(1)} fusion(f32[2,1,384,256]{3,2,1,0:T(8,128)} %shard_map.137), kind=kLoop, calls=%fused_computation.24 | loop fusion | flops 196608 | bytes 1179648 | tf_op jit(solution)/shard_map/convert_element_type | solution.py:221
  53.9 1.1 %copy.69 = bf16[256,2,1,384]{3,1,2,0:T(2,128)(2,1)} copy(bf16[256,2,1,384]{0,3,2,1:T(8,128)(2,1)S(1)} %convert_bitcast_fusion) | data formatting | bytes 786432 | tf_op jit(solution)/shard_map/convert_element_type | solution.py:221
  55.1 5.7 %all-to-all-start.1 = ((bf16[256,2,1,384]{3,1,2,0:T(2,128)(2,1)}), bf16[256,2,1,384]{3,1,2,0:T(2,128)(2,1)S(1)}, u32[]{:S(2)}, u32[]{:S(2)}) async-start(bf16[256,2,1,384]{3,1,2,0:T(2,128)(2,1)} %copy.69), calls=%async_computation.1 | async-start | bytes 786432 | tf_op jit(solution)/shard_map/all_to_all | solution.py:222
  60.8 1.0 %fusion.4 = bf16[2,90,32,384]{3,2,1,0:T(8,128)(2,1)} fusion(bf16[2,90,32,384]{3,2,1,0:T(8,128)(2,1)} %constant_dynamic-update-slice_fusion.5, bf16[2,10,32,384]{3,2,1,0:T(8,128)(2,1)S(1)} %constant_dynamic-update-slice_fusion), kind=kLoop, calls=%fused_computation.20 | loop fusion | bytes 983040
  61.8 1.1 %fusion.5 = bf16[2,90,32,384]{3,2,1,0:T(8,128)(2,1)} fusion(bf16[2,90,32,384]{3,2,1,0:T(8,128)(2,1)} %fusion.4, bf16[2,10,32,384]{3,2,1,0:T(8,128)(2,1)S(1)} %constant_dynamic-update-slice_fusion), kind=kLoop, calls=%fused_computation.21 | loop fusion | bytes 983040
  63.0 0.9 %fusion.6 = bf16[2,90,32,384]{3,2,1,0:T(8,128)(2,1)} fusion(bf16[2,90,32,384]{3,2,1,0:T(8,128)(2,1)} %fusion.5, bf16[2,10,32,384]{3,2,1,0:T(8,128)(2,1)S(1)} %constant_dynamic-update-slice_fusion), kind=kLoop, calls=%fused_computation.22 | loop fusion | bytes 983040
  63.9 1.1 %fusion.7.x_ref = bf16[2,90,32,384]{3,2,1,0:T(8,128)(2,1)} fusion(bf16[2,90,32,384]{3,2,1,0:T(8,128)(2,1)} %fusion.6, bf16[2,10,32,384]{3,2,1,0:T(8,128)(2,1)S(1)} %constant_dynamic-update-slice_fusion), kind=kLoop, calls=%fused_computation.23 | loop fusion | bytes 983040 | tf_op jit(solution)/shard_map/concatenate | solution.py:147
  65.0 16.5 %shard_map.136 = f32[2,32,18,384]{3,2,1,0:T(8,128)} custom-call(bf16[2,90,32,384]{3,2,1,0:T(8,128)(2,1)} %fusion.7.x_ref, f32[152,512]{1,0:T(8,128)} %fusion.8.p_ref), custom_call_target="tpu_custom_call" | custom-call | tf_op jit(solution)/shard_map/pallas_call | solution.py:173
  82.3 5.0 %fusion.20 = f32[2,2,32,384]{3,1,2,0:T(2,128)S(1)} fusion(f32[2,2,32,384]{3,2,1,0:T(8,128)S(1)} %copy-done.1, f32[2,2,32,384]{3,2,1,0:T(8,128)S(1)} %copy-done, f32[2,2,32,384]{3,1,0,2:T(2,128)S(1)} %reduce_sum.9, f32[2,32,18,384]{3,2,1,0:T(8,128)} %shard_map.136), kind=kLoop, calls=%fused_computation.41 | loop fusion | flops 589824 | bytes 3342336 | tf_op jit(solution)/shard_map/add | solution.py:225
  87.4 0.7 copy.73
  (22 shorter events, 2.4 us)
Async XLA Ops:
  0.0 26.0 %copy-start = (f32[2,2,32,384]{3,2,1,0:T(8,128)S(1)}, f32[2,2,32,384]{3,2,1,0:T(8,128)}, u32[]{:S(2)}) copy-start(f32[2,2,32,384]{3,2,1,0:T(8,128)} %param.14) | copy-start | bytes 589828
  1.0 25.0 %collective-permute-start = (bf16[2,2,32,384]{3,2,1,0:T(8,128)(2,1)S(1)}, bf16[2,2,32,384]{3,2,1,0:T(8,128)(2,1)S(1)}, u32[]{:S(2)}, u32[]{:S(2)}) collective-permute-start(bf16[2,2,32,384]{3,2,1,0:T(8,128)(2,1)S(1)} %convert_element_type.55), channel_id=1, source_target_pairs={{0,1},{1,2},{2,3},{3,4},{4,5},{5,6},{6,7},{7,8},{8,9},{9,10},{10,1... | collective-permute-start | bytes 294920 | tf_op jit(solution)/shard_map/ppermute | solution.py:20
  6.0 20.1 %collective-permute-start.1 = (bf16[2,2,32,384]{3,2,1,0:T(8,128)(2,1)S(1)}, bf16[2,2,32,384]{3,2,1,0:T(8,128)(2,1)S(1)}, u32[]{:S(2)}, u32[]{:S(2)}) collective-permute-start(bf16[2,2,32,384]{3,2,1,0:T(8,128)(2,1)S(1)} %convert_element_type.55), channel_id=1, source_target_pairs={{1,0},{2,1},{3,2},{4,3},{5,4},{6,5},{7,6},{8,7},{9,8},{10,9},{11,1... | collective-permute-start | bytes 294920 | tf_op jit(solution)/shard_map/ppermute | solution.py:21
  10.1 27.6 %all-to-all-start = ((f32[2,2,128,384]{3,1,0,2:T(2,128)}), f32[2,2,128,384]{3,1,0,2:T(2,128)S(1)}, u32[]{:S(2)}, u32[]{:S(2)}) async-start(f32[2,2,128,384]{3,1,0,2:T(2,128)} %bitcast.7), calls=%async_computation | async-start | bytes 1572864 | tf_op jit(solution)/shard_map/all_to_all | solution.py:218
  55.1 26.5 %all-to-all-start.1 = ((bf16[256,2,1,384]{3,1,2,0:T(2,128)(2,1)}), bf16[256,2,1,384]{3,1,2,0:T(2,128)(2,1)S(1)}, u32[]{:S(2)}, u32[]{:S(2)}) async-start(bf16[256,2,1,384]{3,1,2,0:T(2,128)(2,1)} %copy.69), calls=%async_computation.1 | async-start | bytes 786432 | tf_op jit(solution)/shard_map/all_to_all | solution.py:222
  65.0 17.3 %copy-start.1 = (f32[2,2,32,384]{3,2,1,0:T(8,128)S(1)}, f32[2,2,32,384]{3,2,1,0:T(8,128)}, u32[]{:S(2)}) copy-start(f32[2,2,32,384]{3,2,1,0:T(8,128)} %param.15) | copy-start | bytes 589828

commit v9 on v8

--- a/solution.py
+++ b/solution.py
@@ -115,7 +115,7 @@
     taps_in = x_ref.shape[1]
     rows = x_ref.shape[2]
     cols = x_ref.shape[3]
-    outs = q_ref.shape[2]
+    outs = q_ref.shape[1]
     x = jnp.concatenate([x_ref[0, :, row, :] for row in range(rows)], axis=1)
     w1 = p_ref[:width, 0:taps_in].astype(jnp.bfloat16)
     w2 = p_ref[:width, width : 2 * width].astype(jnp.bfloat16)
@@ -132,7 +132,7 @@
     h = jax.nn.silu(h).astype(jnp.bfloat16)
     q = jnp.dot(wl, h, preferred_element_type=jnp.float32)
     for row in range(rows):
-        q_ref[0, row] = q[:, row * cols : (row + 1) * cols]
+        q_ref[0, :, row, :] = q[:, row * cols : (row + 1) * cols]
 
 
 def score_net(window, w_first, b_first, w_second, b_second, w_third, b_third, w_last):
@@ -177,18 +177,18 @@
             pl.BlockSpec((1, taps_in, rows, col_count), lambda z, n: (z, 0, n, 0)),
             pl.BlockSpec(packed.shape, lambda z, n: (0, 0)),
         ],
-        out_specs=pl.BlockSpec((1, rows, outs, col_count), lambda z, n: (z, n, 0, 0)),
-        out_shape=jax.ShapeDtypeStruct((slice_count, row_count, outs, col_count), jnp.float32),
+        out_specs=pl.BlockSpec((1, outs, rows, col_count), lambda z, n: (z, 0, n, 0)),
+        out_shape=jax.ShapeDtypeStruct((slice_count, outs, row_count, col_count), jnp.float32),
     )(columns, packed)
-    q = jnp.pad(q, ((0, 0), (1, 1), (0, 0), (1, 1)))
-    score_field = jnp.zeros((slice_count, row_count, 2, col_count), jnp.float32)
+    q = jnp.pad(q, ((0, 0), (0, 0), (1, 1), (1, 1)))
+    score_field = jnp.zeros((slice_count, 2, row_count, col_count), jnp.float32)
     for shift_x in range(3):
         for shift_y in range(3):
             tap = (shift_x * 3 + shift_y) * 2
             score_field = score_field + q[
-                :, shift_x : shift_x + row_count, tap : tap + 2, shift_y : shift_y + col_count
+                :, tap : tap + 2, shift_x : shift_x + row_count, shift_y : shift_y + col_count
             ]
-    return jnp.transpose(score_field, (0, 2, 1, 3))
+    return score_field
 
 
 def slab_slices(image):

time: 88.7 us -> 85.8 us (0.967)
  other arithmetic: 11.5 us -> 9.05 us
    add x1, other arithmetic: 5.05 us -> 2.61 us  [on_device(): return image + STEP_SIZE * (score_field - gradient) + noise]
  transfers between devices with their start and end apart: 4 -> 4, of which waited for: 1 -> 1; matrix products, arithmetic and copies ran while one was open for 21% -> 22% of each run, Pallas kernels for 19% -> 20%
where the time goes in v9:
time: 85.8 us; the launch traced here: 85.1 us
  Pallas kernels  30.6 us (36%)
  starting transfers between devices  23.5 us (27%)
  local copies, waits for them, and re-layouts  17.8 us (21%)
  other arithmetic  9.05 us (11%)
  waiting for transfers between devices  4.07 us (5%)
    pallas_call x1, Pallas kernels, score_net(): pl.pallas_call(net_kernel, grid=(slice_count, row_count // rows), in_spec...  16.7 us
    pallas_call x1, Pallas kernels, coil_adjoint(): pl.pallas_call(adjoint_kernel, grid=(coils,), in_specs=[pl.BlockSpec((2,...  13.9 us
    unnamed x18, local copies, waits for them, and re-layouts  12.2 us
    all_to_all x1, starting transfers between devices, on_device(): lax.all_to_all(copies, ('slab', 'coil'), split_axis=2, concat_axis=0, til...  10.9 us
    all_to_all x1, starting transfers between devices, on_device(): lax.all_to_all(by_depth, ('slab', 'coil'), split_axis=0, concat_axis=2, t...  5.7 us
    ppermute x1, starting transfers between devices, with_halo(): before = lax.ppermute(last, axis, up)  4.94 us
    all_to_all x1, waiting for transfers between devices, on_device(): lax.all_to_all(copies, ('slab', 'coil'), split_axis=2, concat_axis=0, til...  4.06 us
    add x1, other arithmetic, on_device(): return image + STEP_SIZE * (score_field - gradient) + noise  2.61 us
  transfers between devices with their start and end apart: 4, of which 1 were waited for; matrix products, arithmetic and copies ran while one was open for 22% of the time, Pallas kernels for 20%

profile of v9, /device:TPU:1, one launch (start us, length us, event | category | flops | bytes accessed | tf_op | source)
XLA Modules:
  0.0 85.1 jit_solution(17239237700203157490)
XLA Ops:
  0.0 1.0 %convert_element_type.55 = bf16[2,2,32,384]{3,2,1,0:T(8,128)(2,1)S(1)} convert(f32[2,2,32,384]{3,2,1,0:T(8,128)} %param.14) | non-fusion elementwise | flops 49152 | bytes 294912 | tf_op jit(solution)/shard_map/convert_element_type | solution.py:212
  1.0 4.9 %collective-permute-start = (bf16[2,2,32,384]{3,2,1,0:T(8,128)(2,1)S(1)}, bf16[2,2,32,384]{3,2,1,0:T(8,128)(2,1)S(1)}, u32[]{:S(2)}, u32[]{:S(2)}) collective-permute-start(bf16[2,2,32,384]{3,2,1,0:T(8,128)(2,1)S(1)} %convert_element_type.55), channel_id=1, source_target_pairs={{0,1},{1,2},{2,3},{3,4},{4,5},{5,6},{6,7},{7,8},{8,9},{9,10},{10,1... | collective-permute-start | bytes 294920 | tf_op jit(solution)/shard_map/ppermute | solution.py:20
  6.0 1.9 %collective-permute-start.1 = (bf16[2,2,32,384]{3,2,1,0:T(8,128)(2,1)S(1)}, bf16[2,2,32,384]{3,2,1,0:T(8,128)(2,1)S(1)}, u32[]{:S(2)}, u32[]{:S(2)}) collective-permute-start(bf16[2,2,32,384]{3,2,1,0:T(8,128)(2,1)S(1)} %convert_element_type.55), channel_id=1, source_target_pairs={{1,0},{2,1},{3,2},{4,3},{5,4},{6,5},{7,6},{8,7},{9,8},{10,9},{11,1... | collective-permute-start | bytes 294920 | tf_op jit(solution)/shard_map/ppermute | solution.py:21
  7.9 1.1 %copy.46 = f32[2,2,32,384]{3,1,0,2:T(2,128)S(1)} copy(f32[2,2,32,384]{3,2,1,0:T(8,128)} %param.14) | data formatting | bytes 393216 | tf_op args[0]
  9.0 1.1 %broadcast_in_dim.2 = f32[2,2,32,4,384]{4,1,0,3,2:T(2,128)} broadcast(f32[2,2,32,384]{3,1,0,2:T(2,128)S(1)} %copy.46), dimensions={0,1,2,4} | broadcast | bytes 983040 | tf_op jit(solution)/shard_map/broadcast_in_dim | solution.py:216
  10.1 10.9 %all-to-all-start = ((f32[2,2,128,384]{3,1,0,2:T(2,128)}), f32[2,2,128,384]{3,1,0,2:T(2,128)S(1)}, u32[]{:S(2)}, u32[]{:S(2)}) async-start(f32[2,2,128,384]{3,1,0,2:T(2,128)} %bitcast.6), calls=%async_computation | async-start | bytes 1572864 | tf_op jit(solution)/shard_map/all_to_all | solution.py:218
  21.0 0.9 %copy.43 = bf16[128,128]{0,1:T(8,128)(2,1)S(1)} copy(bf16[128,128]{1,0:T(8,128)(2,1)} %param.21) | data formatting | bytes 65536 | tf_op args[7]
  21.9 0.9 %copy.44 = bf16[128,128]{0,1:T(8,128)(2,1)S(1)} copy(bf16[128,128]{1,0:T(8,128)(2,1)} %param.23) | data formatting | bytes 65536 | tf_op args[9]
  22.8 0.8 copy.41
  23.7 0.7 pad_maximum_fusion.2
  24.5 0.7 convert_element_type.61
  25.2 0.7 fusion.8.p_ref
  26.1 1.1 %fusion = bf16[2,90,32,384]{3,2,1,0:T(8,128)(2,1)} fusion(bf16[2,10,32,384]{3,2,1,0:T(8,128)(2,1)S(1)} %constant_dynamic-update-slice_fusion), kind=kLoop, calls=%fused_computation.16 | loop fusion | bytes 983040
  27.2 0.9 %fusion.1 = bf16[2,90,32,384]{3,2,1,0:T(8,128)(2,1)} fusion(bf16[2,90,32,384]{3,2,1,0:T(8,128)(2,1)} %fusion, bf16[2,10,32,384]{3,2,1,0:T(8,128)(2,1)S(1)} %constant_dynamic-update-slice_fusion), kind=kLoop, calls=%fused_computation.17 | loop fusion | bytes 983040
  28.1 1.2 %fusion.2 = bf16[2,90,32,384]{3,2,1,0:T(8,128)(2,1)} fusion(bf16[2,90,32,384]{3,2,1,0:T(8,128)(2,1)} %fusion.1, bf16[2,10,32,384]{3,2,1,0:T(8,128)(2,1)S(1)} %constant_dynamic-update-slice_fusion), kind=kLoop, calls=%fused_computation.18 | loop fusion | bytes 983040
  29.3 1.1 %fusion.3 = bf16[2,90,32,384]{3,2,1,0:T(8,128)(2,1)} fusion(bf16[2,90,32,384]{3,2,1,0:T(8,128)(2,1)} %fusion.2, bf16[2,10,32,384]{3,2,1,0:T(8,128)(2,1)S(1)} %constant_dynamic-update-slice_fusion), kind=kLoop, calls=%fused_computation.19 | loop fusion | bytes 983040
  31.0 0.7 constant_dynamic-update-slice_fusion.8
  31.6 0.6 constant_dynamic-update-slice_fusion.7
  32.3 0.7 constant_dynamic-update-slice_fusion.6
  33.0 0.6 constant_dynamic-update-slice_fusion.5
  33.6 4.1 %all-to-all-done = f32[2,2,128,384]{3,1,0,2:T(2,128)S(1)} async-done(((f32[2,2,128,384]{3,1,0,2:T(2,128)}), f32[2,2,128,384]{3,1,0,2:T(2,128)S(1)}, u32[]{:S(2)}, u32[]{:S(2)}) %all-to-all-start) | async-done | bytes 786464 | tf_op jit(solution)/shard_map/all_to_all | solution.py:218
  37.7 1.2 %copy.47 = f32[256,2,1,384]{0,3,2,1:T(8,128)} copy(f32[256,2,1,384]{3,1,0,2:T(2,128)S(1)} %bitcast.22) | data formatting | bytes 1572864 | tf_op jit(solution)/shard_map/all_to_all | solution.py:218
  38.9 13.9 %shard_map.137 = f32[2,1,384,256]{3,2,1,0:T(8,128)} custom-call(f32[2,1,384,256]{3,2,1,0:T(8,128)} %bitcast.24, bf16[4,2,1,384,256]{4,3,2,1,0:T(8,128)(2,1)} %sens_ref.1, bf16[4,2,1,384,256]{4,3,2,1,0:T(8,128)(2,1)} %meas_ref.1, s32[384,256]{1,0:T(8,128)} %mask_ref.1, bf16[768,384]{1,0:T(8,128)(2,1)} %constant.13.clone.ty_ref, ...), custom_call_target="tpu_custom_call" | custom-call | tf_op jit(solution)/shard_map/pallas_call | solution.py:97
  52.8 1.2 %convert_bitcast_fusion = bf16[256,2,1,384]{0,3,2,1:T(8,128)(2,1)S(1)} fusion(f32[2,1,384,256]{3,2,1,0:T(8,128)} %shard_map.137), kind=kLoop, calls=%fused_computation.24 | loop fusion | flops 196608 | bytes 1179648 | tf_op jit(solution)/shard_map/convert_element_type | solution.py:221
  53.9 1.1 %copy.48 = bf16[256,2,1,384]{3,1,2,0:T(2,128)(2,1)} copy(bf16[256,2,1,384]{0,3,2,1:T(8,128)(2,1)S(1)} %convert_bitcast_fusion) | data formatting | bytes 786432 | tf_op jit(solution)/shard_map/convert_element_type | solution.py:221
  55.0 5.7 %all-to-all-start.1 = ((bf16[256,2,1,384]{3,1,2,0:T(2,128)(2,1)}), bf16[256,2,1,384]{3,1,2,0:T(2,128)(2,1)S(1)}, u32[]{:S(2)}, u32[]{:S(2)}) async-start(bf16[256,2,1,384]{3,1,2,0:T(2,128)(2,1)} %copy.48), calls=%async_computation.1 | async-start | bytes 786432 | tf_op jit(solution)/shard_map/all_to_all | solution.py:222
  60.8 1.0 %fusion.4 = bf16[2,90,32,384]{3,2,1,0:T(8,128)(2,1)} fusion(bf16[2,90,32,384]{3,2,1,0:T(8,128)(2,1)} %constant_dynamic-update-slice_fusion.5, bf16[2,10,32,384]{3,2,1,0:T(8,128)(2,1)S(1)} %constant_dynamic-update-slice_fusion), kind=kLoop, calls=%fused_computation.20 | loop fusion | bytes 983040
  61.8 1.1 %fusion.5 = bf16[2,90,32,384]{3,2,1,0:T(8,128)(2,1)} fusion(bf16[2,90,32,384]{3,2,1,0:T(8,128)(2,1)} %fusion.4, bf16[2,10,32,384]{3,2,1,0:T(8,128)(2,1)S(1)} %constant_dynamic-update-slice_fusion), kind=kLoop, calls=%fused_computation.21 | loop fusion | bytes 983040
  62.9 0.9 %fusion.6 = bf16[2,90,32,384]{3,2,1,0:T(8,128)(2,1)} fusion(bf16[2,90,32,384]{3,2,1,0:T(8,128)(2,1)} %fusion.5, bf16[2,10,32,384]{3,2,1,0:T(8,128)(2,1)S(1)} %constant_dynamic-update-slice_fusion), kind=kLoop, calls=%fused_computation.22 | loop fusion | bytes 983040
  63.9 1.1 %fusion.7.x_ref = bf16[2,90,32,384]{3,2,1,0:T(8,128)(2,1)} fusion(bf16[2,90,32,384]{3,2,1,0:T(8,128)(2,1)} %fusion.6, bf16[2,10,32,384]{3,2,1,0:T(8,128)(2,1)S(1)} %constant_dynamic-update-slice_fusion), kind=kLoop, calls=%fused_computation.23 | loop fusion | bytes 983040 | tf_op jit(solution)/shard_map/concatenate | solution.py:147
  65.0 16.7 %shard_map.136 = f32[2,18,32,384]{3,2,1,0:T(8,128)} custom-call(bf16[2,90,32,384]{3,2,1,0:T(8,128)(2,1)} %fusion.7.x_ref, f32[152,512]{1,0:T(8,128)} %fusion.8.p_ref), custom_call_target="tpu_custom_call" | custom-call | tf_op jit(solution)/shard_map/pallas_call | solution.py:173
  82.5 2.6 %add_add_fusion = f32[2,2,32,384]{3,2,1,0:T(8,128)} fusion(f32[2,2,32,384]{3,2,1,0:T(8,128)S(1)} %copy-done.1, f32[2,2,32,384]{3,2,1,0:T(8,128)S(1)} %copy-done, f32[2,2,32,384]{3,1,0,2:T(2,128)S(1)} %reduce_sum.9, f32[2,18,32,384]{3,2,1,0:T(8,128)} %shard_map.136), kind=kLoop, calls=%fused_computation.39 | loop fusion | flops 589824 | bytes 2752512 | tf_op jit(solution)/shard_map/add | solution.py:225
  (21 shorter events, 1.8 us)
Async XLA Ops:
  0.0 26.0 %copy-start = (f32[2,2,32,384]{3,2,1,0:T(8,128)S(1)}, f32[2,2,32,384]{3,2,1,0:T(8,128)}, u32[]{:S(2)}) copy-start(f32[2,2,32,384]{3,2,1,0:T(8,128)} %param.14) | copy-start | bytes 589828
  1.0 25.0 %collective-permute-start = (bf16[2,2,32,384]{3,2,1,0:T(8,128)(2,1)S(1)}, bf16[2,2,32,384]{3,2,1,0:T(8,128)(2,1)S(1)}, u32[]{:S(2)}, u32[]{:S(2)}) collective-permute-start(bf16[2,2,32,384]{3,2,1,0:T(8,128)(2,1)S(1)} %convert_element_type.55), channel_id=1, source_target_pairs={{0,1},{1,2},{2,3},{3,4},{4,5},{5,6},{6,7},{7,8},{8,9},{9,10},{10,1... | collective-permute-start | bytes 294920 | tf_op jit(solution)/shard_map/ppermute | solution.py:20
  6.0 20.1 %collective-permute-start.1 = (bf16[2,2,32,384]{3,2,1,0:T(8,128)(2,1)S(1)}, bf16[2,2,32,384]{3,2,1,0:T(8,128)(2,1)S(1)}, u32[]{:S(2)}, u32[]{:S(2)}) collective-permute-start(bf16[2,2,32,384]{3,2,1,0:T(8,128)(2,1)S(1)} %convert_element_type.55), channel_id=1, source_target_pairs={{1,0},{2,1},{3,2},{4,3},{5,4},{6,5},{7,6},{8,7},{9,8},{10,9},{11,1... | collective-permute-start | bytes 294920 | tf_op jit(solution)/shard_map/ppermute | solution.py:21
  10.1 27.6 %all-to-all-start = ((f32[2,2,128,384]{3,1,0,2:T(2,128)}), f32[2,2,128,384]{3,1,0,2:T(2,128)S(1)}, u32[]{:S(2)}, u32[]{:S(2)}) async-start(f32[2,2,128,384]{3,1,0,2:T(2,128)} %bitcast.6), calls=%async_computation | async-start | bytes 1572864 | tf_op jit(solution)/shard_map/all_to_all | solution.py:218
  55.0 26.7 %all-to-all-start.1 = ((bf16[256,2,1,384]{3,1,2,0:T(2,128)(2,1)}), bf16[256,2,1,384]{3,1,2,0:T(2,128)(2,1)S(1)}, u32[]{:S(2)}, u32[]{:S(2)}) async-start(bf16[256,2,1,384]{3,1,2,0:T(2,128)(2,1)} %copy.48), calls=%async_computation.1 | async-start | bytes 786432 | tf_op jit(solution)/shard_map/all_to_all | solution.py:222
  65.0 17.5 %copy-start.1 = (f32[2,2,32,384]{3,2,1,0:T(8,128)S(1)}, f32[2,2,32,384]{3,2,1,0:T(8,128)}, u32[]{:S(2)}) copy-start(f32[2,2,32,384]{3,2,1,0:T(8,128)} %param.15) | copy-start | bytes 589828

commit v10 on v9

--- a/solution.py
+++ b/solution.py
@@ -135,7 +135,7 @@
         q_ref[0, :, row, :] = q[:, row * cols : (row + 1) * cols]
 
 
-def score_net(window, w_first, b_first, w_second, b_second, w_third, b_third, w_last):
+def score_net(window, w_first, b_first, w_second, b_second, w_third, b_third, w_last, tie):
     slice_count = window.shape[0] - 4
     row_count = window.shape[2]
     col_count = window.shape[3]
@@ -170,16 +170,23 @@
     bottom = jnp.pad(wl.astype(jnp.float32), ((0, -(-outs // 8) * 8 - outs), (0, 3 * width)))
     packed = jnp.concatenate([top, bottom], axis=0)
     rows = 16
-    q = pl.pallas_call(
+    net_call = pl.pallas_call(
         net_kernel,
-        grid=(slice_count, row_count // rows),
+        grid=(1, row_count // rows),
         in_specs=[
-            pl.BlockSpec((1, taps_in, rows, col_count), lambda z, n: (z, 0, n, 0)),
+            pl.BlockSpec((1, taps_in, rows, col_count), lambda z, n: (0, 0, n, 0)),
             pl.BlockSpec(packed.shape, lambda z, n: (0, 0)),
         ],
-        out_specs=pl.BlockSpec((1, outs, rows, col_count), lambda z, n: (z, 0, n, 0)),
-        out_shape=jax.ShapeDtypeStruct((slice_count, outs, row_count, col_count), jnp.float32),
-    )(columns, packed)
+        out_specs=pl.BlockSpec((1, outs, rows, col_count), lambda z, n: (0, 0, n, 0)),
+        out_shape=jax.ShapeDtypeStruct((1, outs, row_count, col_count), jnp.float32),
+    )
+    planes = []
+    for depth in range(slice_count):
+        plane = net_call(columns[depth : depth + 1], packed)
+        if depth == 0:
+            plane, tie = lax.optimization_barrier((plane, tie))
+        planes.append(plane)
+    q = jnp.concatenate(planes, axis=0)
     q = jnp.pad(q, ((0, 0), (0, 0), (1, 1), (1, 1)))
     score_field = jnp.zeros((slice_count, 2, row_count, col_count), jnp.float32)
     for shift_x in range(3):
@@ -188,7 +195,7 @@
             score_field = score_field + q[
                 :, tap : tap + 2, shift_x : shift_x + row_count, shift_y : shift_y + col_count
             ]
-    return score_field
+    return score_field, tie
 
 
 def slab_slices(image):
@@ -210,12 +217,14 @@
     w_last,
 ):
     window = with_halo(image.astype(jnp.bfloat16), ((("slab", "coil"), 0),), 2)
-    score_field = score_net(window, w_first, b_first, w_second, b_second, w_third, b_third, w_last)
     groups = lax.axis_size("coil")
     depth, parts, rows, lines = image.shape
     copies = jnp.broadcast_to(image[:, :, :, None], (depth, parts, rows, groups, lines))
     copies = copies.reshape(depth, parts, rows * groups, lines)
     planes_in = lax.all_to_all(copies, ("slab", "coil"), split_axis=2, concat_axis=0, tiled=True)
+    score_field, planes_in = score_net(
+        window, w_first, b_first, w_second, b_second, w_third, b_third, w_last, planes_in
+    )
     planes = jnp.transpose(planes_in, (1, 2, 3, 0))
     partial_sum = coil_adjoint(planes, sens, measured, mask)
     by_depth = jnp.transpose(partial_sum, (3, 0, 1, 2)).astype(jnp.bfloat16)

time: 85.8 us -> 87.7 us (1.022)
  local copies, waits for them, and re-layouts: 17.8 us -> 12.9 us
  starting transfers between devices: 23.5 us -> 28 us
  other arithmetic: 9.05 us -> 11.8 us
  waiting for transfers between devices: 4.07 us -> 1.71 us
  Pallas kernels: 30.6 us -> 32.5 us
    unnamed x18 -> x20, local copies, waits for them, and re-layouts: 12.2 us -> 5.58 us
    all_to_all x1, starting transfers between devices: 5.7 us -> 10.2 us  [on_device(): lax.all_to_all(by_depth, ('slab', 'coil'), split_axis=0, concat_axis=2, t...]
    all_to_all x1, waiting for transfers between devices: 4.06 us -> 0.01 us  [on_device(): lax.all_to_all(copies, ('slab', 'coil'), split_axis=2, concat_axis=0, til...]
    slice x0 -> x1, local copies, waits for them, and re-layouts: none -> 2.45 us  [score_net(): plane = net_call(columns[depth:depth + 1], packed)]
    pallas_call x1 -> x2, Pallas kernels: 16.7 us -> 18.7 us  [score_net(): plane = net_call(columns[depth:depth + 1], packed)]
    unnamed x6, other arithmetic: 2.02 us -> 0.12 us
    convert_element_type x1, other arithmetic: 0.27 us -> 2.15 us  [on_device(): by_device.astype(jnp.float32).reshape(depth, parts, rows, groups, lines)]
    all_to_all x1, waiting for transfers between devices: 0.01 us -> 1.7 us  [on_device(): lax.all_to_all(by_depth, ('slab', 'coil'), split_axis=0, concat_axis=2, t...]
  transfers between devices with their start and end apart: 4 -> 4, of which waited for: 1 -> 1; matrix products, arithmetic and copies ran while one was open for 22% -> 16% of each run, Pallas kernels for 20% -> 21%
where the time goes in v10:
time: 87.7 us; the launch traced here: 87 us
  Pallas kernels  32.5 us (37%)
  starting transfers between devices  28 us (32%)
  local copies, waits for them, and re-layouts  12.9 us (15%)
  other arithmetic  11.8 us (13%)
  waiting for transfers between devices  1.71 us (2%)
    pallas_call x2, Pallas kernels, score_net(): plane = net_call(columns[depth:depth + 1], packed)  18.7 us
    pallas_call x1, Pallas kernels, coil_adjoint(): pl.pallas_call(adjoint_kernel, grid=(coils,), in_specs=[pl.BlockSpec((2,...  13.8 us
    all_to_all x1, starting transfers between devices, on_device(): lax.all_to_all(copies, ('slab', 'coil'), split_axis=2, concat_axis=0, til...  10.9 us
    all_to_all x1, starting transfers between devices, on_device(): lax.all_to_all(by_depth, ('slab', 'coil'), split_axis=0, concat_axis=2, t...  10.2 us
    unnamed x20, local copies, waits for them, and re-layouts  5.58 us
    ppermute x1, starting transfers between devices, with_halo(): before = lax.ppermute(last, axis, up)  4.94 us
    slice x1, local copies, waits for them, and re-layouts, score_net(): plane = net_call(columns[depth:depth + 1], packed)  2.45 us
    reduce_sum x1, other arithmetic, on_device(): gradient = jnp.sum(by_device, axis=3)  2.19 us
  transfers between devices with their start and end apart: 4, of which 1 were waited for; matrix products, arithmetic and copies ran while one was open for 16% of the time, Pallas kernels for 21%

profile of v10, /device:TPU:1, one launch (start us, length us, event | category | flops | bytes accessed | tf_op | source)
XLA Modules:
  0.0 87.0 jit_solution(15166393809164113745)
XLA Ops:
  0.0 1.0 %convert_element_type.55 = bf16[2,2,32,384]{3,2,1,0:T(8,128)(2,1)S(1)} convert(f32[2,2,32,384]{3,2,1,0:T(8,128)} %param.14) | non-fusion elementwise | flops 49152 | bytes 294912 | tf_op jit(solution)/shard_map/convert_element_type | solution.py:219
  1.0 4.9 %collective-permute-start = (bf16[2,2,32,384]{3,2,1,0:T(8,128)(2,1)S(1)}, bf16[2,2,32,384]{3,2,1,0:T(8,128)(2,1)S(1)}, u32[]{:S(2)}, u32[]{:S(2)}) collective-permute-start(bf16[2,2,32,384]{3,2,1,0:T(8,128)(2,1)S(1)} %convert_element_type.55), channel_id=1, source_target_pairs={{0,1},{1,2},{2,3},{3,4},{4,5},{5,6},{6,7},{7,8},{8,9},{9,10},{10,1... | collective-permute-start | bytes 294920 | tf_op jit(solution)/shard_map/ppermute | solution.py:20
  6.0 1.9 %collective-permute-start.1 = (bf16[2,2,32,384]{3,2,1,0:T(8,128)(2,1)S(1)}, bf16[2,2,32,384]{3,2,1,0:T(8,128)(2,1)S(1)}, u32[]{:S(2)}, u32[]{:S(2)}) collective-permute-start(bf16[2,2,32,384]{3,2,1,0:T(8,128)(2,1)S(1)} %convert_element_type.55), channel_id=1, source_target_pairs={{1,0},{2,1},{3,2},{4,3},{5,4},{6,5},{7,6},{8,7},{9,8},{10,9},{11,1... | collective-permute-start | bytes 294920 | tf_op jit(solution)/shard_map/ppermute | solution.py:21
  7.9 1.1 %copy.46 = f32[2,2,32,384]{3,1,0,2:T(2,128)S(1)} copy(f32[2,2,32,384]{3,2,1,0:T(8,128)} %param.14) | data formatting | bytes 393216 | tf_op args[0]
  9.0 1.1 %broadcast_in_dim.2 = f32[2,2,32,4,384]{4,1,0,3,2:T(2,128)} broadcast(f32[2,2,32,384]{3,1,0,2:T(2,128)S(1)} %copy.46), dimensions={0,1,2,4} | broadcast | bytes 983040 | tf_op jit(solution)/shard_map/broadcast_in_dim | solution.py:222
  10.1 10.9 %all-to-all-start = ((f32[2,2,128,384]{3,1,0,2:T(2,128)}), f32[2,2,128,384]{3,1,0,2:T(2,128)S(1)}, u32[]{:S(2)}, u32[]{:S(2)}) async-start(f32[2,2,128,384]{3,1,0,2:T(2,128)} %bitcast.6), calls=%async_computation | async-start | bytes 1572864 | tf_op jit(solution)/shard_map/all_to_all | solution.py:224
  21.1 0.9 copy.43
  21.9 0.9 %copy.44 = bf16[128,128]{0,1:T(8,128)(2,1)S(1)} copy(bf16[128,128]{1,0:T(8,128)(2,1)} %param.23) | data formatting | bytes 65536 | tf_op args[9]
  22.8 0.8 copy.41
  23.7 0.7 pad_maximum_fusion.3
  24.6 0.7 convert_element_type.61
  25.3 0.8 fusion.8.p_ref
  26.2 0.3 fusion
  26.5 0.2 fusion.1
  26.6 0.4 fusion.2
  27.0 0.3 fusion.3
  27.5 0.3 fusion.4
  27.7 0.4 fusion.5
  28.3 0.4 fusion.7
  28.7 2.5 %fusion.20 = (bf16[1,90,32,384]{3,2,1,0:T(8,128)(2,1)}, bf16[1,90,32,384]{3,2,1,0:T(8,128)(2,1)}) fusion(bf16[2,90,32,384]{3,2,1,0:T(8,128)(2,1)S(1)} %fusion.7), kind=kLoop, calls=%fused_computation.61 | loop fusion | bytes 8847360 | tf_op jit(solution)/shard_map/slice | solution.py:185
  31.1 9.3 %shard_map.136 = f32[1,18,32,384]{3,2,1,0:T(8,128)} custom-call(bf16[1,90,32,384]{3,2,1,0:T(8,128)(2,1)} %get-tuple-element.10.x_ref, f32[152,512]{1,0:T(8,128)} %fusion.8.p_ref), custom_call_target="tpu_custom_call" | custom-call | tf_op jit(solution)/shard_map/pallas_call | solution.py:185
  40.4 1.2 %copy.47 = f32[256,2,1,384]{0,3,2,1:T(8,128)} copy(f32[256,2,1,384]{3,1,0,2:T(2,128)S(1)} %bitcast.22) | data formatting | bytes 1572864 | tf_op jit(solution)/shard_map/optimization_barrier | solution.py:187
  41.7 13.8 %shard_map.138 = f32[2,1,384,256]{3,2,1,0:T(8,128)} custom-call(f32[2,1,384,256]{3,2,1,0:T(8,128)} %bitcast.24, bf16[4,2,1,384,256]{4,3,2,1,0:T(8,128)(2,1)} %sens_ref.1, bf16[4,2,1,384,256]{4,3,2,1,0:T(8,128)(2,1)} %meas_ref.1, s32[384,256]{1,0:T(8,128)} %mask_ref.1, bf16[768,384]{1,0:T(8,128)(2,1)} %constant.13.clone.ty_ref, ...), custom_call_target="tpu_custom_call" | custom-call | tf_op jit(solution)/shard_map/pallas_call | solution.py:97
  55.5 1.3 %convert_bitcast_fusion = bf16[256,2,1,384]{0,3,2,1:T(8,128)(2,1)S(1)} fusion(f32[2,1,384,256]{3,2,1,0:T(8,128)} %shard_map.138), kind=kLoop, calls=%fused_computation.27 | loop fusion | flops 196608 | bytes 1179648 | tf_op jit(solution)/shard_map/convert_element_type | solution.py:230
  56.8 1.1 %copy.48 = bf16[256,2,1,384]{3,1,2,0:T(2,128)(2,1)} copy(bf16[256,2,1,384]{0,3,2,1:T(8,128)(2,1)S(1)} %convert_bitcast_fusion) | data formatting | bytes 786432 | tf_op jit(solution)/shard_map/convert_element_type | solution.py:230
  57.9 10.2 %all-to-all-start.1 = ((bf16[256,2,1,384]{3,1,2,0:T(2,128)(2,1)}), bf16[256,2,1,384]{3,1,2,0:T(2,128)(2,1)}, u32[]{:S(2)}, u32[]{:S(2)}) async-start(bf16[256,2,1,384]{3,1,2,0:T(2,128)(2,1)} %copy.48), calls=%async_computation.1 | async-start | bytes 786432 | tf_op jit(solution)/shard_map/all_to_all | solution.py:231
  68.0 9.3 %shard_map.137 = f32[1,18,32,384]{3,2,1,0:T(8,128)} custom-call(bf16[1,90,32,384]{3,2,1,0:T(8,128)(2,1)} %get-tuple-element.9.x_ref, f32[152,512]{1,0:T(8,128)} %fusion.8.p_ref), custom_call_target="tpu_custom_call" | custom-call | tf_op jit(solution)/shard_map/pallas_call | solution.py:185
  77.4 1.4 %pad_maximum_fusion = f32[2,18,32,384]{3,2,1,0:T(8,128)S(1)} fusion(f32[1,18,32,384]{3,2,1,0:T(8,128)} %shard_map.137, f32[1,18,32,384]{3,2,1,0:T(8,128)S(1)} %copy-done), kind=kLoop, calls=%fused_computation.9 | loop fusion | flops 442368 | bytes 3538944 | tf_op jit(solution)/shard_map/concatenate | solution.py:189
  78.7 1.7 %all-to-all-done.1 = bf16[256,2,1,384]{3,1,2,0:T(2,128)(2,1)} async-done(((bf16[256,2,1,384]{3,1,2,0:T(2,128)(2,1)}), bf16[256,2,1,384]{3,1,2,0:T(2,128)(2,1)}, u32[]{:S(2)}, u32[]{:S(2)}) %all-to-all-start.1) | async-done | bytes 393248 | tf_op jit(solution)/shard_map/all_to_all | solution.py:231
  80.5 2.2 %convert.8 = f32[128,2,2,1,384]{4,2,1,0,3:T(2,128)} convert(bf16[128,2,2,1,384]{4,2,1,0,3:T(2,128)(2,1)} %bitcast.17) | non-fusion elementwise | flops 196608 | bytes 1179648 | tf_op jit(solution)/shard_map/convert_element_type | solution.py:232
  82.6 2.2 %reduce_sum.9 = f32[2,2,32,384]{3,1,0,2:T(2,128)} reduce(f32[2,2,32,4,384]{4,1,0,3,2:T(2,128)} %bitcast.23, f32[]{:T(128)} %constant.11.clone.1), dimensions={3}, to_apply=%region_0.1 | reduce | flops 147456 | bytes 983044 | tf_op jit(solution)/shard_map/reduce_sum | solution.py:233
  84.8 2.2 %add_add_fusion = f32[2,2,32,384]{3,2,1,0:T(8,128)} fusion(f32[2,2,32,384]{3,2,1,0:T(8,128)} %param.15, f32[2,2,32,384]{3,2,1,0:T(8,128)} %param.14, f32[2,2,32,384]{3,1,0,2:T(2,128)} %reduce_sum.9, f32[2,18,32,384]{3,2,1,0:T(8,128)S(1)} %pad_maximum_fusion, f32[1,18,32,384]{3,2,1,0:T(8,128)S(1)} %copy-done.1, f32[1,18,32,384]{3,2,1,0:T(8,128)S(1)} %copy-done), kind=kLoop, calls=%fused_computation.43 | loop fusion | flops 638976 | bytes 4325376 | tf_op jit(solution)/shard_map/add | solution.py:234
  (26 shorter events, 0.7 us)
Async XLA Ops:
  0.0 26.1 %copy-start.2 = (f32[2,2,32,384]{3,2,1,0:T(8,128)S(1)}, f32[2,2,32,384]{3,2,1,0:T(8,128)}, u32[]{:S(2)}) copy-start(f32[2,2,32,384]{3,2,1,0:T(8,128)} %param.14) | copy-start | bytes 589828
  1.0 25.0 %collective-permute-start = (bf16[2,2,32,384]{3,2,1,0:T(8,128)(2,1)S(1)}, bf16[2,2,32,384]{3,2,1,0:T(8,128)(2,1)S(1)}, u32[]{:S(2)}, u32[]{:S(2)}) collective-permute-start(bf16[2,2,32,384]{3,2,1,0:T(8,128)(2,1)S(1)} %convert_element_type.55), channel_id=1, source_target_pairs={{0,1},{1,2},{2,3},{3,4},{4,5},{5,6},{6,7},{7,8},{8,9},{9,10},{10,1... | collective-permute-start | bytes 294920 | tf_op jit(solution)/shard_map/ppermute | solution.py:20
  6.0 20.2 %collective-permute-start.1 = (bf16[2,2,32,384]{3,2,1,0:T(8,128)(2,1)S(1)}, bf16[2,2,32,384]{3,2,1,0:T(8,128)(2,1)S(1)}, u32[]{:S(2)}, u32[]{:S(2)}) collective-permute-start(bf16[2,2,32,384]{3,2,1,0:T(8,128)(2,1)S(1)} %convert_element_type.55), channel_id=1, source_target_pairs={{1,0},{2,1},{3,2},{4,3},{5,4},{6,5},{7,6},{8,7},{9,8},{10,9},{11,1... | collective-permute-start | bytes 294920 | tf_op jit(solution)/shard_map/ppermute | solution.py:21
  10.1 30.3 %all-to-all-start = ((f32[2,2,128,384]{3,1,0,2:T(2,128)}), f32[2,2,128,384]{3,1,0,2:T(2,128)S(1)}, u32[]{:S(2)}, u32[]{:S(2)}) async-start(f32[2,2,128,384]{3,1,0,2:T(2,128)} %bitcast.6), calls=%async_computation | async-start | bytes 1572864 | tf_op jit(solution)/shard_map/all_to_all | solution.py:224
  55.5 21.9 %copy-start = (f32[1,18,32,384]{3,2,1,0:T(8,128)S(1)}, f32[1,18,32,384]{3,2,1,0:T(8,128)}, u32[]{:S(2)}) copy-start(f32[1,18,32,384]{3,2,1,0:T(8,128)} %shard_map.136) | copy-start | bytes 2654212
  57.9 22.6 %all-to-all-start.1 = ((bf16[256,2,1,384]{3,1,2,0:T(2,128)(2,1)}), bf16[256,2,1,384]{3,1,2,0:T(2,128)(2,1)}, u32[]{:S(2)}, u32[]{:S(2)}) async-start(bf16[256,2,1,384]{3,1,2,0:T(2,128)(2,1)} %copy.48), calls=%async_computation.1 | async-start | bytes 786432 | tf_op jit(solution)/shard_map/all_to_all | solution.py:231
  77.4 7.4 %copy-start.1 = (f32[1,18,32,384]{3,2,1,0:T(8,128)S(1)}, f32[1,18,32,384]{3,2,1,0:T(8,128)}, u32[]{:S(2)}) copy-start(f32[1,18,32,384]{3,2,1,0:T(8,128)} %shard_map.137) | copy-start | bytes 2654212

commit v11 on v9

--- a/solution.py
+++ b/solution.py
@@ -209,13 +209,14 @@
     b_third,
     w_last,
 ):
-    window = with_halo(image.astype(jnp.bfloat16), ((("slab", "coil"), 0),), 2)
-    score_field = score_net(window, w_first, b_first, w_second, b_second, w_third, b_third, w_last)
     groups = lax.axis_size("coil")
     depth, parts, rows, lines = image.shape
     copies = jnp.broadcast_to(image[:, :, :, None], (depth, parts, rows, groups, lines))
     copies = copies.reshape(depth, parts, rows * groups, lines)
     planes_in = lax.all_to_all(copies, ("slab", "coil"), split_axis=2, concat_axis=0, tiled=True)
+    planes_in, local = lax.optimization_barrier((planes_in, image))
+    window = with_halo(local.astype(jnp.bfloat16), ((("slab", "coil"), 0),), 2)
+    score_field = score_net(window, w_first, b_first, w_second, b_second, w_third, b_third, w_last)
     planes = jnp.transpose(planes_in, (1, 2, 3, 0))
     partial_sum = coil_adjoint(planes, sens, measured, mask)
     by_depth = jnp.transpose(partial_sum, (3, 0, 1, 2)).astype(jnp.bfloat16)

time: 85.8 us -> 92.3 us (1.076)
  waiting for transfers between devices: 4.07 us -> 11.7 us
  other arithmetic: 9.05 us -> 8.05 us
    all_to_all x1, waiting for transfers between devices: 4.06 us -> 11.7 us  [on_device(): lax.all_to_all(copies, ('slab', 'coil'), split_axis=2, concat_axis=0, til...]
    ppermute x1, starting transfers between devices: 4.94 us -> 2.6 us  [with_halo(): before = lax.ppermute(last, axis, up)]
    all_to_all x1, starting transfers between devices: 5.7 us -> 7.41 us  [on_device(): lax.all_to_all(by_depth, ('slab', 'coil'), split_axis=0, concat_axis=2, t...]
    optimization_barrier x0 -> x1, local copies, waits for them, and re-layouts: none -> 1.23 us  [on_device(): planes_in, local = lax.optimization_barrier((planes_in, image))]
    all_to_all x1 -> x0, local copies, waits for them, and re-layouts: 1.22 us -> none  [on_device(): lax.all_to_all(copies, ('slab', 'coil'), split_axis=2, concat_axis=0, til...]
    convert_element_type x1, other arithmetic: 1.01 us -> 0.01 us  [on_device(): window = with_halo(local.astype(jnp.bfloat16), ((('slab', 'coil'), 0),), 2)]
  transfers between devices with their start and end apart: 4 -> 4, of which waited for: 1 -> 1; matrix products, arithmetic and copies ran while one was open for 22% -> 22% of each run, Pallas kernels for 20% -> 33%
where the time goes in v11:
time: 92.3 us; the launch traced here: 91.7 us
  Pallas kernels  30.6 us (33%)
  starting transfers between devices  23.4 us (25%)
  local copies, waits for them, and re-layouts  17.8 us (19%)
  waiting for transfers between devices  11.7 us (13%)
  other arithmetic  8.05 us (9%)
    pallas_call x1, Pallas kernels, score_net(): pl.pallas_call(net_kernel, grid=(slice_count, row_count // rows), in_spec...  16.7 us
    pallas_call x1, Pallas kernels, coil_adjoint(): pl.pallas_call(adjoint_kernel, grid=(coils,), in_specs=[pl.BlockSpec((2,...  13.9 us
    unnamed x18, local copies, waits for them, and re-layouts  12.3 us
    all_to_all x1, waiting for transfers between devices, on_device(): lax.all_to_all(copies, ('slab', 'coil'), split_axis=2, concat_axis=0, til...  11.7 us
    all_to_all x1, starting transfers between devices, on_device(): lax.all_to_all(copies, ('slab', 'coil'), split_axis=2, concat_axis=0, til...  11.5 us
    all_to_all x1, starting transfers between devices, on_device(): lax.all_to_all(by_depth, ('slab', 'coil'), split_axis=0, concat_axis=2, t...  7.41 us
    add x1, other arithmetic, on_device(): return image + STEP_SIZE * (score_field - gradient) + noise  2.61 us
    ppermute x1, starting transfers between devices, with_halo(): before = lax.ppermute(last, axis, up)  2.6 us
  transfers between devices with their start and end apart: 4, of which 1 were waited for; matrix products, arithmetic and copies ran while one was open for 22% of the time, Pallas kernels for 33%

profile of v11, /device:TPU:1, one launch (start us, length us, event | category | flops | bytes accessed | tf_op | source)
XLA Modules:
  0.0 91.7 jit_solution(13528454425350542605)
XLA Ops:
  0.0 1.2 %copy.41 = f32[2,2,32,384]{3,1,0,2:T(2,128)S(1)} copy(f32[2,2,32,384]{3,2,1,0:T(8,128)} %param.14) | data formatting | bytes 393216 | tf_op args[0]
  1.2 1.1 %broadcast_in_dim.2 = f32[2,2,32,4,384]{4,1,0,3,2:T(2,128)} broadcast(f32[2,2,32,384]{3,1,0,2:T(2,128)S(1)} %copy.41), dimensions={0,1,2,4} | broadcast | bytes 983040 | tf_op jit(solution)/shard_map/broadcast_in_dim | solution.py:214
  2.3 11.5 %all-to-all-start = ((f32[2,2,128,384]{3,1,0,2:T(2,128)}), f32[2,2,128,384]{3,1,0,2:T(2,128)S(1)}, u32[]{:S(2)}, u32[]{:S(2)}) async-start(f32[2,2,128,384]{3,1,0,2:T(2,128)} %bitcast), calls=%async_computation | async-start | bytes 1572864 | tf_op jit(solution)/shard_map/all_to_all | solution.py:216
  13.8 0.7 pad_maximum_fusion.2
  14.6 0.7 convert_element_type.61
  15.3 0.9 copy.45
  16.1 0.9 copy.44
  17.0 0.8 copy.42
  18.0 0.7 fusion.8.p_ref
  18.7 11.7 %all-to-all-done = f32[2,2,128,384]{3,1,0,2:T(2,128)S(1)} async-done(((f32[2,2,128,384]{3,1,0,2:T(2,128)}), f32[2,2,128,384]{3,1,0,2:T(2,128)S(1)}, u32[]{:S(2)}, u32[]{:S(2)}) %all-to-all-start) | async-done | bytes 786464 | tf_op jit(solution)/shard_map/all_to_all | solution.py:216
  30.4 2.6 %collective-permute-start = (bf16[2,2,32,384]{3,2,1,0:T(8,128)(2,1)S(1)}, bf16[2,2,32,384]{3,2,1,0:T(8,128)(2,1)S(1)}, u32[]{:S(2)}, u32[]{:S(2)}) collective-permute-start(bf16[2,2,32,384]{3,2,1,0:T(8,128)(2,1)S(1)} %convert_element_type.55), channel_id=1, source_target_pairs={{0,1},{1,2},{2,3},{3,4},{4,5},{5,6},{6,7},{7,8},{8,9},{9,10},{10,1... | collective-permute-start | bytes 294920 | tf_op jit(solution)/shard_map/ppermute | solution.py:20
  33.0 1.9 %collective-permute-start.1 = (bf16[2,2,32,384]{3,2,1,0:T(8,128)(2,1)S(1)}, bf16[2,2,32,384]{3,2,1,0:T(8,128)(2,1)S(1)}, u32[]{:S(2)}, u32[]{:S(2)}) collective-permute-start(bf16[2,2,32,384]{3,2,1,0:T(8,128)(2,1)S(1)} %convert_element_type.55), channel_id=1, source_target_pairs={{1,0},{2,1},{3,2},{4,3},{5,4},{6,5},{7,6},{8,7},{9,8},{10,9},{11,1... | collective-permute-start | bytes 294920 | tf_op jit(solution)/shard_map/ppermute | solution.py:21
  35.0 1.2 %copy.47 = f32[256,2,1,384]{0,3,2,1:T(8,128)} copy(f32[256,2,1,384]{3,1,0,2:T(2,128)S(1)} %bitcast.22) | data formatting | bytes 1572864 | tf_op jit(solution)/shard_map/optimization_barrier | solution.py:217
  36.2 13.9 %shard_map.137 = f32[2,1,384,256]{3,2,1,0:T(8,128)} custom-call(f32[2,1,384,256]{3,2,1,0:T(8,128)} %bitcast.24, bf16[4,2,1,384,256]{4,3,2,1,0:T(8,128)(2,1)} %sens_ref.1, bf16[4,2,1,384,256]{4,3,2,1,0:T(8,128)(2,1)} %meas_ref.1, s32[384,256]{1,0:T(8,128)} %mask_ref.1, bf16[768,384]{1,0:T(8,128)(2,1)} %constant.13.clone.ty_ref, ...), custom_call_target="tpu_custom_call" | custom-call | tf_op jit(solution)/shard_map/pallas_call | solution.py:97
  50.0 1.2 %convert_bitcast_fusion = bf16[256,2,1,384]{0,3,2,1:T(8,128)(2,1)S(1)} fusion(f32[2,1,384,256]{3,2,1,0:T(8,128)} %shard_map.137), kind=kLoop, calls=%fused_computation.24 | loop fusion | flops 196608 | bytes 1179648 | tf_op jit(solution)/shard_map/convert_element_type | solution.py:222
  51.2 1.1 %copy.48 = bf16[256,2,1,384]{3,1,2,0:T(2,128)(2,1)} copy(bf16[256,2,1,384]{0,3,2,1:T(8,128)(2,1)S(1)} %convert_bitcast_fusion) | data formatting | bytes 786432 | tf_op jit(solution)/shard_map/convert_element_type | solution.py:222
  52.3 7.4 %all-to-all-start.1 = ((bf16[256,2,1,384]{3,1,2,0:T(2,128)(2,1)}), bf16[256,2,1,384]{3,1,2,0:T(2,128)(2,1)S(1)}, u32[]{:S(2)}, u32[]{:S(2)}) async-start(bf16[256,2,1,384]{3,1,2,0:T(2,128)(2,1)} %copy.48), calls=%async_computation.1 | async-start | bytes 786432 | tf_op jit(solution)/shard_map/all_to_all | solution.py:223
  59.9 1.1 %fusion = bf16[2,90,32,384]{3,2,1,0:T(8,128)(2,1)} fusion(bf16[2,10,32,384]{3,2,1,0:T(8,128)(2,1)S(1)} %constant_dynamic-update-slice_fusion), kind=kLoop, calls=%fused_computation.16 | loop fusion | bytes 983040
  60.9 0.9 %fusion.1 = bf16[2,90,32,384]{3,2,1,0:T(8,128)(2,1)} fusion(bf16[2,90,32,384]{3,2,1,0:T(8,128)(2,1)} %fusion, bf16[2,10,32,384]{3,2,1,0:T(8,128)(2,1)S(1)} %constant_dynamic-update-slice_fusion), kind=kLoop, calls=%fused_computation.17 | loop fusion | bytes 983040
  61.9 1.2 %fusion.2 = bf16[2,90,32,384]{3,2,1,0:T(8,128)(2,1)} fusion(bf16[2,90,32,384]{3,2,1,0:T(8,128)(2,1)} %fusion.1, bf16[2,10,32,384]{3,2,1,0:T(8,128)(2,1)S(1)} %constant_dynamic-update-slice_fusion), kind=kLoop, calls=%fused_computation.18 | loop fusion | bytes 983040
  63.0 1.1 %fusion.3 = bf16[2,90,32,384]{3,2,1,0:T(8,128)(2,1)} fusion(bf16[2,90,32,384]{3,2,1,0:T(8,128)(2,1)} %fusion.2, bf16[2,10,32,384]{3,2,1,0:T(8,128)(2,1)S(1)} %constant_dynamic-update-slice_fusion), kind=kLoop, calls=%fused_computation.19 | loop fusion | bytes 983040
  64.1 0.6 constant_dynamic-update-slice_fusion.9
  64.7 0.7 constant_dynamic-update-slice_fusion.8
  65.4 0.6 constant_dynamic-update-slice_fusion.7
  66.0 0.7 constant_dynamic-update-slice_fusion.6
  66.7 0.6 constant_dynamic-update-slice_fusion.5
  67.3 1.0 %fusion.4 = bf16[2,90,32,384]{3,2,1,0:T(8,128)(2,1)} fusion(bf16[2,90,32,384]{3,2,1,0:T(8,128)(2,1)} %constant_dynamic-update-slice_fusion.5, bf16[2,10,32,384]{3,2,1,0:T(8,128)(2,1)S(1)} %constant_dynamic-update-slice_fusion), kind=kLoop, calls=%fused_computation.20 | loop fusion | bytes 983040
  68.4 1.1 %fusion.5 = bf16[2,90,32,384]{3,2,1,0:T(8,128)(2,1)} fusion(bf16[2,90,32,384]{3,2,1,0:T(8,128)(2,1)} %fusion.4, bf16[2,10,32,384]{3,2,1,0:T(8,128)(2,1)S(1)} %constant_dynamic-update-slice_fusion), kind=kLoop, calls=%fused_computation.21 | loop fusion | bytes 983040
  69.5 0.9 %fusion.6 = bf16[2,90,32,384]{3,2,1,0:T(8,128)(2,1)} fusion(bf16[2,90,32,384]{3,2,1,0:T(8,128)(2,1)} %fusion.5, bf16[2,10,32,384]{3,2,1,0:T(8,128)(2,1)S(1)} %constant_dynamic-update-slice_fusion), kind=kLoop, calls=%fused_computation.22 | loop fusion | bytes 983040
  70.4 1.1 %fusion.7.x_ref = bf16[2,90,32,384]{3,2,1,0:T(8,128)(2,1)} fusion(bf16[2,90,32,384]{3,2,1,0:T(8,128)(2,1)} %fusion.6, bf16[2,10,32,384]{3,2,1,0:T(8,128)(2,1)S(1)} %constant_dynamic-update-slice_fusion), kind=kLoop, calls=%fused_computation.23 | loop fusion | bytes 983040 | tf_op jit(solution)/shard_map/concatenate | solution.py:147
  71.6 16.7 %shard_map.136 = f32[2,18,32,384]{3,2,1,0:T(8,128)} custom-call(bf16[2,90,32,384]{3,2,1,0:T(8,128)(2,1)} %fusion.7.x_ref, f32[152,512]{1,0:T(8,128)} %fusion.8.p_ref), custom_call_target="tpu_custom_call" | custom-call | tf_op jit(solution)/shard_map/pallas_call | solution.py:173
  89.1 2.6 %add_add_fusion = f32[2,2,32,384]{3,2,1,0:T(8,128)} fusion(f32[2,2,32,384]{3,2,1,0:T(8,128)S(1)} %copy-done.1, f32[2,2,32,384]{3,2,1,0:T(8,128)S(1)} %copy-done, f32[2,2,32,384]{3,1,0,2:T(2,128)S(1)} %reduce_sum.9, f32[2,18,32,384]{3,2,1,0:T(8,128)} %shard_map.136), kind=kLoop, calls=%fused_computation.39 | loop fusion | flops 589824 | bytes 2752512 | tf_op jit(solution)/shard_map/add | solution.py:226
  (21 shorter events, 1.2 us)
Async XLA Ops:
  0.0 30.4 %copy-start = (f32[2,2,32,384]{3,2,1,0:T(8,128)S(1)}, f32[2,2,32,384]{3,2,1,0:T(8,128)}, u32[]{:S(2)}) copy-start(f32[2,2,32,384]{3,2,1,0:T(8,128)} %param.14) | copy-start | bytes 589828
  2.3 28.1 %all-to-all-start = ((f32[2,2,128,384]{3,1,0,2:T(2,128)}), f32[2,2,128,384]{3,1,0,2:T(2,128)S(1)}, u32[]{:S(2)}, u32[]{:S(2)}) async-start(f32[2,2,128,384]{3,1,0,2:T(2,128)} %bitcast), calls=%async_computation | async-start | bytes 1572864 | tf_op jit(solution)/shard_map/all_to_all | solution.py:216
  30.4 29.3 %collective-permute-start = (bf16[2,2,32,384]{3,2,1,0:T(8,128)(2,1)S(1)}, bf16[2,2,32,384]{3,2,1,0:T(8,128)(2,1)S(1)}, u32[]{:S(2)}, u32[]{:S(2)}) collective-permute-start(bf16[2,2,32,384]{3,2,1,0:T(8,128)(2,1)S(1)} %convert_element_type.55), channel_id=1, source_target_pairs={{0,1},{1,2},{2,3},{3,4},{4,5},{5,6},{6,7},{7,8},{8,9},{9,10},{10,1... | collective-permute-start | bytes 294920 | tf_op jit(solution)/shard_map/ppermute | solution.py:20
  33.0 26.8 %collective-permute-start.1 = (bf16[2,2,32,384]{3,2,1,0:T(8,128)(2,1)S(1)}, bf16[2,2,32,384]{3,2,1,0:T(8,128)(2,1)S(1)}, u32[]{:S(2)}, u32[]{:S(2)}) collective-permute-start(bf16[2,2,32,384]{3,2,1,0:T(8,128)(2,1)S(1)} %convert_element_type.55), channel_id=1, source_target_pairs={{1,0},{2,1},{3,2},{4,3},{5,4},{6,5},{7,6},{8,7},{9,8},{10,9},{11,1... | collective-permute-start | bytes 294920 | tf_op jit(solution)/shard_map/ppermute | solution.py:21
  52.3 36.0 %all-to-all-start.1 = ((bf16[256,2,1,384]{3,1,2,0:T(2,128)(2,1)}), bf16[256,2,1,384]{3,1,2,0:T(2,128)(2,1)S(1)}, u32[]{:S(2)}, u32[]{:S(2)}) async-start(bf16[256,2,1,384]{3,1,2,0:T(2,128)(2,1)} %copy.48), calls=%async_computation.1 | async-start | bytes 786432 | tf_op jit(solution)/shard_map/all_to_all | solution.py:223
  71.6 17.5 %copy-start.1 = (f32[2,2,32,384]{3,2,1,0:T(8,128)S(1)}, f32[2,2,32,384]{3,2,1,0:T(8,128)}, u32[]{:S(2)}) copy-start(f32[2,2,32,384]{3,2,1,0:T(8,128)} %param.15) | copy-start | bytes 589828

commit v12 on v9

--- a/solution.py
+++ b/solution.py
@@ -111,28 +111,33 @@
 
 
 def net_kernel(x_ref, p_ref, q_ref):
-    width = p_ref.shape[1] // 4
+    width = p_ref.shape[0] - 24
     taps_in = x_ref.shape[1]
-    rows = x_ref.shape[2]
-    cols = x_ref.shape[3]
+    row_count = q_ref.shape[2]
+    cols = q_ref.shape[3]
     outs = q_ref.shape[1]
-    x = jnp.concatenate([x_ref[0, :, row, :] for row in range(rows)], axis=1)
-    w1 = p_ref[:width, 0:taps_in].astype(jnp.bfloat16)
-    w2 = p_ref[:width, width : 2 * width].astype(jnp.bfloat16)
-    w3 = p_ref[:width, 2 * width : 3 * width].astype(jnp.bfloat16)
+    rows = 16
+    w1 = [p_ref[:width, a * width : a * width + taps_in].astype(jnp.bfloat16) for a in range(3)]
+    w2 = p_ref[:width, 3 * width : 4 * width].astype(jnp.bfloat16)
+    w3 = p_ref[:width, 4 * width : 5 * width].astype(jnp.bfloat16)
     wl = p_ref[width : width + outs, 0:width].astype(jnp.bfloat16)
-    b1 = p_ref[:width, 3 * width : 3 * width + 1]
-    b2 = p_ref[:width, 3 * width + 1 : 3 * width + 2]
-    b3 = p_ref[:width, 3 * width + 2 : 3 * width + 3]
-    h = jnp.dot(w1, x, preferred_element_type=jnp.float32) + b1
-    h = jax.nn.silu(h).astype(jnp.bfloat16)
-    h = jnp.dot(w2, h, preferred_element_type=jnp.float32) + b2
-    h = jax.nn.silu(h).astype(jnp.bfloat16)
-    h = jnp.dot(w3, h, preferred_element_type=jnp.float32) + b3
-    h = jax.nn.silu(h).astype(jnp.bfloat16)
-    q = jnp.dot(wl, h, preferred_element_type=jnp.float32)
-    for row in range(rows):
-        q_ref[0, :, row, :] = q[:, row * cols : (row + 1) * cols]
+    b1 = p_ref[:width, 5 * width : 5 * width + 1]
+    b2 = p_ref[:width, 5 * width + 1 : 5 * width + 2]
+    b3 = p_ref[:width, 5 * width + 2 : 5 * width + 3]
+    for chunk in range(row_count // rows):
+        first = chunk * rows
+        h = b1
+        for a in range(3):
+            x = jnp.concatenate([x_ref[0, :, first + row + a, :] for row in range(rows)], axis=1)
+            h = h + jnp.dot(w1[a], x, preferred_element_type=jnp.float32)
+        h = jax.nn.silu(h).astype(jnp.bfloat16)
+        h = jnp.dot(w2, h, preferred_element_type=jnp.float32) + b2
+        h = jax.nn.silu(h).astype(jnp.bfloat16)
+        h = jnp.dot(w3, h, preferred_element_type=jnp.float32) + b3
+        h = jax.nn.silu(h).astype(jnp.bfloat16)
+        q = jnp.dot(wl, h, preferred_element_type=jnp.float32)
+        for row in range(rows):
+            q_ref[0, :, first + row, :] = q[:, row * cols : (row + 1) * cols]
 
 
 def score_net(window, w_first, b_first, w_second, b_second, w_third, b_third, w_last):
@@ -144,42 +149,34 @@
         [window[offset : offset + slice_count] for offset in range(5)], axis=1
     )
     framed = jnp.pad(stacked, ((0, 0), (0, 0), (1, 1), (1, 1)))
-    columns = jnp.concatenate(
-        [
-            framed[:, :, shift_x : shift_x + row_count, shift_y : shift_y + col_count]
-            for shift_x in range(3)
-            for shift_y in range(3)
+    shifted = jnp.concatenate(
+        [framed[:, :, :, shift_y : shift_y + col_count] for shift_y in range(3)], axis=1
+    )
+    taps_in = shifted.shape[1]
+    wl = w_last.reshape(-1, width)
+    outs = wl.shape[0]
+    pad_to = lambda m: jnp.pad(m.astype(jnp.float32), ((0, 0), (0, width - m.shape[1])))
+    top = jnp.concatenate(
+        [pad_to(w_first[shift_x].reshape(taps_in, width).T) for shift_x in range(3)]
+        + [
+            pad_to(w_second.T),
+            pad_to(w_third.T),
+            pad_to(jnp.stack([b_first, b_second, b_third], axis=1)),
         ],
         axis=1,
     )
-    taps_in = columns.shape[1]
-    wl = w_last.reshape(-1, width)
-    outs = wl.shape[0]
-    top = jnp.concatenate(
-        [
-            jnp.pad(w_first.reshape(taps_in, width).T, ((0, 0), (0, width - taps_in))).astype(jnp.float32),
-            w_second.T.astype(jnp.float32),
-            w_third.T.astype(jnp.float32),
-            jnp.pad(
-                jnp.stack([b_first, b_second, b_third], axis=1),
-                ((0, 0), (0, width - 3)),
-            ),
-        ],
-        axis=1,
-    ).astype(jnp.float32)
-    bottom = jnp.pad(wl.astype(jnp.float32), ((0, -(-outs // 8) * 8 - outs), (0, 3 * width)))
+    bottom = jnp.pad(wl.astype(jnp.float32), ((0, 24 - outs), (0, 5 * width)))
     packed = jnp.concatenate([top, bottom], axis=0)
-    rows = 16
     q = pl.pallas_call(
         net_kernel,
-        grid=(slice_count, row_count // rows),
+        grid=(slice_count,),
         in_specs=[
-            pl.BlockSpec((1, taps_in, rows, col_count), lambda z, n: (z, 0, n, 0)),
-            pl.BlockSpec(packed.shape, lambda z, n: (0, 0)),
+            pl.BlockSpec((1,) + shifted.shape[1:], lambda z: (z, 0, 0, 0)),
+            pl.BlockSpec(packed.shape, lambda z: (0, 0)),
         ],
-        out_specs=pl.BlockSpec((1, outs, rows, col_count), lambda z, n: (z, 0, n, 0)),
+        out_specs=pl.BlockSpec((1, outs, row_count, col_count), lambda z: (z, 0, 0, 0)),
         out_shape=jax.ShapeDtypeStruct((slice_count, outs, row_count, col_count), jnp.float32),
-    )(columns, packed)
+    )(shifted, packed)
     q = jnp.pad(q, ((0, 0), (0, 0), (1, 1), (1, 1)))
     score_field = jnp.zeros((slice_count, 2, row_count, col_count), jnp.float32)
     for shift_x in range(3):

time: 85.8 us -> 80.8 us (0.942)
  local copies, waits for them, and re-layouts: 17.8 us -> 7.15 us
  waiting for transfers between devices: 4.07 us -> 14.7 us
  other arithmetic: 9.05 us -> 6.45 us
  starting transfers between devices: 23.5 us -> 21.5 us
    all_to_all x1, waiting for transfers between devices: 4.06 us -> 14.7 us  [on_device(): lax.all_to_all(copies, ('slab', 'coil'), split_axis=2, concat_axis=0, til...]
    unnamed x18 -> x24, local copies, waits for them, and re-layouts: 12.2 us -> 2.04 us
    all_to_all x1, starting transfers between devices: 5.7 us -> 3.73 us  [on_device(): lax.all_to_all(by_depth, ('slab', 'coil'), split_axis=0, concat_axis=2, t...]
    unnamed x6 -> x8, other arithmetic: 2.02 us -> 0.11 us
    add x1, other arithmetic: 2.61 us -> 1.06 us  [on_device(): return image + STEP_SIZE * (score_field - gradient) + noise]
    concatenate x0 -> x1, other arithmetic: none -> 1.53 us  [score_net(): jnp.concatenate([framed[:, :, :, shift_y:shift_y + col_count] for shift_y...]
    concatenate x1, local copies, waits for them, and re-layouts: 1.15 us -> 0.01 us  [score_net(): jnp.concatenate([pad_to(w_first[shift_x].reshape(taps_in, width).T) for s...]
    slice x0 -> x5, local copies, waits for them, and re-layouts: none -> 1.08 us  [the longest x1 1.05 us: score_net(): framed[:, :, :, shift_y:shift_y + col_count]]
  transfers between devices with their start and end apart: 4 -> 4, of which waited for: 1 -> 1; matrix products, arithmetic and copies ran while one was open for 22% -> 8% of each run, Pallas kernels for 20% -> 20%
where the time goes in v12:
time: 80.8 us; the launch traced here: 80.4 us
  Pallas kernels  30.3 us (38%)
  starting transfers between devices  21.5 us (27%)
  waiting for transfers between devices  14.7 us (18%)
  local copies, waits for them, and re-layouts  7.15 us (9%)
  other arithmetic  6.45 us (8%)
    pallas_call x1, Pallas kernels, score_net(): pl.pallas_call(net_kernel, grid=(slice_count,), in_specs=[pl.BlockSpec((1...  16.5 us
    all_to_all x1, waiting for transfers between devices, on_device(): lax.all_to_all(copies, ('slab', 'coil'), split_axis=2, concat_axis=0, til...  14.7 us
    pallas_call x1, Pallas kernels, coil_adjoint(): pl.pallas_call(adjoint_kernel, grid=(coils,), in_specs=[pl.BlockSpec((2,...  13.8 us
    all_to_all x1, starting transfers between devices, on_device(): lax.all_to_all(copies, ('slab', 'coil'), split_axis=2, concat_axis=0, til...  10.9 us
    ppermute x1, starting transfers between devices, with_halo(): before = lax.ppermute(last, axis, up)  4.94 us
    all_to_all x1, starting transfers between devices, on_device(): lax.all_to_all(by_depth, ('slab', 'coil'), split_axis=0, concat_axis=2, t...  3.73 us
    unnamed x24, local copies, waits for them, and re-layouts  2.04 us
    ppermute x1, starting transfers between devices, with_halo(): after = lax.ppermute(first, axis, down)  1.92 us
  transfers between devices with their start and end apart: 4, of which 1 were waited for; matrix products, arithmetic and copies ran while one was open for 8% of the time, Pallas kernels for 20%

profile of v12, /device:TPU:1, one launch (start us, length us, event | category | flops | bytes accessed | tf_op | source)
XLA Modules:
  0.0 80.4 jit_solution(10540669446521336388)
XLA Ops:
  0.0 0.0 copy-start.9
  0.0 0.0 copy-start.8
  0.0 1.0 %convert_element_type.75 = bf16[2,2,32,384]{3,2,1,0:T(8,128)(2,1)S(1)} convert(f32[2,2,32,384]{3,2,1,0:T(8,128)} %param.14) | non-fusion elementwise | flops 49152 | bytes 294912 | tf_op jit(solution)/shard_map/convert_element_type | solution.py:209
  1.0 0.0 copy-start.6
  1.0 4.9 %collective-permute-start = (bf16[2,2,32,384]{3,2,1,0:T(8,128)(2,1)S(1)}, bf16[2,2,32,384]{3,2,1,0:T(8,128)(2,1)S(1)}, u32[]{:S(2)}, u32[]{:S(2)}) collective-permute-start(bf16[2,2,32,384]{3,2,1,0:T(8,128)(2,1)S(1)} %convert_element_type.75), channel_id=1, source_target_pairs={{0,1},{1,2},{2,3},{3,4},{4,5},{5,6},{6,7},{7,8},{8,9},{9,10},{10,1... | collective-permute-start | bytes 294920 | tf_op jit(solution)/shard_map/ppermute | solution.py:20
  6.0 1.9 %collective-permute-start.1 = (bf16[2,2,32,384]{3,2,1,0:T(8,128)(2,1)S(1)}, bf16[2,2,32,384]{3,2,1,0:T(8,128)(2,1)S(1)}, u32[]{:S(2)}, u32[]{:S(2)}) collective-permute-start(bf16[2,2,32,384]{3,2,1,0:T(8,128)(2,1)S(1)} %convert_element_type.75), channel_id=1, source_target_pairs={{1,0},{2,1},{3,2},{4,3},{5,4},{6,5},{7,6},{8,7},{9,8},{10,9},{11,1... | collective-permute-start | bytes 294920 | tf_op jit(solution)/shard_map/ppermute | solution.py:21
  7.9 1.1 %copy.60 = f32[2,2,32,384]{3,1,0,2:T(2,128)S(1)} copy(f32[2,2,32,384]{3,2,1,0:T(8,128)} %param.14) | data formatting | bytes 393216 | tf_op args[0]
  9.0 1.1 %broadcast_in_dim.2 = f32[2,2,32,4,384]{4,1,0,3,2:T(2,128)} broadcast(f32[2,2,32,384]{3,1,0,2:T(2,128)S(1)} %copy.60), dimensions={0,1,2,4} | broadcast | bytes 983040 | tf_op jit(solution)/shard_map/broadcast_in_dim | solution.py:213
  10.1 10.9 %all-to-all-start = ((f32[2,2,128,384]{3,1,0,2:T(2,128)}), f32[2,2,128,384]{3,1,0,2:T(2,128)S(1)}, u32[]{:S(2)}, u32[]{:S(2)}) async-start(f32[2,2,128,384]{3,1,0,2:T(2,128)} %bitcast.8), calls=%async_computation | async-start | bytes 1572864 | tf_op jit(solution)/shard_map/all_to_all | solution.py:215
  21.1 0.1 copy.52
  21.3 0.1 copy.54
  21.4 0.1 copy.56
  21.6 0.1 copy.57
  21.7 0.1 copy.58
  21.9 0.1 copy.59
  22.1 0.8 pad_maximum_fusion.1.p_ref
  22.9 0.0 collective-permute-done
  23.0 0.0 collective-permute-done.1
  23.0 14.7 %all-to-all-done = f32[2,2,128,384]{3,1,0,2:T(2,128)S(1)} async-done(((f32[2,2,128,384]{3,1,0,2:T(2,128)}), f32[2,2,128,384]{3,1,0,2:T(2,128)S(1)}, u32[]{:S(2)}, u32[]{:S(2)}) %all-to-all-start) | async-done | bytes 786464 | tf_op jit(solution)/shard_map/all_to_all | solution.py:215
  37.7 1.2 %copy.61 = f32[256,2,1,384]{0,3,2,1:T(8,128)} copy(f32[256,2,1,384]{3,1,0,2:T(2,128)S(1)} %bitcast.24) | data formatting | bytes 1572864 | tf_op jit(solution)/shard_map/all_to_all | solution.py:215
  38.9 13.8 %shard_map.137 = f32[2,1,384,256]{3,2,1,0:T(8,128)} custom-call(f32[2,1,384,256]{3,2,1,0:T(8,128)} %bitcast.26, bf16[4,2,1,384,256]{4,3,2,1,0:T(8,128)(2,1)} %sens_ref.1, bf16[4,2,1,384,256]{4,3,2,1,0:T(8,128)(2,1)} %meas_ref.1, s32[384,256]{1,0:T(8,128)} %mask_ref.1, bf16[768,384]{1,0:T(8,128)(2,1)} %constant.13.clone.ty_ref, ...), custom_call_target="tpu_custom_call" | custom-call | tf_op jit(solution)/shard_map/pallas_call | solution.py:97
  52.8 1.2 %convert_bitcast_fusion = bf16[256,2,1,384]{0,3,2,1:T(8,128)(2,1)S(1)} fusion(f32[2,1,384,256]{3,2,1,0:T(8,128)} %shard_map.137), kind=kLoop, calls=%fused_computation.13 | loop fusion | flops 196608 | bytes 1179648 | tf_op jit(solution)/shard_map/convert_element_type | solution.py:218
  54.0 1.1 %copy.62 = bf16[256,2,1,384]{3,1,2,0:T(2,128)(2,1)} copy(bf16[256,2,1,384]{0,3,2,1:T(8,128)(2,1)S(1)} %convert_bitcast_fusion) | data formatting | bytes 786432 | tf_op jit(solution)/shard_map/convert_element_type | solution.py:218
  55.1 3.7 %all-to-all-start.1 = ((bf16[256,2,1,384]{3,1,2,0:T(2,128)(2,1)}), bf16[256,2,1,384]{3,1,2,0:T(2,128)(2,1)S(1)}, u32[]{:S(2)}, u32[]{:S(2)}) async-start(bf16[256,2,1,384]{3,1,2,0:T(2,128)(2,1)} %copy.62), calls=%async_computation.1 | async-start | bytes 786432 | tf_op jit(solution)/shard_map/all_to_all | solution.py:219
  58.8 1.1 %pad_slice_fusion.10 = (bf16[2,10,34,384]{3,2,1,0:T(8,128)(2,1)S(1)}, bf16[2,10,34,384]{3,2,1,0:T(8,128)(2,1)S(1)}, bf16[2,10,34,384]{3,2,1,0:T(8,128)(2,1)S(1)}) fusion(bf16[2,10,32,384]{3,2,1,0:T(8,128)(2,1)S(1)} %constant_dynamic-update-slice_fusion), kind=kLoop, calls=%fused_computation.11 | loop fusion | bytes 2058240 | tf_op jit(solution)/shard_map/slice | solution.py:153
  59.9 1.5 %pad_maximum_fusion.x_ref = bf16[2,30,34,384]{3,2,1,0:T(8,128)(2,1)} fusion(bf16[2,10,34,384]{3,2,1,0:T(8,128)(2,1)S(1)} %get-tuple-element.7, bf16[2,10,34,384]{3,2,1,0:T(8,128)(2,1)S(1)} %get-tuple-element.6, bf16[2,10,34,384]{3,2,1,0:T(8,128)(2,1)S(1)} %get-tuple-element.5), kind=kLoop, calls=%fused_computation.8 | loop fusion | flops 1566720 | bytes 3133440 | tf_op jit(solution)/shard_map/concatenate | solution.py:152
  61.4 16.5 %shard_map.136 = f32[2,18,32,384]{3,2,1,0:T(8,128)} custom-call(bf16[2,30,34,384]{3,2,1,0:T(8,128)(2,1)} %pad_maximum_fusion.x_ref, f32[152,768]{1,0:T(8,128)} %pad_maximum_fusion.1.p_ref), custom_call_target="tpu_custom_call" | custom-call | tf_op jit(solution)/shard_map/pallas_call | solution.py:170
  77.9 0.0 all-to-all-done.1
  77.9 0.3 convert.20
  78.2 0.5 reduce_sum.9
  78.7 0.7 copy-done
  79.4 1.1 %add_add_fusion = f32[2,2,32,384]{3,2,1,0:T(8,128)} fusion(f32[2,2,32,384]{3,2,1,0:T(8,128)S(1)} %copy-done.2, f32[2,2,32,384]{3,2,1,0:T(8,128)S(1)} %copy-done.1, f32[2,2,32,384]{3,1,0,2:T(2,128)S(1)} %reduce_sum.9, f32[2,18,32,384]{3,2,1,0:T(8,128)S(1)} %copy-done), kind=kLoop, calls=%fused_computation.23 | loop fusion | flops 589824 | bytes 2752512 | tf_op jit(solution)/shard_map/add | solution.py:222
  (37 shorter events, 0.3 us)
Async XLA Ops:
  0.0 21.1 %copy-start.5 = (bf16[3,3,10,128]{3,1,2,0:T(4,128)(2,1)S(1)}, bf16[3,3,10,128]{3,1,2,0:T(4,128)(2,1)}, u32[]{:S(2)}) copy-start(bf16[3,3,10,128]{3,1,2,0:T(4,128)(2,1)} %param.19) | copy-start | bytes 69124
  0.0 21.6 %copy-start.3 = (bf16[128,128]{1,0:T(8,128)(2,1)S(1)}, bf16[128,128]{1,0:T(8,128)(2,1)}, u32[]{:S(2)}) copy-start(bf16[128,128]{1,0:T(8,128)(2,1)} %param.21) | copy-start | bytes 98308
  0.0 21.7 %copy-start.4 = (bf16[128,128]{1,0:T(8,128)(2,1)S(1)}, bf16[128,128]{1,0:T(8,128)(2,1)}, u32[]{:S(2)}) copy-start(bf16[128,128]{1,0:T(8,128)(2,1)} %param.23) | copy-start | bytes 98308
  0.0 21.8 %copy-start.9 = (f32[128]{0:T(128)S(1)}, f32[128]{0:T(128)}, u32[]{:S(2)}) copy-start(f32[128]{0:T(128)} %param.20) | copy-start | bytes 1540
  0.0 21.8 %copy-start.8 = (f32[128]{0:T(128)S(1)}, f32[128]{0:T(128)}, u32[]{:S(2)}) copy-start(f32[128]{0:T(128)} %param.22) | copy-start | bytes 1540
  0.0 21.8 %copy-start.7 = (f32[128]{0:T(128)S(1)}, f32[128]{0:T(128)}, u32[]{:S(2)}) copy-start(f32[128]{0:T(128)} %param.24) | copy-start | bytes 1540
  1.0 21.0 %copy-start.6 = (bf16[3,3,2,128]{3,2,1,0:T(2,128)(2,1)S(1)}, bf16[3,3,2,128]{3,2,1,0:T(2,128)(2,1)}, u32[]{:S(2)}) copy-start(bf16[3,3,2,128]{3,2,1,0:T(2,128)(2,1)} %param.25) | copy-start | bytes 13828
  1.0 21.9 %collective-permute-start = (bf16[2,2,32,384]{3,2,1,0:T(8,128)(2,1)S(1)}, bf16[2,2,32,384]{3,2,1,0:T(8,128)(2,1)S(1)}, u32[]{:S(2)}, u32[]{:S(2)}) collective-permute-start(bf16[2,2,32,384]{3,2,1,0:T(8,128)(2,1)S(1)} %convert_element_type.75), channel_id=1, source_target_pairs={{0,1},{1,2},{2,3},{3,4},{4,5},{5,6},{6,7},{7,8},{8,9},{9,10},{10,1... | collective-permute-start | bytes 294920 | tf_op jit(solution)/shard_map/ppermute | solution.py:20
  6.0 17.0 %collective-permute-start.1 = (bf16[2,2,32,384]{3,2,1,0:T(8,128)(2,1)S(1)}, bf16[2,2,32,384]{3,2,1,0:T(8,128)(2,1)S(1)}, u32[]{:S(2)}, u32[]{:S(2)}) collective-permute-start(bf16[2,2,32,384]{3,2,1,0:T(8,128)(2,1)S(1)} %convert_element_type.75), channel_id=1, source_target_pairs={{1,0},{2,1},{3,2},{4,3},{5,4},{6,5},{7,6},{8,7},{9,8},{10,9},{11,1... | collective-permute-start | bytes 294920 | tf_op jit(solution)/shard_map/ppermute | solution.py:21
  10.1 12.8 %copy-start.1 = (f32[2,2,32,384]{3,2,1,0:T(8,128)S(1)}, f32[2,2,32,384]{3,2,1,0:T(8,128)}, u32[]{:S(2)}) copy-start(f32[2,2,32,384]{3,2,1,0:T(8,128)} %param.14) | copy-start | bytes 589828
  10.1 27.6 %all-to-all-start = ((f32[2,2,128,384]{3,1,0,2:T(2,128)}), f32[2,2,128,384]{3,1,0,2:T(2,128)S(1)}, u32[]{:S(2)}, u32[]{:S(2)}) async-start(f32[2,2,128,384]{3,1,0,2:T(2,128)} %bitcast.8), calls=%async_computation | async-start | bytes 1572864 | tf_op jit(solution)/shard_map/all_to_all | solution.py:215
  55.1 22.8 %all-to-all-start.1 = ((bf16[256,2,1,384]{3,1,2,0:T(2,128)(2,1)}), bf16[256,2,1,384]{3,1,2,0:T(2,128)(2,1)S(1)}, u32[]{:S(2)}, u32[]{:S(2)}) async-start(bf16[256,2,1,384]{3,1,2,0:T(2,128)(2,1)} %copy.62), calls=%async_computation.1 | async-start | bytes 786432 | tf_op jit(solution)/shard_map/all_to_all | solution.py:219
  77.9 1.5 %copy-start = (f32[2,18,32,384]{3,2,1,0:T(8,128)S(1)}, f32[2,18,32,384]{3,2,1,0:T(8,128)}, u32[]{:S(2)}) copy-start(f32[2,18,32,384]{3,2,1,0:T(8,128)} %shard_map.136) | copy-start | bytes 5308420
  77.9 1.5 %copy-start.2 = (f32[2,2,32,384]{3,2,1,0:T(8,128)S(1)}, f32[2,2,32,384]{3,2,1,0:T(8,128)}, u32[]{:S(2)}) copy-start(f32[2,2,32,384]{3,2,1,0:T(8,128)} %param.15) | copy-start | bytes 589828

commit v13 on v12

--- a/solution.py
+++ b/solution.py
@@ -213,6 +213,7 @@
     copies = jnp.broadcast_to(image[:, :, :, None], (depth, parts, rows, groups, lines))
     copies = copies.reshape(depth, parts, rows * groups, lines)
     planes_in = lax.all_to_all(copies, ("slab", "coil"), split_axis=2, concat_axis=0, tiled=True)
+    score_field, planes_in = lax.optimization_barrier((score_field, planes_in))
     planes = jnp.transpose(planes_in, (1, 2, 3, 0))
     partial_sum = coil_adjoint(planes, sens, measured, mask)
     by_depth = jnp.transpose(partial_sum, (3, 0, 1, 2)).astype(jnp.bfloat16)

time: 80.8 us -> 85 us (1.052)
  blocking collectives: 0 us -> 22.3 us
  waiting for transfers between devices: 14.7 us -> 0.01 us
  starting transfers between devices: 21.5 us -> 17.8 us
  other arithmetic: 6.45 us -> 8.06 us
  local copies, waits for them, and re-layouts: 7.15 us -> 5.83 us
    all_to_all x0 -> x1, blocking collectives: none -> 22.3 us  [on_device(): lax.all_to_all(by_depth, ('slab', 'coil'), split_axis=0, concat_axis=2, t...]
    all_to_all x1, waiting for transfers between devices: 14.7 us -> 0.01 us  [on_device(): lax.all_to_all(copies, ('slab', 'coil'), split_axis=2, concat_axis=0, til...]
    all_to_all x1 -> x0, starting transfers between devices: 3.73 us -> none  [on_device(): lax.all_to_all(by_depth, ('slab', 'coil'), split_axis=0, concat_axis=2, t...]
    add x0 -> x1, other arithmetic: none -> 1.91 us  [score_net(): score_field + q[:, tap:tap + 2, shift_x:shift_x + row_count, shift_y:shif...]
    optimization_barrier x0 -> x1, local copies, waits for them, and re-layouts: none -> 1.23 us  [on_device(): score_field, planes_in = lax.optimization_barrier((score_field, planes_in))]
    all_to_all x1 -> x0, local copies, waits for them, and re-layouts: 1.23 us -> none  [on_device(): lax.all_to_all(copies, ('slab', 'coil'), split_axis=2, concat_axis=0, til...]
    unnamed x24 -> x22, local copies, waits for them, and re-layouts: 2.04 us -> 1.36 us
  transfers between devices with their start and end apart: 4 -> 3, of which waited for: 1 -> 0; matrix products, arithmetic and copies ran while one was open for 8% -> 10% of each run, Pallas kernels for 20% -> 19%
where the time goes in v13:
time: 85 us; the launch traced here: 84.6 us
  Pallas kernels  30.3 us (36%)
  blocking collectives  22.3 us (26%)
  starting transfers between devices  17.8 us (21%)
  other arithmetic  8.06 us (9%)
  local copies, waits for them, and re-layouts  5.83 us (7%)
    all_to_all x1, blocking collectives, on_device(): lax.all_to_all(by_depth, ('slab', 'coil'), split_axis=0, concat_axis=2, t...  22.3 us
    pallas_call x1, Pallas kernels, score_net(): pl.pallas_call(net_kernel, grid=(slice_count,), in_specs=[pl.BlockSpec((1...  16.4 us
    pallas_call x1, Pallas kernels, coil_adjoint(): pl.pallas_call(adjoint_kernel, grid=(coils,), in_specs=[pl.BlockSpec((2,...  13.9 us
    all_to_all x1, starting transfers between devices, on_device(): lax.all_to_all(copies, ('slab', 'coil'), split_axis=2, concat_axis=0, til...  10.9 us
    ppermute x1, starting transfers between devices, with_halo(): before = lax.ppermute(last, axis, up)  4.94 us
    ppermute x1, starting transfers between devices, with_halo(): after = lax.ppermute(first, axis, down)  1.92 us
    add x1, other arithmetic, score_net(): score_field + q[:, tap:tap + 2, shift_x:shift_x + row_count, shift_y:shif...  1.91 us
  transfers between devices with their start and end apart: 3, of which 0 were waited for; matrix products, arithmetic and copies ran while one was open for 10% of the time, Pallas kernels for 19%

profile of v13, /device:TPU:1, one launch (start us, length us, event | category | flops | bytes accessed | tf_op | source)
XLA Modules:
  0.0 84.6 jit_solution(2177204956689884862)
XLA Ops:
  0.0 0.0 copy-start.8
  0.0 0.0 copy-start.7
  0.0 1.0 %convert_element_type.75 = bf16[2,2,32,384]{3,2,1,0:T(8,128)(2,1)S(1)} convert(f32[2,2,32,384]{3,2,1,0:T(8,128)} %param.14) | non-fusion elementwise | flops 49152 | bytes 294912 | tf_op jit(solution)/shard_map/convert_element_type | solution.py:209
  1.0 0.0 copy-start.5
  1.0 4.9 %collective-permute-start = (bf16[2,2,32,384]{3,2,1,0:T(8,128)(2,1)S(1)}, bf16[2,2,32,384]{3,2,1,0:T(8,128)(2,1)S(1)}, u32[]{:S(2)}, u32[]{:S(2)}) collective-permute-start(bf16[2,2,32,384]{3,2,1,0:T(8,128)(2,1)S(1)} %convert_element_type.75), channel_id=1, source_target_pairs={{0,1},{1,2},{2,3},{3,4},{4,5},{5,6},{6,7},{7,8},{8,9},{9,10},{10,1... | collective-permute-start | bytes 294920 | tf_op jit(solution)/shard_map/ppermute | solution.py:20
  6.0 1.9 %collective-permute-start.1 = (bf16[2,2,32,384]{3,2,1,0:T(8,128)(2,1)S(1)}, bf16[2,2,32,384]{3,2,1,0:T(8,128)(2,1)S(1)}, u32[]{:S(2)}, u32[]{:S(2)}) collective-permute-start(bf16[2,2,32,384]{3,2,1,0:T(8,128)(2,1)S(1)} %convert_element_type.75), channel_id=1, source_target_pairs={{1,0},{2,1},{3,2},{4,3},{5,4},{6,5},{7,6},{8,7},{9,8},{10,9},{11,1... | collective-permute-start | bytes 294920 | tf_op jit(solution)/shard_map/ppermute | solution.py:21
  7.9 1.1 %copy.60 = f32[2,2,32,384]{3,1,0,2:T(2,128)S(1)} copy(f32[2,2,32,384]{3,2,1,0:T(8,128)} %param.14) | data formatting | bytes 393216 | tf_op args[0]
  9.0 1.1 %broadcast_in_dim.2 = f32[2,2,32,4,384]{4,1,0,3,2:T(2,128)} broadcast(f32[2,2,32,384]{3,1,0,2:T(2,128)S(1)} %copy.60), dimensions={0,1,2,4} | broadcast | bytes 983040 | tf_op jit(solution)/shard_map/broadcast_in_dim | solution.py:213
  10.1 10.9 %all-to-all-start = ((f32[2,2,128,384]{3,1,0,2:T(2,128)}), f32[2,2,128,384]{3,1,0,2:T(2,128)S(1)}, u32[]{:S(2)}, u32[]{:S(2)}) async-start(f32[2,2,128,384]{3,1,0,2:T(2,128)} %bitcast.8), calls=%async_computation | async-start | bytes 1572864 | tf_op jit(solution)/shard_map/all_to_all | solution.py:215
  21.1 0.1 copy.52
  21.3 0.1 copy.54
  21.4 0.1 copy.56
  21.6 0.1 copy.57
  21.7 0.1 copy.58
  21.8 0.1 copy.59
  22.1 0.8 pad_maximum_fusion.1.p_ref
  22.9 0.0 collective-permute-done
  23.0 0.0 collective-permute-done.1
  23.1 1.1 %pad_slice_fusion.10 = (bf16[2,10,34,384]{3,2,1,0:T(8,128)(2,1)S(1)}, bf16[2,10,34,384]{3,2,1,0:T(8,128)(2,1)S(1)}, bf16[2,10,34,384]{3,2,1,0:T(8,128)(2,1)S(1)}) fusion(bf16[2,10,32,384]{3,2,1,0:T(8,128)(2,1)S(1)} %constant_dynamic-update-slice_fusion), kind=kLoop, calls=%fused_computation.11 | loop fusion | bytes 2058240 | tf_op jit(solution)/shard_map/slice | solution.py:153
  24.1 1.5 %pad_maximum_fusion.x_ref = bf16[2,30,34,384]{3,2,1,0:T(8,128)(2,1)} fusion(bf16[2,10,34,384]{3,2,1,0:T(8,128)(2,1)S(1)} %get-tuple-element.11, bf16[2,10,34,384]{3,2,1,0:T(8,128)(2,1)S(1)} %get-tuple-element.10, bf16[2,10,34,384]{3,2,1,0:T(8,128)(2,1)S(1)} %get-tuple-element.9), kind=kLoop, calls=%fused_computation.8 | loop fusion | flops 1566720 | bytes 3133440 | tf_op jit(solution)/shard_map/concatenate | solution.py:152
  25.6 16.4 %shard_map.136 = f32[2,18,32,384]{3,2,1,0:T(8,128)} custom-call(bf16[2,30,34,384]{3,2,1,0:T(8,128)(2,1)} %pad_maximum_fusion.x_ref, f32[152,768]{1,0:T(8,128)} %pad_maximum_fusion.1.p_ref), custom_call_target="tpu_custom_call" | custom-call | tf_op jit(solution)/shard_map/pallas_call | solution.py:170
  42.1 1.9 %fusion.7 = f32[2,2,32,384]{3,2,1,0:T(8,128)S(1)} fusion(f32[2,18,32,384]{3,2,1,0:T(8,128)} %shard_map.136), kind=kLoop, calls=%fused_computation.21 | loop fusion | flops 393216 | bytes 2162688 | tf_op jit(solution)/shard_map/add | solution.py:185
  44.0 0.0 all-to-all-done
  44.0 1.2 %copy.61 = f32[256,2,1,384]{0,3,2,1:T(8,128)} copy(f32[256,2,1,384]{3,1,0,2:T(2,128)S(1)} %bitcast.24) | data formatting | bytes 1572864 | tf_op jit(solution)/shard_map/optimization_barrier | solution.py:216
  45.2 13.9 %shard_map.137 = f32[2,1,384,256]{3,2,1,0:T(8,128)} custom-call(f32[2,1,384,256]{3,2,1,0:T(8,128)} %bitcast.26, bf16[4,2,1,384,256]{4,3,2,1,0:T(8,128)(2,1)} %sens_ref.1, bf16[4,2,1,384,256]{4,3,2,1,0:T(8,128)(2,1)} %meas_ref.1, s32[384,256]{1,0:T(8,128)} %mask_ref.1, bf16[768,384]{1,0:T(8,128)(2,1)} %constant.13.clone.ty_ref, ...), custom_call_target="tpu_custom_call" | custom-call | tf_op jit(solution)/shard_map/pallas_call | solution.py:97
  59.1 1.2 %convert_bitcast_fusion = bf16[256,2,1,384]{0,3,2,1:T(8,128)(2,1)S(1)} fusion(f32[2,1,384,256]{3,2,1,0:T(8,128)} %shard_map.137), kind=kLoop, calls=%fused_computation.13 | loop fusion | flops 196608 | bytes 1179648 | tf_op jit(solution)/shard_map/convert_element_type | solution.py:219
  60.3 0.0 copy-start.1
  60.3 0.5 copy.62
  60.8 22.3 %all_to_all.27 = bf16[256,2,1,384]{3,1,2,0:T(2,128)(2,1)S(1)} all-to-all(bf16[256,2,1,384]{3,1,2,0:T(2,128)(2,1)S(1)} %copy.62), channel_id=1, replica_groups=mesh['slab'=32,'coil'=4] {'slab','coil'}, dimensions={0} | all-to-all | bytes 786432 | tf_op jit(solution)/shard_map/all_to_all | solution.py:220
  83.1 0.3 convert.20
  83.3 0.5 reduce_sum.9
  83.9 0.7 fusion.10
  (35 shorter events, 0.3 us)
Async XLA Ops:
  0.0 21.0 %copy-start.4 = (bf16[3,3,10,128]{3,1,2,0:T(4,128)(2,1)S(1)}, bf16[3,3,10,128]{3,1,2,0:T(4,128)(2,1)}, u32[]{:S(2)}) copy-start(bf16[3,3,10,128]{3,1,2,0:T(4,128)(2,1)} %param.19) | copy-start | bytes 69124
  0.0 21.5 %copy-start.2 = (bf16[128,128]{1,0:T(8,128)(2,1)S(1)}, bf16[128,128]{1,0:T(8,128)(2,1)}, u32[]{:S(2)}) copy-start(bf16[128,128]{1,0:T(8,128)(2,1)} %param.21) | copy-start | bytes 98308
  0.0 21.7 %copy-start.3 = (bf16[128,128]{1,0:T(8,128)(2,1)S(1)}, bf16[128,128]{1,0:T(8,128)(2,1)}, u32[]{:S(2)}) copy-start(bf16[128,128]{1,0:T(8,128)(2,1)} %param.23) | copy-start | bytes 98308
  0.0 21.8 %copy-start.8 = (f32[128]{0:T(128)S(1)}, f32[128]{0:T(128)}, u32[]{:S(2)}) copy-start(f32[128]{0:T(128)} %param.20) | copy-start | bytes 1540
  0.0 21.8 %copy-start.7 = (f32[128]{0:T(128)S(1)}, f32[128]{0:T(128)}, u32[]{:S(2)}) copy-start(f32[128]{0:T(128)} %param.22) | copy-start | bytes 1540
  0.0 21.8 %copy-start.6 = (f32[128]{0:T(128)S(1)}, f32[128]{0:T(128)}, u32[]{:S(2)}) copy-start(f32[128]{0:T(128)} %param.24) | copy-start | bytes 1540
  1.0 20.9 %copy-start.5 = (bf16[3,3,2,128]{3,2,1,0:T(2,128)(2,1)S(1)}, bf16[3,3,2,128]{3,2,1,0:T(2,128)(2,1)}, u32[]{:S(2)}) copy-start(bf16[3,3,2,128]{3,2,1,0:T(2,128)(2,1)} %param.25) | copy-start | bytes 13828
  1.0 21.9 %collective-permute-start = (bf16[2,2,32,384]{3,2,1,0:T(8,128)(2,1)S(1)}, bf16[2,2,32,384]{3,2,1,0:T(8,128)(2,1)S(1)}, u32[]{:S(2)}, u32[]{:S(2)}) collective-permute-start(bf16[2,2,32,384]{3,2,1,0:T(8,128)(2,1)S(1)} %convert_element_type.75), channel_id=1, source_target_pairs={{0,1},{1,2},{2,3},{3,4},{4,5},{5,6},{6,7},{7,8},{8,9},{9,10},{10,1... | collective-permute-start | bytes 294920 | tf_op jit(solution)/shard_map/ppermute | solution.py:20
  6.0 17.0 %collective-permute-start.1 = (bf16[2,2,32,384]{3,2,1,0:T(8,128)(2,1)S(1)}, bf16[2,2,32,384]{3,2,1,0:T(8,128)(2,1)S(1)}, u32[]{:S(2)}, u32[]{:S(2)}) collective-permute-start(bf16[2,2,32,384]{3,2,1,0:T(8,128)(2,1)S(1)} %convert_element_type.75), channel_id=1, source_target_pairs={{1,0},{2,1},{3,2},{4,3},{5,4},{6,5},{7,6},{8,7},{9,8},{10,9},{11,1... | collective-permute-start | bytes 294920 | tf_op jit(solution)/shard_map/ppermute | solution.py:21
  10.1 12.9 %copy-start = (f32[2,2,32,384]{3,2,1,0:T(8,128)S(1)}, f32[2,2,32,384]{3,2,1,0:T(8,128)}, u32[]{:S(2)}) copy-start(f32[2,2,32,384]{3,2,1,0:T(8,128)} %param.14) | copy-start | bytes 589828
  10.1 33.9 %all-to-all-start = ((f32[2,2,128,384]{3,1,0,2:T(2,128)}), f32[2,2,128,384]{3,1,0,2:T(2,128)S(1)}, u32[]{:S(2)}, u32[]{:S(2)}) async-start(f32[2,2,128,384]{3,1,0,2:T(2,128)} %bitcast.8), calls=%async_computation | async-start | bytes 1572864 | tf_op jit(solution)/shard_map/all_to_all | solution.py:215
  60.3 23.6 %copy-start.1 = (f32[2,2,32,384]{3,2,1,0:T(8,128)S(1)}, f32[2,2,32,384]{3,2,1,0:T(8,128)}, u32[]{:S(2)}) copy-start(f32[2,2,32,384]{3,2,1,0:T(8,128)} %param.15) | copy-start | bytes 589828

commit v14 on v12

--- a/solution.py
+++ b/solution.py
@@ -206,13 +206,14 @@
     b_third,
     w_last,
 ):
-    window = with_halo(image.astype(jnp.bfloat16), ((("slab", "coil"), 0),), 2)
-    score_field = score_net(window, w_first, b_first, w_second, b_second, w_third, b_third, w_last)
     groups = lax.axis_size("coil")
     depth, parts, rows, lines = image.shape
     copies = jnp.broadcast_to(image[:, :, :, None], (depth, parts, rows, groups, lines))
     copies = copies.reshape(depth, parts, rows * groups, lines)
     planes_in = lax.all_to_all(copies, ("slab", "coil"), split_axis=2, concat_axis=0, tiled=True)
+    planes_in, local = lax.optimization_barrier((planes_in, image))
+    window = with_halo(local.astype(jnp.bfloat16), ((("slab", "coil"), 0),), 2)
+    score_field = score_net(window, w_first, b_first, w_second, b_second, w_third, b_third, w_last)
     planes = jnp.transpose(planes_in, (1, 2, 3, 0))
     partial_sum = coil_adjoint(planes, sens, measured, mask)
     by_depth = jnp.transpose(partial_sum, (3, 0, 1, 2)).astype(jnp.bfloat16)

time: 80.8 us -> 81.9 us (1.014)
  starting transfers between devices: 21.5 us -> 23.4 us
  other arithmetic: 6.45 us -> 5.46 us
    all_to_all x1, starting transfers between devices: 3.73 us -> 7.41 us  [on_device(): lax.all_to_all(by_depth, ('slab', 'coil'), split_axis=0, concat_axis=2, t...]
    ppermute x1, starting transfers between devices: 4.94 us -> 2.6 us  [with_halo(): before = lax.ppermute(last, axis, up)]
    optimization_barrier x0 -> x1, local copies, waits for them, and re-layouts: none -> 1.24 us  [on_device(): planes_in, local = lax.optimization_barrier((planes_in, image))]
    all_to_all x1 -> x0, local copies, waits for them, and re-layouts: 1.23 us -> none  [on_device(): lax.all_to_all(copies, ('slab', 'coil'), split_axis=2, concat_axis=0, til...]
    convert_element_type x1, other arithmetic: 0.99 us -> 0.01 us  [on_device(): window = with_halo(local.astype(jnp.bfloat16), ((('slab', 'coil'), 0),), 2)]
  transfers between devices with their start and end apart: 4 -> 4, of which waited for: 1 -> 1; matrix products, arithmetic and copies ran while one was open for 8% -> 10% of each run, Pallas kernels for 20% -> 37%
where the time goes in v14:
time: 81.9 us; the launch traced here: 81.5 us
  Pallas kernels  30.3 us (37%)
  starting transfers between devices  23.4 us (29%)
  waiting for transfers between devices  14.8 us (18%)
  local copies, waits for them, and re-layouts  7.21 us (9%)
  other arithmetic  5.46 us (7%)
    pallas_call x1, Pallas kernels, score_net(): pl.pallas_call(net_kernel, grid=(slice_count,), in_specs=[pl.BlockSpec((1...  16.4 us
    all_to_all x1, waiting for transfers between devices, on_device(): lax.all_to_all(copies, ('slab', 'coil'), split_axis=2, concat_axis=0, til...  14.8 us
    pallas_call x1, Pallas kernels, coil_adjoint(): pl.pallas_call(adjoint_kernel, grid=(coils,), in_specs=[pl.BlockSpec((2,...  13.9 us
    all_to_all x1, starting transfers between devices, on_device(): lax.all_to_all(copies, ('slab', 'coil'), split_axis=2, concat_axis=0, til...  11.5 us
    all_to_all x1, starting transfers between devices, on_device(): lax.all_to_all(by_depth, ('slab', 'coil'), split_axis=0, concat_axis=2, t...  7.41 us
    ppermute x1, starting transfers between devices, with_halo(): before = lax.ppermute(last, axis, up)  2.6 us
    unnamed x24, local copies, waits for them, and re-layouts  2.1 us
    ppermute x1, starting transfers between devices, with_halo(): after = lax.ppermute(first, axis, down)  1.92 us
  transfers between devices with their start and end apart: 4, of which 1 were waited for; matrix products, arithmetic and copies ran while one was open for 10% of the time, Pallas kernels for 37%

profile of v14, /device:TPU:1, one launch (start us, length us, event | category | flops | bytes accessed | tf_op | source)
XLA Modules:
  0.0 81.5 jit_solution(17323430554763108109)
XLA Ops:
  0.0 0.0 copy-start.4
  0.0 0.0 copy-start.7
  0.0 0.0 copy-start.8
  0.0 0.0 copy-start.9
  0.0 1.1 %copy.51 = f32[2,2,32,384]{3,1,0,2:T(2,128)S(1)} copy(f32[2,2,32,384]{3,2,1,0:T(8,128)} %param.14) | data formatting | bytes 393216 | tf_op args[0]
  1.2 1.1 %broadcast_in_dim.2 = f32[2,2,32,4,384]{4,1,0,3,2:T(2,128)} broadcast(f32[2,2,32,384]{3,1,0,2:T(2,128)S(1)} %copy.51), dimensions={0,1,2,4} | broadcast | bytes 983040 | tf_op jit(solution)/shard_map/broadcast_in_dim | solution.py:211
  2.3 11.5 %all-to-all-start = ((f32[2,2,128,384]{3,1,0,2:T(2,128)}), f32[2,2,128,384]{3,1,0,2:T(2,128)S(1)}, u32[]{:S(2)}, u32[]{:S(2)}) async-start(f32[2,2,128,384]{3,1,0,2:T(2,128)} %bitcast), calls=%async_computation | async-start | bytes 1572864 | tf_op jit(solution)/shard_map/all_to_all | solution.py:213
  13.9 0.1 copy.53
  14.1 0.1 copy.55
  14.2 0.1 copy.57
  14.4 0.1 copy.58
  14.5 0.1 copy.59
  14.6 0.1 copy.60
  14.9 0.8 pad_maximum_fusion.1.p_ref
  15.6 14.8 %all-to-all-done = f32[2,2,128,384]{3,1,0,2:T(2,128)S(1)} async-done(((f32[2,2,128,384]{3,1,0,2:T(2,128)}), f32[2,2,128,384]{3,1,0,2:T(2,128)S(1)}, u32[]{:S(2)}, u32[]{:S(2)}) %all-to-all-start) | async-done | bytes 786464 | tf_op jit(solution)/shard_map/all_to_all | solution.py:213
  30.5 2.6 %collective-permute-start = (bf16[2,2,32,384]{3,2,1,0:T(8,128)(2,1)S(1)}, bf16[2,2,32,384]{3,2,1,0:T(8,128)(2,1)S(1)}, u32[]{:S(2)}, u32[]{:S(2)}) collective-permute-start(bf16[2,2,32,384]{3,2,1,0:T(8,128)(2,1)S(1)} %convert_element_type.75), channel_id=1, source_target_pairs={{0,1},{1,2},{2,3},{3,4},{4,5},{5,6},{6,7},{7,8},{8,9},{9,10},{10,1... | collective-permute-start | bytes 294920 | tf_op jit(solution)/shard_map/ppermute | solution.py:20
  33.1 1.9 %collective-permute-start.1 = (bf16[2,2,32,384]{3,2,1,0:T(8,128)(2,1)S(1)}, bf16[2,2,32,384]{3,2,1,0:T(8,128)(2,1)S(1)}, u32[]{:S(2)}, u32[]{:S(2)}) collective-permute-start(bf16[2,2,32,384]{3,2,1,0:T(8,128)(2,1)S(1)} %convert_element_type.75), channel_id=1, source_target_pairs={{1,0},{2,1},{3,2},{4,3},{5,4},{6,5},{7,6},{8,7},{9,8},{10,9},{11,1... | collective-permute-start | bytes 294920 | tf_op jit(solution)/shard_map/ppermute | solution.py:21
  35.0 1.2 %copy.61 = f32[256,2,1,384]{0,3,2,1:T(8,128)} copy(f32[256,2,1,384]{3,1,0,2:T(2,128)S(1)} %bitcast.24) | data formatting | bytes 1572864 | tf_op jit(solution)/shard_map/optimization_barrier | solution.py:214
  36.2 13.9 %shard_map.137 = f32[2,1,384,256]{3,2,1,0:T(8,128)} custom-call(f32[2,1,384,256]{3,2,1,0:T(8,128)} %bitcast.26, bf16[4,2,1,384,256]{4,3,2,1,0:T(8,128)(2,1)} %sens_ref.1, bf16[4,2,1,384,256]{4,3,2,1,0:T(8,128)(2,1)} %meas_ref.1, s32[384,256]{1,0:T(8,128)} %mask_ref.1, bf16[768,384]{1,0:T(8,128)(2,1)} %constant.13.clone.ty_ref, ...), custom_call_target="tpu_custom_call" | custom-call | tf_op jit(solution)/shard_map/pallas_call | solution.py:97
  50.1 1.2 %convert_bitcast_fusion = bf16[256,2,1,384]{0,3,2,1:T(8,128)(2,1)S(1)} fusion(f32[2,1,384,256]{3,2,1,0:T(8,128)} %shard_map.137), kind=kLoop, calls=%fused_computation.13 | loop fusion | flops 196608 | bytes 1179648 | tf_op jit(solution)/shard_map/convert_element_type | solution.py:219
  51.3 1.1 %copy.62 = bf16[256,2,1,384]{3,1,2,0:T(2,128)(2,1)} copy(bf16[256,2,1,384]{0,3,2,1:T(8,128)(2,1)S(1)} %convert_bitcast_fusion) | data formatting | bytes 786432 | tf_op jit(solution)/shard_map/convert_element_type | solution.py:219
  52.4 7.4 %all-to-all-start.1 = ((bf16[256,2,1,384]{3,1,2,0:T(2,128)(2,1)}), bf16[256,2,1,384]{3,1,2,0:T(2,128)(2,1)S(1)}, u32[]{:S(2)}, u32[]{:S(2)}) async-start(bf16[256,2,1,384]{3,1,2,0:T(2,128)(2,1)} %copy.62), calls=%async_computation.1 | async-start | bytes 786432 | tf_op jit(solution)/shard_map/all_to_all | solution.py:220
  59.8 0.0 collective-permute-done
  59.9 0.0 collective-permute-done.1
  59.9 1.1 %pad_slice_fusion.10 = (bf16[2,10,34,384]{3,2,1,0:T(8,128)(2,1)S(1)}, bf16[2,10,34,384]{3,2,1,0:T(8,128)(2,1)S(1)}, bf16[2,10,34,384]{3,2,1,0:T(8,128)(2,1)S(1)}) fusion(bf16[2,10,32,384]{3,2,1,0:T(8,128)(2,1)S(1)} %constant_dynamic-update-slice_fusion), kind=kLoop, calls=%fused_computation.11 | loop fusion | bytes 2058240 | tf_op jit(solution)/shard_map/slice | solution.py:153
  61.0 1.5 %pad_maximum_fusion.x_ref = bf16[2,30,34,384]{3,2,1,0:T(8,128)(2,1)} fusion(bf16[2,10,34,384]{3,2,1,0:T(8,128)(2,1)S(1)} %get-tuple-element.11, bf16[2,10,34,384]{3,2,1,0:T(8,128)(2,1)S(1)} %get-tuple-element.10, bf16[2,10,34,384]{3,2,1,0:T(8,128)(2,1)S(1)} %get-tuple-element.9), kind=kLoop, calls=%fused_computation.8 | loop fusion | flops 1566720 | bytes 3133440 | tf_op jit(solution)/shard_map/concatenate | solution.py:152
  62.5 16.4 %shard_map.136 = f32[2,18,32,384]{3,2,1,0:T(8,128)} custom-call(bf16[2,30,34,384]{3,2,1,0:T(8,128)(2,1)} %pad_maximum_fusion.x_ref, f32[152,768]{1,0:T(8,128)} %pad_maximum_fusion.1.p_ref), custom_call_target="tpu_custom_call" | custom-call | tf_op jit(solution)/shard_map/pallas_call | solution.py:170
  79.0 0.0 all-to-all-done.1
  79.0 0.3 convert.20
  79.3 0.5 reduce_sum.9
  79.8 0.7 copy-done
  80.5 1.1 %add_add_fusion = f32[2,2,32,384]{3,2,1,0:T(8,128)} fusion(f32[2,2,32,384]{3,2,1,0:T(8,128)S(1)} %copy-done.2, f32[2,2,32,384]{3,2,1,0:T(8,128)S(1)} %copy-done.1, f32[2,2,32,384]{3,1,0,2:T(2,128)S(1)} %reduce_sum.9, f32[2,18,32,384]{3,2,1,0:T(8,128)S(1)} %copy-done), kind=kLoop, calls=%fused_computation.23 | loop fusion | flops 589824 | bytes 2752512 | tf_op jit(solution)/shard_map/add | solution.py:223
  (37 shorter events, 0.3 us)
Async XLA Ops:
  0.0 13.8 %copy-start.6 = (bf16[3,3,2,128]{3,2,1,0:T(2,128)(2,1)S(1)}, bf16[3,3,2,128]{3,2,1,0:T(2,128)(2,1)}, u32[]{:S(2)}) copy-start(bf16[3,3,2,128]{3,2,1,0:T(2,128)(2,1)} %param.25) | copy-start | bytes 13828
  0.0 13.8 %copy-start.5 = (bf16[3,3,10,128]{3,1,2,0:T(4,128)(2,1)S(1)}, bf16[3,3,10,128]{3,1,2,0:T(4,128)(2,1)}, u32[]{:S(2)}) copy-start(bf16[3,3,10,128]{3,1,2,0:T(4,128)(2,1)} %param.19) | copy-start | bytes 69124
  0.0 14.3 %copy-start.3 = (bf16[128,128]{1,0:T(8,128)(2,1)S(1)}, bf16[128,128]{1,0:T(8,128)(2,1)}, u32[]{:S(2)}) copy-start(bf16[128,128]{1,0:T(8,128)(2,1)} %param.21) | copy-start | bytes 98308
  0.0 14.5 %copy-start.4 = (bf16[128,128]{1,0:T(8,128)(2,1)S(1)}, bf16[128,128]{1,0:T(8,128)(2,1)}, u32[]{:S(2)}) copy-start(bf16[128,128]{1,0:T(8,128)(2,1)} %param.23) | copy-start | bytes 98308
  0.0 14.6 %copy-start.7 = (f32[128]{0:T(128)S(1)}, f32[128]{0:T(128)}, u32[]{:S(2)}) copy-start(f32[128]{0:T(128)} %param.24) | copy-start | bytes 1540
  0.0 14.6 %copy-start.8 = (f32[128]{0:T(128)S(1)}, f32[128]{0:T(128)}, u32[]{:S(2)}) copy-start(f32[128]{0:T(128)} %param.22) | copy-start | bytes 1540
  0.0 14.6 %copy-start.9 = (f32[128]{0:T(128)S(1)}, f32[128]{0:T(128)}, u32[]{:S(2)}) copy-start(f32[128]{0:T(128)} %param.20) | copy-start | bytes 1540
  2.3 28.1 %copy-start.1 = (f32[2,2,32,384]{3,2,1,0:T(8,128)S(1)}, f32[2,2,32,384]{3,2,1,0:T(8,128)}, u32[]{:S(2)}) copy-start(f32[2,2,32,384]{3,2,1,0:T(8,128)} %param.14) | copy-start | bytes 589828
  2.3 28.1 %all-to-all-start = ((f32[2,2,128,384]{3,1,0,2:T(2,128)}), f32[2,2,128,384]{3,1,0,2:T(2,128)S(1)}, u32[]{:S(2)}, u32[]{:S(2)}) async-start(f32[2,2,128,384]{3,1,0,2:T(2,128)} %bitcast), calls=%async_computation | async-start | bytes 1572864 | tf_op jit(solution)/shard_map/all_to_all | solution.py:213
  30.5 29.3 %collective-permute-start = (bf16[2,2,32,384]{3,2,1,0:T(8,128)(2,1)S(1)}, bf16[2,2,32,384]{3,2,1,0:T(8,128)(2,1)S(1)}, u32[]{:S(2)}, u32[]{:S(2)}) collective-permute-start(bf16[2,2,32,384]{3,2,1,0:T(8,128)(2,1)S(1)} %convert_element_type.75), channel_id=1, source_target_pairs={{0,1},{1,2},{2,3},{3,4},{4,5},{5,6},{6,7},{7,8},{8,9},{9,10},{10,1... | collective-permute-start | bytes 294920 | tf_op jit(solution)/shard_map/ppermute | solution.py:20
  33.1 26.8 %collective-permute-start.1 = (bf16[2,2,32,384]{3,2,1,0:T(8,128)(2,1)S(1)}, bf16[2,2,32,384]{3,2,1,0:T(8,128)(2,1)S(1)}, u32[]{:S(2)}, u32[]{:S(2)}) collective-permute-start(bf16[2,2,32,384]{3,2,1,0:T(8,128)(2,1)S(1)} %convert_element_type.75), channel_id=1, source_target_pairs={{1,0},{2,1},{3,2},{4,3},{5,4},{6,5},{7,6},{8,7},{9,8},{10,9},{11,1... | collective-permute-start | bytes 294920 | tf_op jit(solution)/shard_map/ppermute | solution.py:21
  52.4 26.6 %all-to-all-start.1 = ((bf16[256,2,1,384]{3,1,2,0:T(2,128)(2,1)}), bf16[256,2,1,384]{3,1,2,0:T(2,128)(2,1)S(1)}, u32[]{:S(2)}, u32[]{:S(2)}) async-start(bf16[256,2,1,384]{3,1,2,0:T(2,128)(2,1)} %copy.62), calls=%async_computation.1 | async-start | bytes 786432 | tf_op jit(solution)/shard_map/all_to_all | solution.py:220
  79.0 1.5 %copy-start = (f32[2,18,32,384]{3,2,1,0:T(8,128)S(1)}, f32[2,18,32,384]{3,2,1,0:T(8,128)}, u32[]{:S(2)}) copy-start(f32[2,18,32,384]{3,2,1,0:T(8,128)} %shard_map.136) | copy-start | bytes 5308420
  79.0 1.5 %copy-start.2 = (f32[2,2,32,384]{3,2,1,0:T(8,128)S(1)}, f32[2,2,32,384]{3,2,1,0:T(8,128)}, u32[]{:S(2)}) copy-start(f32[2,2,32,384]{3,2,1,0:T(8,128)} %param.15) | copy-start | bytes 589828

commit v15 on v12

--- a/solution.py
+++ b/solution.py
@@ -210,10 +210,11 @@
     score_field = score_net(window, w_first, b_first, w_second, b_second, w_third, b_third, w_last)
     groups = lax.axis_size("coil")
     depth, parts, rows, lines = image.shape
-    copies = jnp.broadcast_to(image[:, :, :, None], (depth, parts, rows, groups, lines))
-    copies = copies.reshape(depth, parts, rows * groups, lines)
-    planes_in = lax.all_to_all(copies, ("slab", "coil"), split_axis=2, concat_axis=0, tiled=True)
-    planes = jnp.transpose(planes_in, (1, 2, 3, 0))
+    by_row = jnp.transpose(image, (2, 0, 1, 3))[:, None]
+    copies = jnp.broadcast_to(by_row, (rows, groups, depth, parts, lines))
+    copies = copies.reshape(rows * groups, depth, parts, lines)
+    planes_in = lax.all_to_all(copies, ("slab", "coil"), split_axis=0, concat_axis=1, tiled=True)
+    planes = jnp.transpose(planes_in, (2, 0, 3, 1))
     partial_sum = coil_adjoint(planes, sens, measured, mask)
     by_depth = jnp.transpose(partial_sum, (3, 0, 1, 2)).astype(jnp.bfloat16)
     by_device = lax.all_to_all(by_depth, ("slab", "coil"), split_axis=0, concat_axis=2, tiled=True)

time: 80.8 us -> 80.8 us (level)
    unnamed x24 -> x23, local copies, waits for them, and re-layouts: 2.04 us -> 0.96 us
    transpose x0 -> x1, local copies, waits for them, and re-layouts: none -> 1.08 us  [on_device(): by_row = jnp.transpose(image, (2, 0, 1, 3))[:, None]]
where the time goes in v15:
time: 80.8 us; the launch traced here: 80.4 us
  Pallas kernels  30.3 us (38%)
  starting transfers between devices  21.5 us (27%)
  waiting for transfers between devices  14.7 us (18%)
  local copies, waits for them, and re-layouts  7.15 us (9%)
  other arithmetic  6.45 us (8%)
    pallas_call x1, Pallas kernels, score_net(): pl.pallas_call(net_kernel, grid=(slice_count,), in_specs=[pl.BlockSpec((1...  16.5 us
    all_to_all x1, waiting for transfers between devices, on_device(): lax.all_to_all(copies, ('slab', 'coil'), split_axis=0, concat_axis=1, til...  14.7 us
    pallas_call x1, Pallas kernels, coil_adjoint(): pl.pallas_call(adjoint_kernel, grid=(coils,), in_specs=[pl.BlockSpec((2,...  13.8 us
    all_to_all x1, starting transfers between devices, on_device(): lax.all_to_all(copies, ('slab', 'coil'), split_axis=0, concat_axis=1, til...  10.9 us
    ppermute x1, starting transfers between devices, with_halo(): before = lax.ppermute(last, axis, up)  4.94 us
    all_to_all x1, starting transfers between devices, on_device(): lax.all_to_all(by_depth, ('slab', 'coil'), split_axis=0, concat_axis=2, t...  3.73 us
    ppermute x1, starting transfers between devices, with_halo(): after = lax.ppermute(first, axis, down)  1.92 us
  transfers between devices with their start and end apart: 4, of which 1 were waited for; matrix products, arithmetic and copies ran while one was open for 8% of the time, Pallas kernels for 20%

profile of v15, /device:TPU:1, one launch (start us, length us, event | category | flops | bytes accessed | tf_op | source)
XLA Modules:
  0.0 80.4 jit_solution(17836790815504781011)
XLA Ops:
  0.0 0.0 copy-start.9
  0.0 0.0 copy-start.8
  0.0 1.0 %convert_element_type.75 = bf16[2,2,32,384]{3,2,1,0:T(8,128)(2,1)S(1)} convert(f32[2,2,32,384]{3,2,1,0:T(8,128)} %param.14) | non-fusion elementwise | flops 49152 | bytes 294912 | tf_op jit(solution)/shard_map/convert_element_type | solution.py:209
  1.0 0.0 copy-start.6
  1.0 4.9 %collective-permute-start = (bf16[2,2,32,384]{3,2,1,0:T(8,128)(2,1)S(1)}, bf16[2,2,32,384]{3,2,1,0:T(8,128)(2,1)S(1)}, u32[]{:S(2)}, u32[]{:S(2)}) collective-permute-start(bf16[2,2,32,384]{3,2,1,0:T(8,128)(2,1)S(1)} %convert_element_type.75), channel_id=1, source_target_pairs={{0,1},{1,2},{2,3},{3,4},{4,5},{5,6},{6,7},{7,8},{8,9},{9,10},{10,1... | collective-permute-start | bytes 294920 | tf_op jit(solution)/shard_map/ppermute | solution.py:20
  6.0 1.9 %collective-permute-start.1 = (bf16[2,2,32,384]{3,2,1,0:T(8,128)(2,1)S(1)}, bf16[2,2,32,384]{3,2,1,0:T(8,128)(2,1)S(1)}, u32[]{:S(2)}, u32[]{:S(2)}) collective-permute-start(bf16[2,2,32,384]{3,2,1,0:T(8,128)(2,1)S(1)} %convert_element_type.75), channel_id=1, source_target_pairs={{1,0},{2,1},{3,2},{4,3},{5,4},{6,5},{7,6},{8,7},{9,8},{10,9},{11,1... | collective-permute-start | bytes 294920 | tf_op jit(solution)/shard_map/ppermute | solution.py:21
  7.9 1.1 %copy.60 = f32[32,2,2,384]{3,2,1,0:T(2,128)S(1)} copy(f32[32,2,2,384]{3,0,2,1:T(8,128)} %bitcast.24) | data formatting | bytes 393216 | tf_op jit(solution)/shard_map/transpose | solution.py:213
  9.0 1.1 %broadcast_in_dim.2 = f32[32,4,2,2,384]{4,3,2,1,0:T(2,128)} broadcast(f32[32,2,2,384]{3,2,1,0:T(2,128)S(1)} %copy.60), dimensions={0,2,3,4} | broadcast | bytes 983040 | tf_op jit(solution)/shard_map/broadcast_in_dim | solution.py:214
  10.1 10.9 %all-to-all-start = ((f32[128,2,2,384]{3,2,1,0:T(2,128)}), f32[128,2,2,384]{3,2,1,0:T(2,128)S(1)}, u32[]{:S(2)}, u32[]{:S(2)}) async-start(f32[128,2,2,384]{3,2,1,0:T(2,128)} %bitcast.9), calls=%async_computation | async-start | bytes 1572864 | tf_op jit(solution)/shard_map/all_to_all | solution.py:216
  21.1 0.1 copy.52
  21.3 0.1 copy.54
  21.4 0.1 copy.56
  21.6 0.1 copy.57
  21.7 0.1 copy.58
  21.9 0.1 copy.59
  22.1 0.8 pad_maximum_fusion.1.p_ref
  22.9 0.0 collective-permute-done
  23.0 0.0 collective-permute-done.1
  23.0 14.7 %all-to-all-done = f32[128,2,2,384]{3,2,1,0:T(2,128)S(1)} async-done(((f32[128,2,2,384]{3,2,1,0:T(2,128)}), f32[128,2,2,384]{3,2,1,0:T(2,128)S(1)}, u32[]{:S(2)}, u32[]{:S(2)}) %all-to-all-start) | async-done | bytes 786464 | tf_op jit(solution)/shard_map/all_to_all | solution.py:216
  37.7 1.2 %copy.61 = f32[1,256,2,384]{1,3,0,2:T(8,128)} copy(f32[1,256,2,384]{3,2,1,0:T(2,128)S(1)} %bitcast.21) | data formatting | bytes 1572864 | tf_op jit(solution)/shard_map/all_to_all | solution.py:216
  38.9 13.8 %shard_map.137 = f32[2,1,384,256]{3,2,1,0:T(8,128)} custom-call(f32[2,1,384,256]{3,2,1,0:T(8,128)} %bitcast.23, bf16[4,2,1,384,256]{4,3,2,1,0:T(8,128)(2,1)} %sens_ref.1, bf16[4,2,1,384,256]{4,3,2,1,0:T(8,128)(2,1)} %meas_ref.1, s32[384,256]{1,0:T(8,128)} %mask_ref.1, bf16[768,384]{1,0:T(8,128)(2,1)} %constant.13.clone.ty_ref, ...), custom_call_target="tpu_custom_call" | custom-call | tf_op jit(solution)/shard_map/pallas_call | solution.py:97
  52.8 1.2 %convert_bitcast_fusion = bf16[256,2,1,384]{0,3,2,1:T(8,128)(2,1)S(1)} fusion(f32[2,1,384,256]{3,2,1,0:T(8,128)} %shard_map.137), kind=kLoop, calls=%fused_computation.13 | loop fusion | flops 196608 | bytes 1179648 | tf_op jit(solution)/shard_map/convert_element_type | solution.py:219
  54.0 1.1 %copy.62 = bf16[256,2,1,384]{3,1,2,0:T(2,128)(2,1)} copy(bf16[256,2,1,384]{0,3,2,1:T(8,128)(2,1)S(1)} %convert_bitcast_fusion) | data formatting | bytes 786432 | tf_op jit(solution)/shard_map/convert_element_type | solution.py:219
  55.1 3.7 %all-to-all-start.1 = ((bf16[256,2,1,384]{3,1,2,0:T(2,128)(2,1)}), bf16[256,2,1,384]{3,1,2,0:T(2,128)(2,1)S(1)}, u32[]{:S(2)}, u32[]{:S(2)}) async-start(bf16[256,2,1,384]{3,1,2,0:T(2,128)(2,1)} %copy.62), calls=%async_computation.1 | async-start | bytes 786432 | tf_op jit(solution)/shard_map/all_to_all | solution.py:220
  58.8 1.1 %pad_slice_fusion.10 = (bf16[2,10,34,384]{3,2,1,0:T(8,128)(2,1)S(1)}, bf16[2,10,34,384]{3,2,1,0:T(8,128)(2,1)S(1)}, bf16[2,10,34,384]{3,2,1,0:T(8,128)(2,1)S(1)}) fusion(bf16[2,10,32,384]{3,2,1,0:T(8,128)(2,1)S(1)} %constant_dynamic-update-slice_fusion), kind=kLoop, calls=%fused_computation.11 | loop fusion | bytes 2058240 | tf_op jit(solution)/shard_map/slice | solution.py:153
  59.9 1.5 %pad_maximum_fusion.x_ref = bf16[2,30,34,384]{3,2,1,0:T(8,128)(2,1)} fusion(bf16[2,10,34,384]{3,2,1,0:T(8,128)(2,1)S(1)} %get-tuple-element.7, bf16[2,10,34,384]{3,2,1,0:T(8,128)(2,1)S(1)} %get-tuple-element.6, bf16[2,10,34,384]{3,2,1,0:T(8,128)(2,1)S(1)} %get-tuple-element.5), kind=kLoop, calls=%fused_computation.8 | loop fusion | flops 1566720 | bytes 3133440 | tf_op jit(solution)/shard_map/concatenate | solution.py:152
  61.4 16.5 %shard_map.136 = f32[2,18,32,384]{3,2,1,0:T(8,128)} custom-call(bf16[2,30,34,384]{3,2,1,0:T(8,128)(2,1)} %pad_maximum_fusion.x_ref, f32[152,768]{1,0:T(8,128)} %pad_maximum_fusion.1.p_ref), custom_call_target="tpu_custom_call" | custom-call | tf_op jit(solution)/shard_map/pallas_call | solution.py:170
  77.9 0.0 all-to-all-done.1
  77.9 0.3 convert.20
  78.2 0.5 reduce_sum.9
  78.7 0.7 copy-done
  79.4 1.1 %add_add_fusion = f32[2,2,32,384]{3,2,1,0:T(8,128)} fusion(f32[2,2,32,384]{3,2,1,0:T(8,128)S(1)} %copy-done.2, f32[2,2,32,384]{3,2,1,0:T(8,128)S(1)} %copy-done.1, f32[2,2,32,384]{3,1,0,2:T(2,128)S(1)} %reduce_sum.9, f32[2,18,32,384]{3,2,1,0:T(8,128)S(1)} %copy-done), kind=kLoop, calls=%fused_computation.23 | loop fusion | flops 589824 | bytes 2752512 | tf_op jit(solution)/shard_map/add | solution.py:223
  (37 shorter events, 0.3 us)
Async XLA Ops:
  0.0 21.1 %copy-start.5 = (bf16[3,3,10,128]{3,1,2,0:T(4,128)(2,1)S(1)}, bf16[3,3,10,128]{3,1,2,0:T(4,128)(2,1)}, u32[]{:S(2)}) copy-start(bf16[3,3,10,128]{3,1,2,0:T(4,128)(2,1)} %param.19) | copy-start | bytes 69124
  0.0 21.6 %copy-start.3 = (bf16[128,128]{1,0:T(8,128)(2,1)S(1)}, bf16[128,128]{1,0:T(8,128)(2,1)}, u32[]{:S(2)}) copy-start(bf16[128,128]{1,0:T(8,128)(2,1)} %param.21) | copy-start | bytes 98308
  0.0 21.7 %copy-start.4 = (bf16[128,128]{1,0:T(8,128)(2,1)S(1)}, bf16[128,128]{1,0:T(8,128)(2,1)}, u32[]{:S(2)}) copy-start(bf16[128,128]{1,0:T(8,128)(2,1)} %param.23) | copy-start | bytes 98308
  0.0 21.8 %copy-start.9 = (f32[128]{0:T(128)S(1)}, f32[128]{0:T(128)}, u32[]{:S(2)}) copy-start(f32[128]{0:T(128)} %param.20) | copy-start | bytes 1540
  0.0 21.8 %copy-start.8 = (f32[128]{0:T(128)S(1)}, f32[128]{0:T(128)}, u32[]{:S(2)}) copy-start(f32[128]{0:T(128)} %param.22) | copy-start | bytes 1540
  0.0 21.8 %copy-start.7 = (f32[128]{0:T(128)S(1)}, f32[128]{0:T(128)}, u32[]{:S(2)}) copy-start(f32[128]{0:T(128)} %param.24) | copy-start | bytes 1540
  1.0 21.0 %copy-start.6 = (bf16[3,3,2,128]{3,2,1,0:T(2,128)(2,1)S(1)}, bf16[3,3,2,128]{3,2,1,0:T(2,128)(2,1)}, u32[]{:S(2)}) copy-start(bf16[3,3,2,128]{3,2,1,0:T(2,128)(2,1)} %param.25) | copy-start | bytes 13828
  1.0 21.9 %collective-permute-start = (bf16[2,2,32,384]{3,2,1,0:T(8,128)(2,1)S(1)}, bf16[2,2,32,384]{3,2,1,0:T(8,128)(2,1)S(1)}, u32[]{:S(2)}, u32[]{:S(2)}) collective-permute-start(bf16[2,2,32,384]{3,2,1,0:T(8,128)(2,1)S(1)} %convert_element_type.75), channel_id=1, source_target_pairs={{0,1},{1,2},{2,3},{3,4},{4,5},{5,6},{6,7},{7,8},{8,9},{9,10},{10,1... | collective-permute-start | bytes 294920 | tf_op jit(solution)/shard_map/ppermute | solution.py:20
  6.0 17.0 %collective-permute-start.1 = (bf16[2,2,32,384]{3,2,1,0:T(8,128)(2,1)S(1)}, bf16[2,2,32,384]{3,2,1,0:T(8,128)(2,1)S(1)}, u32[]{:S(2)}, u32[]{:S(2)}) collective-permute-start(bf16[2,2,32,384]{3,2,1,0:T(8,128)(2,1)S(1)} %convert_element_type.75), channel_id=1, source_target_pairs={{1,0},{2,1},{3,2},{4,3},{5,4},{6,5},{7,6},{8,7},{9,8},{10,9},{11,1... | collective-permute-start | bytes 294920 | tf_op jit(solution)/shard_map/ppermute | solution.py:21
  10.1 12.8 %copy-start.1 = (f32[2,2,32,384]{3,2,1,0:T(8,128)S(1)}, f32[2,2,32,384]{3,2,1,0:T(8,128)}, u32[]{:S(2)}) copy-start(f32[2,2,32,384]{3,2,1,0:T(8,128)} %param.14) | copy-start | bytes 589828
  10.1 27.6 %all-to-all-start = ((f32[128,2,2,384]{3,2,1,0:T(2,128)}), f32[128,2,2,384]{3,2,1,0:T(2,128)S(1)}, u32[]{:S(2)}, u32[]{:S(2)}) async-start(f32[128,2,2,384]{3,2,1,0:T(2,128)} %bitcast.9), calls=%async_computation | async-start | bytes 1572864 | tf_op jit(solution)/shard_map/all_to_all | solution.py:216
  55.1 22.8 %all-to-all-start.1 = ((bf16[256,2,1,384]{3,1,2,0:T(2,128)(2,1)}), bf16[256,2,1,384]{3,1,2,0:T(2,128)(2,1)S(1)}, u32[]{:S(2)}, u32[]{:S(2)}) async-start(bf16[256,2,1,384]{3,1,2,0:T(2,128)(2,1)} %copy.62), calls=%async_computation.1 | async-start | bytes 786432 | tf_op jit(solution)/shard_map/all_to_all | solution.py:220
  77.9 1.5 %copy-start = (f32[2,18,32,384]{3,2,1,0:T(8,128)S(1)}, f32[2,18,32,384]{3,2,1,0:T(8,128)}, u32[]{:S(2)}) copy-start(f32[2,18,32,384]{3,2,1,0:T(8,128)} %shard_map.136) | copy-start | bytes 5308420
  77.9 1.5 %copy-start.2 = (f32[2,2,32,384]{3,2,1,0:T(8,128)S(1)}, f32[2,2,32,384]{3,2,1,0:T(8,128)}, u32[]{:S(2)}) copy-start(f32[2,2,32,384]{3,2,1,0:T(8,128)} %param.15) | copy-start | bytes 589828

commit v16 on v12

--- a/solution.py
+++ b/solution.py
@@ -140,7 +140,7 @@
             q_ref[0, :, first + row, :] = q[:, row * cols : (row + 1) * cols]
 
 
-def score_net(window, w_first, b_first, w_second, b_second, w_third, b_third, w_last):
+def score_net(window, w_first, b_first, w_second, b_second, w_third, b_third, w_last, tie):
     slice_count = window.shape[0] - 4
     row_count = window.shape[2]
     col_count = window.shape[3]
@@ -167,6 +167,7 @@
     )
     bottom = jnp.pad(wl.astype(jnp.float32), ((0, 24 - outs), (0, 5 * width)))
     packed = jnp.concatenate([top, bottom], axis=0)
+    shifted, packed, tie = lax.optimization_barrier((shifted, packed, tie))
     q = pl.pallas_call(
         net_kernel,
         grid=(slice_count,),
@@ -185,7 +186,7 @@
             score_field = score_field + q[
                 :, tap : tap + 2, shift_x : shift_x + row_count, shift_y : shift_y + col_count
             ]
-    return score_field
+    return score_field, tie
 
 
 def slab_slices(image):
@@ -207,12 +208,14 @@
     w_last,
 ):
     window = with_halo(image.astype(jnp.bfloat16), ((("slab", "coil"), 0),), 2)
-    score_field = score_net(window, w_first, b_first, w_second, b_second, w_third, b_third, w_last)
     groups = lax.axis_size("coil")
     depth, parts, rows, lines = image.shape
     copies = jnp.broadcast_to(image[:, :, :, None], (depth, parts, rows, groups, lines))
     copies = copies.reshape(depth, parts, rows * groups, lines)
     planes_in = lax.all_to_all(copies, ("slab", "coil"), split_axis=2, concat_axis=0, tiled=True)
+    score_field, planes_in = score_net(
+        window, w_first, b_first, w_second, b_second, w_third, b_third, w_last, planes_in
+    )
     planes = jnp.transpose(planes_in, (1, 2, 3, 0))
     partial_sum = coil_adjoint(planes, sens, measured, mask)
     by_depth = jnp.transpose(partial_sum, (3, 0, 1, 2)).astype(jnp.bfloat16)

time: 80.8 us -> 78.3 us (0.969)
  waiting for transfers between devices: 14.7 us -> 12 us
    all_to_all x1, waiting for transfers between devices: 14.7 us -> 12 us  [on_device(): lax.all_to_all(copies, ('slab', 'coil'), split_axis=2, concat_axis=0, til...]
    optimization_barrier x0 -> x1, local copies, waits for them, and re-layouts: none -> 1.24 us  [score_net(): shifted, packed, tie = lax.optimization_barrier((shifted, packed, tie))]
    all_to_all x1 -> x0, local copies, waits for them, and re-layouts: 1.23 us -> none  [on_device(): lax.all_to_all(copies, ('slab', 'coil'), split_axis=2, concat_axis=0, til...]
  transfers between devices with their start and end apart: 4 -> 4, of which waited for: 1 -> 1; matrix products, arithmetic and copies ran while one was open for 8% -> 8% of each run, Pallas kernels for 20% -> 21%
where the time goes in v16:
time: 78.3 us; the launch traced here: 77.9 us
  Pallas kernels  30.3 us (39%)
  starting transfers between devices  21.6 us (28%)
  waiting for transfers between devices  12 us (15%)
  local copies, waits for them, and re-layouts  7.19 us (9%)
  other arithmetic  6.47 us (8%)
    pallas_call x1, Pallas kernels, score_net(): pl.pallas_call(net_kernel, grid=(slice_count,), in_specs=[pl.BlockSpec((1...  16.4 us
    pallas_call x1, Pallas kernels, coil_adjoint(): pl.pallas_call(adjoint_kernel, grid=(coils,), in_specs=[pl.BlockSpec((2,...  13.8 us
    all_to_all x1, waiting for transfers between devices, on_device(): lax.all_to_all(copies, ('slab', 'coil'), split_axis=2, concat_axis=0, til...  12 us
    all_to_all x1, starting transfers between devices, on_device(): lax.all_to_all(copies, ('slab', 'coil'), split_axis=2, concat_axis=0, til...  10.9 us
    ppermute x1, starting transfers between devices, with_halo(): before = lax.ppermute(last, axis, up)  5.07 us
    all_to_all x1, starting transfers between devices, on_device(): lax.all_to_all(by_depth, ('slab', 'coil'), split_axis=0, concat_axis=2, t...  3.72 us
    unnamed x24, local copies, waits for them, and re-layouts  2.05 us
    ppermute x1, starting transfers between devices, with_halo(): after = lax.ppermute(first, axis, down)  1.92 us
  transfers between devices with their start and end apart: 4, of which 1 were waited for; matrix products, arithmetic and copies ran while one was open for 8% of the time, Pallas kernels for 21%

profile of v16, /device:TPU:1, one launch (start us, length us, event | category | flops | bytes accessed | tf_op | source)
XLA Modules:
  0.0 77.9 jit_solution(18294383776426230453)
XLA Ops:
  0.0 1.0 %convert_element_type.75 = bf16[2,2,32,384]{3,2,1,0:T(8,128)(2,1)S(1)} convert(f32[2,2,32,384]{3,2,1,0:T(8,128)} %param.14) | non-fusion elementwise | flops 49152 | bytes 294912 | tf_op jit(solution)/shard_map/convert_element_type | solution.py:210
  1.0 0.0 copy-start.7
  1.0 0.0 copy-start.8
  1.0 0.0 copy-start.9
  1.0 5.1 %collective-permute-start = (bf16[2,2,32,384]{3,2,1,0:T(8,128)(2,1)S(1)}, bf16[2,2,32,384]{3,2,1,0:T(8,128)(2,1)S(1)}, u32[]{:S(2)}, u32[]{:S(2)}) collective-permute-start(bf16[2,2,32,384]{3,2,1,0:T(8,128)(2,1)S(1)} %convert_element_type.75), channel_id=1, source_target_pairs={{0,1},{1,2},{2,3},{3,4},{4,5},{5,6},{6,7},{7,8},{8,9},{9,10},{10,1... | collective-permute-start | bytes 294920 | tf_op jit(solution)/shard_map/ppermute | solution.py:20
  6.1 1.9 %collective-permute-start.1 = (bf16[2,2,32,384]{3,2,1,0:T(8,128)(2,1)S(1)}, bf16[2,2,32,384]{3,2,1,0:T(8,128)(2,1)S(1)}, u32[]{:S(2)}, u32[]{:S(2)}) collective-permute-start(bf16[2,2,32,384]{3,2,1,0:T(8,128)(2,1)S(1)} %convert_element_type.75), channel_id=1, source_target_pairs={{1,0},{2,1},{3,2},{4,3},{5,4},{6,5},{7,6},{8,7},{9,8},{10,9},{11,1... | collective-permute-start | bytes 294920 | tf_op jit(solution)/shard_map/ppermute | solution.py:21
  8.0 1.1 %copy.60 = f32[2,2,32,384]{3,1,0,2:T(2,128)S(1)} copy(f32[2,2,32,384]{3,2,1,0:T(8,128)} %param.14) | data formatting | bytes 393216 | tf_op args[0]
  9.1 1.1 %broadcast_in_dim.2 = f32[2,2,32,4,384]{4,1,0,3,2:T(2,128)} broadcast(f32[2,2,32,384]{3,1,0,2:T(2,128)S(1)} %copy.60), dimensions={0,1,2,4} | broadcast | bytes 983040 | tf_op jit(solution)/shard_map/broadcast_in_dim | solution.py:213
  10.3 10.9 %all-to-all-start = ((f32[2,2,128,384]{3,1,0,2:T(2,128)}), f32[2,2,128,384]{3,1,0,2:T(2,128)S(1)}, u32[]{:S(2)}, u32[]{:S(2)}) async-start(f32[2,2,128,384]{3,1,0,2:T(2,128)} %bitcast.8), calls=%async_computation | async-start | bytes 1572864 | tf_op jit(solution)/shard_map/all_to_all | solution.py:215
  21.3 0.1 copy.52
  21.5 0.1 copy.54
  21.6 0.1 copy.56
  21.8 0.1 copy.57
  21.9 0.1 copy.58
  22.1 0.1 copy.59
  22.3 0.8 %pad_maximum_fusion.1.p_ref = f32[152,768]{1,0:T(8,128)} fusion(f32[24,768]{1,0:T(8,128)S(1)} %pad_convert_fusion, f32[128,768]{1,0:T(8,128)S(1)} %pad_dynamic-update-slice_fusion), kind=kLoop, calls=%fused_computation.12 | loop fusion | flops 116736 | bytes 933888 | tf_op jit(solution)/shard_map/concatenate | solution.py:169
  23.1 0.0 collective-permute-done
  23.1 0.0 collective-permute-done.1
  23.2 1.1 %pad_slice_fusion.10 = (bf16[2,10,34,384]{3,2,1,0:T(8,128)(2,1)S(1)}, bf16[2,10,34,384]{3,2,1,0:T(8,128)(2,1)S(1)}, bf16[2,10,34,384]{3,2,1,0:T(8,128)(2,1)S(1)}) fusion(bf16[2,10,32,384]{3,2,1,0:T(8,128)(2,1)S(1)} %constant_dynamic-update-slice_fusion), kind=kLoop, calls=%fused_computation.11 | loop fusion | bytes 2058240 | tf_op jit(solution)/shard_map/slice | solution.py:153
  24.3 1.6 %pad_maximum_fusion.x_ref = bf16[2,30,34,384]{3,2,1,0:T(8,128)(2,1)} fusion(bf16[2,10,34,384]{3,2,1,0:T(8,128)(2,1)S(1)} %get-tuple-element.13, bf16[2,10,34,384]{3,2,1,0:T(8,128)(2,1)S(1)} %get-tuple-element.12, bf16[2,10,34,384]{3,2,1,0:T(8,128)(2,1)S(1)} %get-tuple-element.11), kind=kLoop, calls=%fused_computation.8 | loop fusion | flops 1566720 | bytes 3133440 | tf_op jit(solution)/shard_map/concatenate | solution.py:152
  25.8 12.0 %all-to-all-done = f32[2,2,128,384]{3,1,0,2:T(2,128)S(1)} async-done(((f32[2,2,128,384]{3,1,0,2:T(2,128)}), f32[2,2,128,384]{3,1,0,2:T(2,128)S(1)}, u32[]{:S(2)}, u32[]{:S(2)}) %all-to-all-start) | async-done | bytes 786464 | tf_op jit(solution)/shard_map/all_to_all | solution.py:215
  37.9 1.2 %copy.61 = f32[256,2,1,384]{0,3,2,1:T(8,128)} copy(f32[256,2,1,384]{3,1,0,2:T(2,128)S(1)} %bitcast.24) | data formatting | bytes 1572864 | tf_op jit(solution)/shard_map/optimization_barrier | solution.py:170
  39.1 13.8 %shard_map.137 = f32[2,1,384,256]{3,2,1,0:T(8,128)} custom-call(f32[2,1,384,256]{3,2,1,0:T(8,128)} %bitcast.26, bf16[4,2,1,384,256]{4,3,2,1,0:T(8,128)(2,1)} %sens_ref.1, bf16[4,2,1,384,256]{4,3,2,1,0:T(8,128)(2,1)} %meas_ref.1, s32[384,256]{1,0:T(8,128)} %mask_ref.1, bf16[768,384]{1,0:T(8,128)(2,1)} %constant.13.clone.ty_ref, ...), custom_call_target="tpu_custom_call" | custom-call | tf_op jit(solution)/shard_map/pallas_call | solution.py:97
  52.9 1.2 %convert_bitcast_fusion = bf16[256,2,1,384]{0,3,2,1:T(8,128)(2,1)S(1)} fusion(f32[2,1,384,256]{3,2,1,0:T(8,128)} %shard_map.137), kind=kLoop, calls=%fused_computation.13 | loop fusion | flops 196608 | bytes 1179648 | tf_op jit(solution)/shard_map/convert_element_type | solution.py:221
  54.1 1.1 %copy.62 = bf16[256,2,1,384]{3,1,2,0:T(2,128)(2,1)} copy(bf16[256,2,1,384]{0,3,2,1:T(8,128)(2,1)S(1)} %convert_bitcast_fusion) | data formatting | bytes 786432 | tf_op jit(solution)/shard_map/convert_element_type | solution.py:221
  55.2 3.7 %all-to-all-start.1 = ((bf16[256,2,1,384]{3,1,2,0:T(2,128)(2,1)}), bf16[256,2,1,384]{3,1,2,0:T(2,128)(2,1)S(1)}, u32[]{:S(2)}, u32[]{:S(2)}) async-start(bf16[256,2,1,384]{3,1,2,0:T(2,128)(2,1)} %copy.62), calls=%async_computation.1 | async-start | bytes 786432 | tf_op jit(solution)/shard_map/all_to_all | solution.py:222
  58.9 16.4 %shard_map.136 = f32[2,18,32,384]{3,2,1,0:T(8,128)} custom-call(bf16[2,30,34,384]{3,2,1,0:T(8,128)(2,1)} %pad_maximum_fusion.x_ref, f32[152,768]{1,0:T(8,128)} %pad_maximum_fusion.1.p_ref), custom_call_target="tpu_custom_call" | custom-call | tf_op jit(solution)/shard_map/pallas_call | solution.py:171
  75.4 0.0 all-to-all-done.1
  75.4 0.3 convert.20
  75.7 0.5 reduce_sum.9
  76.2 0.7 copy-done
  76.9 1.1 %add_add_fusion = f32[2,2,32,384]{3,2,1,0:T(8,128)} fusion(f32[2,2,32,384]{3,2,1,0:T(8,128)S(1)} %copy-done.2, f32[2,2,32,384]{3,2,1,0:T(8,128)S(1)} %copy-done.1, f32[2,2,32,384]{3,1,0,2:T(2,128)S(1)} %reduce_sum.9, f32[2,18,32,384]{3,2,1,0:T(8,128)S(1)} %copy-done), kind=kLoop, calls=%fused_computation.23 | loop fusion | flops 589824 | bytes 2752512 | tf_op jit(solution)/shard_map/add | solution.py:225
  (37 shorter events, 0.3 us)
Async XLA Ops:
  0.0 21.2 %copy-start.6 = (bf16[3,3,2,128]{3,2,1,0:T(2,128)(2,1)S(1)}, bf16[3,3,2,128]{3,2,1,0:T(2,128)(2,1)}, u32[]{:S(2)}) copy-start(bf16[3,3,2,128]{3,2,1,0:T(2,128)(2,1)} %param.25) | copy-start | bytes 13828
  0.0 21.3 %copy-start.5 = (bf16[3,3,10,128]{3,1,2,0:T(4,128)(2,1)S(1)}, bf16[3,3,10,128]{3,1,2,0:T(4,128)(2,1)}, u32[]{:S(2)}) copy-start(bf16[3,3,10,128]{3,1,2,0:T(4,128)(2,1)} %param.19) | copy-start | bytes 69124
  0.0 21.8 %copy-start.3 = (bf16[128,128]{1,0:T(8,128)(2,1)S(1)}, bf16[128,128]{1,0:T(8,128)(2,1)}, u32[]{:S(2)}) copy-start(bf16[128,128]{1,0:T(8,128)(2,1)} %param.21) | copy-start | bytes 98308
  0.0 21.9 %copy-start.4 = (bf16[128,128]{1,0:T(8,128)(2,1)S(1)}, bf16[128,128]{1,0:T(8,128)(2,1)}, u32[]{:S(2)}) copy-start(bf16[128,128]{1,0:T(8,128)(2,1)} %param.23) | copy-start | bytes 98308
  1.0 21.0 %copy-start.7 = (f32[128]{0:T(128)S(1)}, f32[128]{0:T(128)}, u32[]{:S(2)}) copy-start(f32[128]{0:T(128)} %param.24) | copy-start | bytes 1540
  1.0 21.0 %copy-start.8 = (f32[128]{0:T(128)S(1)}, f32[128]{0:T(128)}, u32[]{:S(2)}) copy-start(f32[128]{0:T(128)} %param.22) | copy-start | bytes 1540
  1.0 21.0 %copy-start.9 = (f32[128]{0:T(128)S(1)}, f32[128]{0:T(128)}, u32[]{:S(2)}) copy-start(f32[128]{0:T(128)} %param.20) | copy-start | bytes 1540
  1.0 22.0 %collective-permute-start = (bf16[2,2,32,384]{3,2,1,0:T(8,128)(2,1)S(1)}, bf16[2,2,32,384]{3,2,1,0:T(8,128)(2,1)S(1)}, u32[]{:S(2)}, u32[]{:S(2)}) collective-permute-start(bf16[2,2,32,384]{3,2,1,0:T(8,128)(2,1)S(1)} %convert_element_type.75), channel_id=1, source_target_pairs={{0,1},{1,2},{2,3},{3,4},{4,5},{5,6},{6,7},{7,8},{8,9},{9,10},{10,1... | collective-permute-start | bytes 294920 | tf_op jit(solution)/shard_map/ppermute | solution.py:20
  6.1 17.0 %collective-permute-start.1 = (bf16[2,2,32,384]{3,2,1,0:T(8,128)(2,1)S(1)}, bf16[2,2,32,384]{3,2,1,0:T(8,128)(2,1)S(1)}, u32[]{:S(2)}, u32[]{:S(2)}) collective-permute-start(bf16[2,2,32,384]{3,2,1,0:T(8,128)(2,1)S(1)} %convert_element_type.75), channel_id=1, source_target_pairs={{1,0},{2,1},{3,2},{4,3},{5,4},{6,5},{7,6},{8,7},{9,8},{10,9},{11,1... | collective-permute-start | bytes 294920 | tf_op jit(solution)/shard_map/ppermute | solution.py:21
  10.3 12.8 %copy-start.1 = (f32[2,2,32,384]{3,2,1,0:T(8,128)S(1)}, f32[2,2,32,384]{3,2,1,0:T(8,128)}, u32[]{:S(2)}) copy-start(f32[2,2,32,384]{3,2,1,0:T(8,128)} %param.14) | copy-start | bytes 589828
  10.3 27.6 %all-to-all-start = ((f32[2,2,128,384]{3,1,0,2:T(2,128)}), f32[2,2,128,384]{3,1,0,2:T(2,128)S(1)}, u32[]{:S(2)}, u32[]{:S(2)}) async-start(f32[2,2,128,384]{3,1,0,2:T(2,128)} %bitcast.8), calls=%async_computation | async-start | bytes 1572864 | tf_op jit(solution)/shard_map/all_to_all | solution.py:215
  55.2 20.2 %all-to-all-start.1 = ((bf16[256,2,1,384]{3,1,2,0:T(2,128)(2,1)}), bf16[256,2,1,384]{3,1,2,0:T(2,128)(2,1)S(1)}, u32[]{:S(2)}, u32[]{:S(2)}) async-start(bf16[256,2,1,384]{3,1,2,0:T(2,128)(2,1)} %copy.62), calls=%async_computation.1 | async-start | bytes 786432 | tf_op jit(solution)/shard_map/all_to_all | solution.py:222
  75.4 1.5 %copy-start = (f32[2,18,32,384]{3,2,1,0:T(8,128)S(1)}, f32[2,18,32,384]{3,2,1,0:T(8,128)}, u32[]{:S(2)}) copy-start(f32[2,18,32,384]{3,2,1,0:T(8,128)} %shard_map.136) | copy-start | bytes 5308420
  75.4 1.5 %copy-start.2 = (f32[2,2,32,384]{3,2,1,0:T(8,128)S(1)}, f32[2,2,32,384]{3,2,1,0:T(8,128)}, u32[]{:S(2)}) copy-start(f32[2,2,32,384]{3,2,1,0:T(8,128)} %param.15) | copy-start | bytes 589828

commit v17 on v16

--- a/solution.py
+++ b/solution.py
@@ -51,13 +51,13 @@
     return (last_real, last_imag)
 
 
-def adjoint_kernel(planes_ref, sens_ref, meas_ref, mask_ref, ty_ref, tz_ref, out_ref):
+def adjoint_kernel(planes_ref, sens_ref, meas_ref, mask_ref, ty_ref, tz_ref, out_ref, acc_ref):
     ny = planes_ref.shape[1]
     nz = planes_ref.shape[2]
 
     @pl.when(pl.program_id(0) == 0)
     def _():
-        out_ref[...] = jnp.zeros_like(out_ref)
+        acc_ref[...] = jnp.zeros_like(acc_ref)
 
     ty = ty_ref[...]
     tz = tz_ref[...]
@@ -82,8 +82,12 @@
     full = jnp.dot(jnp.concatenate([back_real, back_imag], axis=0), tz, preferred_element_type=jnp.float32)
     grad_real = full[:ny, :nz] - full[ny:, nz:]
     grad_imag = full[ny:, :nz] + full[:ny, nz:]
-    out_ref[0] += sens_real * grad_real + sens_imag * grad_imag
-    out_ref[1] += sens_real * grad_imag - sens_imag * grad_real
+    acc_ref[0] += sens_real * grad_real + sens_imag * grad_imag
+    acc_ref[1] += sens_real * grad_imag - sens_imag * grad_real
+
+    @pl.when(pl.program_id(0) == pl.num_programs(0) - 1)
+    def _():
+        out_ref[...] = acc_ref[...].astype(out_ref.dtype)
 
 
 def coil_adjoint(planes, sens, measured, mask):
@@ -106,7 +110,8 @@
             pl.BlockSpec((nz, 2 * nz), lambda c: (0, 0)),
         ],
         out_specs=pl.BlockSpec((2, None, ny, nz), lambda c: (0, 0, 0, 0)),
-        out_shape=jax.ShapeDtypeStruct(planes.shape, jnp.float32),
+        out_shape=jax.ShapeDtypeStruct(planes.shape, jnp.bfloat16),
+        scratch_shapes=[pltpu.VMEM((2, ny, nz), jnp.float32)],
     )(planes, sens, measured, mask, ty, tz)
 
 
@@ -218,7 +223,7 @@
     )
     planes = jnp.transpose(planes_in, (1, 2, 3, 0))
     partial_sum = coil_adjoint(planes, sens, measured, mask)
-    by_depth = jnp.transpose(partial_sum, (3, 0, 1, 2)).astype(jnp.bfloat16)
+    by_depth = jnp.transpose(partial_sum, (3, 0, 1, 2))
     by_device = lax.all_to_all(by_depth, ("slab", "coil"), split_axis=0, concat_axis=2, tiled=True)
     by_device = by_device.astype(jnp.float32).reshape(depth, parts, rows, groups, lines)
     gradient = jnp.sum(by_device, axis=3)

time: 78.3 us -> 77.9 us (level)
  other arithmetic: 6.47 us -> 5.3 us
  local copies, waits for them, and re-layouts: 7.19 us -> 8.02 us
    transpose x0 -> x1, local copies, waits for them, and re-layouts: none -> 1.94 us  [on_device(): by_depth = jnp.transpose(partial_sum, (3, 0, 1, 2))]
    convert_element_type x1 -> x0, other arithmetic: 1.17 us -> none  [on_device(): by_depth = jnp.transpose(partial_sum, (3, 0, 1, 2)).astype(jnp.bfloat16)]
    convert_element_type x1 -> x0, local copies, waits for them, and re-layouts: 1.11 us -> none  [on_device(): by_depth = jnp.transpose(partial_sum, (3, 0, 1, 2)).astype(jnp.bfloat16)]
  transfers between devices with their start and end apart: 4 -> 4, of which waited for: 1 -> 1; matrix products, arithmetic and copies ran while one was open for 8% -> 9% of each run, Pallas kernels for 21% -> 21%
where the time goes in v17:
time: 77.9 us; the launch traced here: 77.5 us
  Pallas kernels  30.2 us (39%)
  starting transfers between devices  21.6 us (28%)
  waiting for transfers between devices  12 us (15%)
  local copies, waits for them, and re-layouts  8.02 us (10%)
  other arithmetic  5.3 us (7%)
    pallas_call x1, Pallas kernels, score_net(): pl.pallas_call(net_kernel, grid=(slice_count,), in_specs=[pl.BlockSpec((1...  16.4 us
    pallas_call x1, Pallas kernels, coil_adjoint(): pl.pallas_call(adjoint_kernel, grid=(coils,), in_specs=[pl.BlockSpec((2,...  13.8 us
    all_to_all x1, waiting for transfers between devices, on_device(): lax.all_to_all(copies, ('slab', 'coil'), split_axis=2, concat_axis=0, til...  12 us
    all_to_all x1, starting transfers between devices, on_device(): lax.all_to_all(copies, ('slab', 'coil'), split_axis=2, concat_axis=0, til...  10.9 us
    ppermute x1, starting transfers between devices, with_halo(): before = lax.ppermute(last, axis, up)  5.07 us
    all_to_all x1, starting transfers between devices, on_device(): lax.all_to_all(by_depth, ('slab', 'coil'), split_axis=0, concat_axis=2, t...  3.72 us
    unnamed x24, local copies, waits for them, and re-layouts  2.05 us
    transpose x1, local copies, waits for them, and re-layouts, on_device(): by_depth = jnp.transpose(partial_sum, (3, 0, 1, 2))  1.94 us
  transfers between devices with their start and end apart: 4, of which 1 were waited for; matrix products, arithmetic and copies ran while one was open for 9% of the time, Pallas kernels for 21%

profile of v17, /device:TPU:1, one launch (start us, length us, event | category | flops | bytes accessed | tf_op | source)
XLA Modules:
  0.0 77.5 jit_solution(12699371500812623510)
XLA Ops:
  0.0 0.0 copy-start.4
  0.0 1.0 %convert_element_type.69 = bf16[2,2,32,384]{3,2,1,0:T(8,128)(2,1)S(1)} convert(f32[2,2,32,384]{3,2,1,0:T(8,128)} %param.14) | non-fusion elementwise | flops 49152 | bytes 294912 | tf_op jit(solution)/shard_map/convert_element_type | solution.py:215
  1.0 0.0 copy-start.7
  1.0 0.0 copy-start.8
  1.0 0.0 copy-start.9
  1.0 5.1 %collective-permute-start = (bf16[2,2,32,384]{3,2,1,0:T(8,128)(2,1)S(1)}, bf16[2,2,32,384]{3,2,1,0:T(8,128)(2,1)S(1)}, u32[]{:S(2)}, u32[]{:S(2)}) collective-permute-start(bf16[2,2,32,384]{3,2,1,0:T(8,128)(2,1)S(1)} %convert_element_type.69), channel_id=1, source_target_pairs={{0,1},{1,2},{2,3},{3,4},{4,5},{5,6},{6,7},{7,8},{8,9},{9,10},{10,1... | collective-permute-start | bytes 294920 | tf_op jit(solution)/shard_map/ppermute | solution.py:20
  6.1 1.9 %collective-permute-start.1 = (bf16[2,2,32,384]{3,2,1,0:T(8,128)(2,1)S(1)}, bf16[2,2,32,384]{3,2,1,0:T(8,128)(2,1)S(1)}, u32[]{:S(2)}, u32[]{:S(2)}) collective-permute-start(bf16[2,2,32,384]{3,2,1,0:T(8,128)(2,1)S(1)} %convert_element_type.69), channel_id=1, source_target_pairs={{1,0},{2,1},{3,2},{4,3},{5,4},{6,5},{7,6},{8,7},{9,8},{10,9},{11,1... | collective-permute-start | bytes 294920 | tf_op jit(solution)/shard_map/ppermute | solution.py:21
  8.0 1.1 %copy.60 = f32[2,2,32,384]{3,1,0,2:T(2,128)S(1)} copy(f32[2,2,32,384]{3,2,1,0:T(8,128)} %param.14) | data formatting | bytes 393216 | tf_op args[0]
  9.1 1.1 %broadcast_in_dim.2 = f32[2,2,32,4,384]{4,1,0,3,2:T(2,128)} broadcast(f32[2,2,32,384]{3,1,0,2:T(2,128)S(1)} %copy.60), dimensions={0,1,2,4} | broadcast | bytes 983040 | tf_op jit(solution)/shard_map/broadcast_in_dim | solution.py:218
  10.3 10.9 %all-to-all-start = ((f32[2,2,128,384]{3,1,0,2:T(2,128)}), f32[2,2,128,384]{3,1,0,2:T(2,128)S(1)}, u32[]{:S(2)}, u32[]{:S(2)}) async-start(f32[2,2,128,384]{3,1,0,2:T(2,128)} %bitcast.8), calls=%async_computation | async-start | bytes 1572864 | tf_op jit(solution)/shard_map/all_to_all | solution.py:220
  21.3 0.1 copy.52
  21.5 0.1 copy.54
  21.6 0.1 copy.56
  21.8 0.1 copy.57
  21.9 0.1 copy.58
  22.1 0.1 copy.59
  22.3 0.8 %pad_maximum_fusion.1.p_ref = f32[152,768]{1,0:T(8,128)} fusion(f32[24,768]{1,0:T(8,128)S(1)} %pad_convert_fusion, f32[128,768]{1,0:T(8,128)S(1)} %pad_dynamic-update-slice_fusion), kind=kLoop, calls=%fused_computation.12 | loop fusion | flops 116736 | bytes 933888 | tf_op jit(solution)/shard_map/concatenate | solution.py:174
  23.1 0.0 collective-permute-done
  23.1 0.0 collective-permute-done.1
  23.2 1.1 %pad_slice_fusion.10 = (bf16[2,10,34,384]{3,2,1,0:T(8,128)(2,1)S(1)}, bf16[2,10,34,384]{3,2,1,0:T(8,128)(2,1)S(1)}, bf16[2,10,34,384]{3,2,1,0:T(8,128)(2,1)S(1)}) fusion(bf16[2,10,32,384]{3,2,1,0:T(8,128)(2,1)S(1)} %constant_dynamic-update-slice_fusion), kind=kLoop, calls=%fused_computation.11 | loop fusion | bytes 2058240 | tf_op jit(solution)/shard_map/slice | solution.py:158
  24.3 1.6 %pad_maximum_fusion.x_ref = bf16[2,30,34,384]{3,2,1,0:T(8,128)(2,1)} fusion(bf16[2,10,34,384]{3,2,1,0:T(8,128)(2,1)S(1)} %get-tuple-element.13, bf16[2,10,34,384]{3,2,1,0:T(8,128)(2,1)S(1)} %get-tuple-element.12, bf16[2,10,34,384]{3,2,1,0:T(8,128)(2,1)S(1)} %get-tuple-element.11), kind=kLoop, calls=%fused_computation.8 | loop fusion | flops 1566720 | bytes 3133440 | tf_op jit(solution)/shard_map/concatenate | solution.py:157
  25.8 12.0 %all-to-all-done = f32[2,2,128,384]{3,1,0,2:T(2,128)S(1)} async-done(((f32[2,2,128,384]{3,1,0,2:T(2,128)}), f32[2,2,128,384]{3,1,0,2:T(2,128)S(1)}, u32[]{:S(2)}, u32[]{:S(2)}) %all-to-all-start) | async-done | bytes 786464 | tf_op jit(solution)/shard_map/all_to_all | solution.py:220
  37.9 1.2 %copy.61 = f32[256,2,1,384]{0,3,2,1:T(8,128)} copy(f32[256,2,1,384]{3,1,0,2:T(2,128)S(1)} %bitcast.23) | data formatting | bytes 1572864 | tf_op jit(solution)/shard_map/optimization_barrier | solution.py:175
  39.1 13.8 %shard_map.137 = bf16[2,1,384,256]{3,2,1,0:T(8,128)(2,1)} custom-call(f32[2,1,384,256]{3,2,1,0:T(8,128)} %bitcast.25, bf16[4,2,1,384,256]{4,3,2,1,0:T(8,128)(2,1)} %sens_ref.1, bf16[4,2,1,384,256]{4,3,2,1,0:T(8,128)(2,1)} %meas_ref.1, s32[384,256]{1,0:T(8,128)} %mask_ref.1, bf16[768,384]{1,0:T(8,128)(2,1)} %constant.13.clone.ty_ref, ...), custom_call_target="tpu_custom_call" | custom-call | tf_op jit(solution)/shard_map/pallas_call | solution.py:101
  52.8 1.9 %copy.62 = bf16[256,2,1,384]{3,1,2,0:T(2,128)(2,1)} copy(bf16[256,2,1,384]{0,3,2,1:T(8,128)(2,1)} %bitcast.27) | data formatting | bytes 786432 | tf_op jit(solution)/shard_map/transpose | solution.py:226
  54.8 3.7 %all-to-all-start.1 = ((bf16[256,2,1,384]{3,1,2,0:T(2,128)(2,1)}), bf16[256,2,1,384]{3,1,2,0:T(2,128)(2,1)S(1)}, u32[]{:S(2)}, u32[]{:S(2)}) async-start(bf16[256,2,1,384]{3,1,2,0:T(2,128)(2,1)} %copy.62), calls=%async_computation.1 | async-start | bytes 786432 | tf_op jit(solution)/shard_map/all_to_all | solution.py:227
  58.5 16.4 %shard_map.136 = f32[2,18,32,384]{3,2,1,0:T(8,128)} custom-call(bf16[2,30,34,384]{3,2,1,0:T(8,128)(2,1)} %pad_maximum_fusion.x_ref, f32[152,768]{1,0:T(8,128)} %pad_maximum_fusion.1.p_ref), custom_call_target="tpu_custom_call" | custom-call | tf_op jit(solution)/shard_map/pallas_call | solution.py:176
  75.0 0.0 all-to-all-done.1
  75.0 0.3 convert.20
  75.2 0.5 reduce_sum.9
  75.7 0.7 copy-done
  76.4 1.1 %add_add_fusion = f32[2,2,32,384]{3,2,1,0:T(8,128)} fusion(f32[2,2,32,384]{3,2,1,0:T(8,128)S(1)} %copy-done.2, f32[2,2,32,384]{3,2,1,0:T(8,128)S(1)} %copy-done.1, f32[2,2,32,384]{3,1,0,2:T(2,128)S(1)} %reduce_sum.9, f32[2,18,32,384]{3,2,1,0:T(8,128)S(1)} %copy-done), kind=kLoop, calls=%fused_computation.22 | loop fusion | flops 589824 | bytes 2752512 | tf_op jit(solution)/shard_map/add | solution.py:230
  (36 shorter events, 0.3 us)
Async XLA Ops:
  0.0 21.2 %copy-start.6 = (bf16[3,3,2,128]{3,2,1,0:T(2,128)(2,1)S(1)}, bf16[3,3,2,128]{3,2,1,0:T(2,128)(2,1)}, u32[]{:S(2)}) copy-start(bf16[3,3,2,128]{3,2,1,0:T(2,128)(2,1)} %param.25) | copy-start | bytes 13828
  0.0 21.3 %copy-start.5 = (bf16[3,3,10,128]{3,1,2,0:T(4,128)(2,1)S(1)}, bf16[3,3,10,128]{3,1,2,0:T(4,128)(2,1)}, u32[]{:S(2)}) copy-start(bf16[3,3,10,128]{3,1,2,0:T(4,128)(2,1)} %param.19) | copy-start | bytes 69124
  0.0 21.8 %copy-start.3 = (bf16[128,128]{1,0:T(8,128)(2,1)S(1)}, bf16[128,128]{1,0:T(8,128)(2,1)}, u32[]{:S(2)}) copy-start(bf16[128,128]{1,0:T(8,128)(2,1)} %param.21) | copy-start | bytes 98308
  0.0 21.9 %copy-start.4 = (bf16[128,128]{1,0:T(8,128)(2,1)S(1)}, bf16[128,128]{1,0:T(8,128)(2,1)}, u32[]{:S(2)}) copy-start(bf16[128,128]{1,0:T(8,128)(2,1)} %param.23) | copy-start | bytes 98308
  1.0 21.0 %copy-start.7 = (f32[128]{0:T(128)S(1)}, f32[128]{0:T(128)}, u32[]{:S(2)}) copy-start(f32[128]{0:T(128)} %param.24) | copy-start | bytes 1540
  1.0 21.0 %copy-start.8 = (f32[128]{0:T(128)S(1)}, f32[128]{0:T(128)}, u32[]{:S(2)}) copy-start(f32[128]{0:T(128)} %param.22) | copy-start | bytes 1540
  1.0 21.0 %copy-start.9 = (f32[128]{0:T(128)S(1)}, f32[128]{0:T(128)}, u32[]{:S(2)}) copy-start(f32[128]{0:T(128)} %param.20) | copy-start | bytes 1540
  1.0 22.0 %collective-permute-start = (bf16[2,2,32,384]{3,2,1,0:T(8,128)(2,1)S(1)}, bf16[2,2,32,384]{3,2,1,0:T(8,128)(2,1)S(1)}, u32[]{:S(2)}, u32[]{:S(2)}) collective-permute-start(bf16[2,2,32,384]{3,2,1,0:T(8,128)(2,1)S(1)} %convert_element_type.69), channel_id=1, source_target_pairs={{0,1},{1,2},{2,3},{3,4},{4,5},{5,6},{6,7},{7,8},{8,9},{9,10},{10,1... | collective-permute-start | bytes 294920 | tf_op jit(solution)/shard_map/ppermute | solution.py:20
  6.1 17.0 %collective-permute-start.1 = (bf16[2,2,32,384]{3,2,1,0:T(8,128)(2,1)S(1)}, bf16[2,2,32,384]{3,2,1,0:T(8,128)(2,1)S(1)}, u32[]{:S(2)}, u32[]{:S(2)}) collective-permute-start(bf16[2,2,32,384]{3,2,1,0:T(8,128)(2,1)S(1)} %convert_element_type.69), channel_id=1, source_target_pairs={{1,0},{2,1},{3,2},{4,3},{5,4},{6,5},{7,6},{8,7},{9,8},{10,9},{11,1... | collective-permute-start | bytes 294920 | tf_op jit(solution)/shard_map/ppermute | solution.py:21
  10.3 12.8 %copy-start.1 = (f32[2,2,32,384]{3,2,1,0:T(8,128)S(1)}, f32[2,2,32,384]{3,2,1,0:T(8,128)}, u32[]{:S(2)}) copy-start(f32[2,2,32,384]{3,2,1,0:T(8,128)} %param.14) | copy-start | bytes 589828
  10.3 27.6 %all-to-all-start = ((f32[2,2,128,384]{3,1,0,2:T(2,128)}), f32[2,2,128,384]{3,1,0,2:T(2,128)S(1)}, u32[]{:S(2)}, u32[]{:S(2)}) async-start(f32[2,2,128,384]{3,1,0,2:T(2,128)} %bitcast.8), calls=%async_computation | async-start | bytes 1572864 | tf_op jit(solution)/shard_map/all_to_all | solution.py:220
  54.8 20.2 %all-to-all-start.1 = ((bf16[256,2,1,384]{3,1,2,0:T(2,128)(2,1)}), bf16[256,2,1,384]{3,1,2,0:T(2,128)(2,1)S(1)}, u32[]{:S(2)}, u32[]{:S(2)}) async-start(bf16[256,2,1,384]{3,1,2,0:T(2,128)(2,1)} %copy.62), calls=%async_computation.1 | async-start | bytes 786432 | tf_op jit(solution)/shard_map/all_to_all | solution.py:227
  75.0 1.5 %copy-start = (f32[2,18,32,384]{3,2,1,0:T(8,128)S(1)}, f32[2,18,32,384]{3,2,1,0:T(8,128)}, u32[]{:S(2)}) copy-start(f32[2,18,32,384]{3,2,1,0:T(8,128)} %shard_map.136) | copy-start | bytes 5308420
  75.0 1.5 %copy-start.2 = (f32[2,2,32,384]{3,2,1,0:T(8,128)S(1)}, f32[2,2,32,384]{3,2,1,0:T(8,128)}, u32[]{:S(2)}) copy-start(f32[2,2,32,384]{3,2,1,0:T(8,128)} %param.15) | copy-start | bytes 589828

commit v18 on v17

--- a/solution.py
+++ b/solution.py
@@ -121,7 +121,7 @@
     row_count = q_ref.shape[2]
     cols = q_ref.shape[3]
     outs = q_ref.shape[1]
-    rows = 16
+    rows = 8
     w1 = [p_ref[:width, a * width : a * width + taps_in].astype(jnp.bfloat16) for a in range(3)]
     w2 = p_ref[:width, 3 * width : 4 * width].astype(jnp.bfloat16)
     w3 = p_ref[:width, 4 * width : 5 * width].astype(jnp.bfloat16)

time: 77.9 us -> 76.6 us (0.983)
  Pallas kernels: 30.2 us -> 29 us
    pallas_call x1, Pallas kernels: 16.4 us -> 15.2 us  [score_net(): pl.pallas_call(net_kernel, grid=(slice_count,), in_specs=[pl.BlockSpec((1...]
  transfers between devices with their start and end apart: 4 -> 4, of which waited for: 1 -> 1; matrix products, arithmetic and copies ran while one was open for 9% -> 9% of each run, Pallas kernels for 21% -> 20%
where the time goes in v18:
time: 76.6 us; the launch traced here: 76.3 us
  Pallas kernels  29 us (38%)
  starting transfers between devices  21.6 us (28%)
  waiting for transfers between devices  12 us (16%)
  local copies, waits for them, and re-layouts  8.02 us (10%)
  other arithmetic  5.3 us (7%)
    pallas_call x1, Pallas kernels, score_net(): pl.pallas_call(net_kernel, grid=(slice_count,), in_specs=[pl.BlockSpec((1...  15.2 us
    pallas_call x1, Pallas kernels, coil_adjoint(): pl.pallas_call(adjoint_kernel, grid=(coils,), in_specs=[pl.BlockSpec((2,...  13.8 us
    all_to_all x1, waiting for transfers between devices, on_device(): lax.all_to_all(copies, ('slab', 'coil'), split_axis=2, concat_axis=0, til...  12 us
    all_to_all x1, starting transfers between devices, on_device(): lax.all_to_all(copies, ('slab', 'coil'), split_axis=2, concat_axis=0, til...  10.9 us
    ppermute x1, starting transfers between devices, with_halo(): before = lax.ppermute(last, axis, up)  5.07 us
    all_to_all x1, starting transfers between devices, on_device(): lax.all_to_all(by_depth, ('slab', 'coil'), split_axis=0, concat_axis=2, t...  3.72 us
    unnamed x24, local copies, waits for them, and re-layouts  2.05 us
    transpose x1, local copies, waits for them, and re-layouts, on_device(): by_depth = jnp.transpose(partial_sum, (3, 0, 1, 2))  1.94 us
  transfers between devices with their start and end apart: 4, of which 1 were waited for; matrix products, arithmetic and copies ran while one was open for 9% of the time, Pallas kernels for 20%

profile of v18, /device:TPU:1, one launch (start us, length us, event | category | flops | bytes accessed | tf_op | source)
XLA Modules:
  0.0 76.3 jit_solution(11613602005172243137)
XLA Ops:
  0.0 0.0 copy-start.4
  0.0 1.0 %convert_element_type.69 = bf16[2,2,32,384]{3,2,1,0:T(8,128)(2,1)S(1)} convert(f32[2,2,32,384]{3,2,1,0:T(8,128)} %param.14) | non-fusion elementwise | flops 49152 | bytes 294912 | tf_op jit(solution)/shard_map/convert_element_type | solution.py:215
  1.0 0.0 copy-start.7
  1.0 0.0 copy-start.8
  1.0 0.0 copy-start.9
  1.0 5.1 %collective-permute-start = (bf16[2,2,32,384]{3,2,1,0:T(8,128)(2,1)S(1)}, bf16[2,2,32,384]{3,2,1,0:T(8,128)(2,1)S(1)}, u32[]{:S(2)}, u32[]{:S(2)}) collective-permute-start(bf16[2,2,32,384]{3,2,1,0:T(8,128)(2,1)S(1)} %convert_element_type.69), channel_id=1, source_target_pairs={{0,1},{1,2},{2,3},{3,4},{4,5},{5,6},{6,7},{7,8},{8,9},{9,10},{10,1... | collective-permute-start | bytes 294920 | tf_op jit(solution)/shard_map/ppermute | solution.py:20
  6.1 1.9 %collective-permute-start.1 = (bf16[2,2,32,384]{3,2,1,0:T(8,128)(2,1)S(1)}, bf16[2,2,32,384]{3,2,1,0:T(8,128)(2,1)S(1)}, u32[]{:S(2)}, u32[]{:S(2)}) collective-permute-start(bf16[2,2,32,384]{3,2,1,0:T(8,128)(2,1)S(1)} %convert_element_type.69), channel_id=1, source_target_pairs={{1,0},{2,1},{3,2},{4,3},{5,4},{6,5},{7,6},{8,7},{9,8},{10,9},{11,1... | collective-permute-start | bytes 294920 | tf_op jit(solution)/shard_map/ppermute | solution.py:21
  8.0 1.1 %copy.60 = f32[2,2,32,384]{3,1,0,2:T(2,128)S(1)} copy(f32[2,2,32,384]{3,2,1,0:T(8,128)} %param.14) | data formatting | bytes 393216 | tf_op args[0]
  9.1 1.1 %broadcast_in_dim.2 = f32[2,2,32,4,384]{4,1,0,3,2:T(2,128)} broadcast(f32[2,2,32,384]{3,1,0,2:T(2,128)S(1)} %copy.60), dimensions={0,1,2,4} | broadcast | bytes 983040 | tf_op jit(solution)/shard_map/broadcast_in_dim | solution.py:218
  10.3 10.9 %all-to-all-start = ((f32[2,2,128,384]{3,1,0,2:T(2,128)}), f32[2,2,128,384]{3,1,0,2:T(2,128)S(1)}, u32[]{:S(2)}, u32[]{:S(2)}) async-start(f32[2,2,128,384]{3,1,0,2:T(2,128)} %bitcast.8), calls=%async_computation | async-start | bytes 1572864 | tf_op jit(solution)/shard_map/all_to_all | solution.py:220
  21.3 0.1 copy.52
  21.5 0.1 copy.54
  21.6 0.1 copy.56
  21.8 0.1 copy.57
  21.9 0.1 copy.58
  22.1 0.1 copy.59
  22.3 0.8 %pad_maximum_fusion.1.p_ref = f32[152,768]{1,0:T(8,128)} fusion(f32[24,768]{1,0:T(8,128)S(1)} %pad_convert_fusion, f32[128,768]{1,0:T(8,128)S(1)} %pad_dynamic-update-slice_fusion), kind=kLoop, calls=%fused_computation.12 | loop fusion | flops 116736 | bytes 933888 | tf_op jit(solution)/shard_map/concatenate | solution.py:174
  23.1 0.0 collective-permute-done
  23.1 0.0 collective-permute-done.1
  23.2 1.1 %pad_slice_fusion.10 = (bf16[2,10,34,384]{3,2,1,0:T(8,128)(2,1)S(1)}, bf16[2,10,34,384]{3,2,1,0:T(8,128)(2,1)S(1)}, bf16[2,10,34,384]{3,2,1,0:T(8,128)(2,1)S(1)}) fusion(bf16[2,10,32,384]{3,2,1,0:T(8,128)(2,1)S(1)} %constant_dynamic-update-slice_fusion), kind=kLoop, calls=%fused_computation.11 | loop fusion | bytes 2058240 | tf_op jit(solution)/shard_map/slice | solution.py:158
  24.3 1.6 %pad_maximum_fusion.x_ref = bf16[2,30,34,384]{3,2,1,0:T(8,128)(2,1)} fusion(bf16[2,10,34,384]{3,2,1,0:T(8,128)(2,1)S(1)} %get-tuple-element.13, bf16[2,10,34,384]{3,2,1,0:T(8,128)(2,1)S(1)} %get-tuple-element.12, bf16[2,10,34,384]{3,2,1,0:T(8,128)(2,1)S(1)} %get-tuple-element.11), kind=kLoop, calls=%fused_computation.8 | loop fusion | flops 1566720 | bytes 3133440 | tf_op jit(solution)/shard_map/concatenate | solution.py:157
  25.8 12.0 %all-to-all-done = f32[2,2,128,384]{3,1,0,2:T(2,128)S(1)} async-done(((f32[2,2,128,384]{3,1,0,2:T(2,128)}), f32[2,2,128,384]{3,1,0,2:T(2,128)S(1)}, u32[]{:S(2)}, u32[]{:S(2)}) %all-to-all-start) | async-done | bytes 786464 | tf_op jit(solution)/shard_map/all_to_all | solution.py:220
  37.9 1.2 %copy.61 = f32[256,2,1,384]{0,3,2,1:T(8,128)} copy(f32[256,2,1,384]{3,1,0,2:T(2,128)S(1)} %bitcast.23) | data formatting | bytes 1572864 | tf_op jit(solution)/shard_map/optimization_barrier | solution.py:175
  39.1 13.8 %shard_map.137 = bf16[2,1,384,256]{3,2,1,0:T(8,128)(2,1)} custom-call(f32[2,1,384,256]{3,2,1,0:T(8,128)} %bitcast.25, bf16[4,2,1,384,256]{4,3,2,1,0:T(8,128)(2,1)} %sens_ref.1, bf16[4,2,1,384,256]{4,3,2,1,0:T(8,128)(2,1)} %meas_ref.1, s32[384,256]{1,0:T(8,128)} %mask_ref.1, bf16[768,384]{1,0:T(8,128)(2,1)} %constant.13.clone.ty_ref, ...), custom_call_target="tpu_custom_call" | custom-call | tf_op jit(solution)/shard_map/pallas_call | solution.py:101
  52.8 1.9 %copy.62 = bf16[256,2,1,384]{3,1,2,0:T(2,128)(2,1)} copy(bf16[256,2,1,384]{0,3,2,1:T(8,128)(2,1)} %bitcast.27) | data formatting | bytes 786432 | tf_op jit(solution)/shard_map/transpose | solution.py:226
  54.8 3.7 %all-to-all-start.1 = ((bf16[256,2,1,384]{3,1,2,0:T(2,128)(2,1)}), bf16[256,2,1,384]{3,1,2,0:T(2,128)(2,1)S(1)}, u32[]{:S(2)}, u32[]{:S(2)}) async-start(bf16[256,2,1,384]{3,1,2,0:T(2,128)(2,1)} %copy.62), calls=%async_computation.1 | async-start | bytes 786432 | tf_op jit(solution)/shard_map/all_to_all | solution.py:227
  58.5 15.2 %shard_map.136 = f32[2,18,32,384]{3,2,1,0:T(8,128)} custom-call(bf16[2,30,34,384]{3,2,1,0:T(8,128)(2,1)} %pad_maximum_fusion.x_ref, f32[152,768]{1,0:T(8,128)} %pad_maximum_fusion.1.p_ref), custom_call_target="tpu_custom_call" | custom-call | tf_op jit(solution)/shard_map/pallas_call | solution.py:176
  73.7 0.0 all-to-all-done.1
  73.7 0.3 convert.20
  74.0 0.5 reduce_sum.9
  74.5 0.7 copy-done
  75.2 1.1 %add_add_fusion = f32[2,2,32,384]{3,2,1,0:T(8,128)} fusion(f32[2,2,32,384]{3,2,1,0:T(8,128)S(1)} %copy-done.2, f32[2,2,32,384]{3,2,1,0:T(8,128)S(1)} %copy-done.1, f32[2,2,32,384]{3,1,0,2:T(2,128)S(1)} %reduce_sum.9, f32[2,18,32,384]{3,2,1,0:T(8,128)S(1)} %copy-done), kind=kLoop, calls=%fused_computation.22 | loop fusion | flops 589824 | bytes 2752512 | tf_op jit(solution)/shard_map/add | solution.py:230
  (36 shorter events, 0.3 us)
Async XLA Ops:
  0.0 21.2 %copy-start.6 = (bf16[3,3,2,128]{3,2,1,0:T(2,128)(2,1)S(1)}, bf16[3,3,2,128]{3,2,1,0:T(2,128)(2,1)}, u32[]{:S(2)}) copy-start(bf16[3,3,2,128]{3,2,1,0:T(2,128)(2,1)} %param.25) | copy-start | bytes 13828
  0.0 21.3 %copy-start.5 = (bf16[3,3,10,128]{3,1,2,0:T(4,128)(2,1)S(1)}, bf16[3,3,10,128]{3,1,2,0:T(4,128)(2,1)}, u32[]{:S(2)}) copy-start(bf16[3,3,10,128]{3,1,2,0:T(4,128)(2,1)} %param.19) | copy-start | bytes 69124
  0.0 21.8 %copy-start.3 = (bf16[128,128]{1,0:T(8,128)(2,1)S(1)}, bf16[128,128]{1,0:T(8,128)(2,1)}, u32[]{:S(2)}) copy-start(bf16[128,128]{1,0:T(8,128)(2,1)} %param.21) | copy-start | bytes 98308
  0.0 21.9 %copy-start.4 = (bf16[128,128]{1,0:T(8,128)(2,1)S(1)}, bf16[128,128]{1,0:T(8,128)(2,1)}, u32[]{:S(2)}) copy-start(bf16[128,128]{1,0:T(8,128)(2,1)} %param.23) | copy-start | bytes 98308
  1.0 21.0 %copy-start.7 = (f32[128]{0:T(128)S(1)}, f32[128]{0:T(128)}, u32[]{:S(2)}) copy-start(f32[128]{0:T(128)} %param.24) | copy-start | bytes 1540
  1.0 21.0 %copy-start.8 = (f32[128]{0:T(128)S(1)}, f32[128]{0:T(128)}, u32[]{:S(2)}) copy-start(f32[128]{0:T(128)} %param.22) | copy-start | bytes 1540
  1.0 21.0 %copy-start.9 = (f32[128]{0:T(128)S(1)}, f32[128]{0:T(128)}, u32[]{:S(2)}) copy-start(f32[128]{0:T(128)} %param.20) | copy-start | bytes 1540
  1.0 22.0 %collective-permute-start = (bf16[2,2,32,384]{3,2,1,0:T(8,128)(2,1)S(1)}, bf16[2,2,32,384]{3,2,1,0:T(8,128)(2,1)S(1)}, u32[]{:S(2)}, u32[]{:S(2)}) collective-permute-start(bf16[2,2,32,384]{3,2,1,0:T(8,128)(2,1)S(1)} %convert_element_type.69), channel_id=1, source_target_pairs={{0,1},{1,2},{2,3},{3,4},{4,5},{5,6},{6,7},{7,8},{8,9},{9,10},{10,1... | collective-permute-start | bytes 294920 | tf_op jit(solution)/shard_map/ppermute | solution.py:20
  6.1 17.0 %collective-permute-start.1 = (bf16[2,2,32,384]{3,2,1,0:T(8,128)(2,1)S(1)}, bf16[2,2,32,384]{3,2,1,0:T(8,128)(2,1)S(1)}, u32[]{:S(2)}, u32[]{:S(2)}) collective-permute-start(bf16[2,2,32,384]{3,2,1,0:T(8,128)(2,1)S(1)} %convert_element_type.69), channel_id=1, source_target_pairs={{1,0},{2,1},{3,2},{4,3},{5,4},{6,5},{7,6},{8,7},{9,8},{10,9},{11,1... | collective-permute-start | bytes 294920 | tf_op jit(solution)/shard_map/ppermute | solution.py:21
  10.3 12.8 %copy-start.1 = (f32[2,2,32,384]{3,2,1,0:T(8,128)S(1)}, f32[2,2,32,384]{3,2,1,0:T(8,128)}, u32[]{:S(2)}) copy-start(f32[2,2,32,384]{3,2,1,0:T(8,128)} %param.14) | copy-start | bytes 589828
  10.3 27.6 %all-to-all-start = ((f32[2,2,128,384]{3,1,0,2:T(2,128)}), f32[2,2,128,384]{3,1,0,2:T(2,128)S(1)}, u32[]{:S(2)}, u32[]{:S(2)}) async-start(f32[2,2,128,384]{3,1,0,2:T(2,128)} %bitcast.8), calls=%async_computation | async-start | bytes 1572864 | tf_op jit(solution)/shard_map/all_to_all | solution.py:220
  54.8 18.9 %all-to-all-start.1 = ((bf16[256,2,1,384]{3,1,2,0:T(2,128)(2,1)}), bf16[256,2,1,384]{3,1,2,0:T(2,128)(2,1)S(1)}, u32[]{:S(2)}, u32[]{:S(2)}) async-start(bf16[256,2,1,384]{3,1,2,0:T(2,128)(2,1)} %copy.62), calls=%async_computation.1 | async-start | bytes 786432 | tf_op jit(solution)/shard_map/all_to_all | solution.py:227
  73.7 1.5 %copy-start = (f32[2,18,32,384]{3,2,1,0:T(8,128)S(1)}, f32[2,18,32,384]{3,2,1,0:T(8,128)}, u32[]{:S(2)}) copy-start(f32[2,18,32,384]{3,2,1,0:T(8,128)} %shard_map.136) | copy-start | bytes 5308420
  73.7 1.5 %copy-start.2 = (f32[2,2,32,384]{3,2,1,0:T(8,128)S(1)}, f32[2,2,32,384]{3,2,1,0:T(8,128)}, u32[]{:S(2)}) copy-start(f32[2,2,32,384]{3,2,1,0:T(8,128)} %param.15) | copy-start | bytes 589828

commit v19 on v18

--- a/solution.py
+++ b/solution.py
@@ -121,7 +121,7 @@
     row_count = q_ref.shape[2]
     cols = q_ref.shape[3]
     outs = q_ref.shape[1]
-    rows = 8
+    rows = 4
     w1 = [p_ref[:width, a * width : a * width + taps_in].astype(jnp.bfloat16) for a in range(3)]
     w2 = p_ref[:width, 3 * width : 4 * width].astype(jnp.bfloat16)
     w3 = p_ref[:width, 4 * width : 5 * width].astype(jnp.bfloat16)

time: 76.6 us -> 80.7 us (1.054)
  Pallas kernels: 29 us -> 33 us
    pallas_call x1, Pallas kernels: 15.2 us -> 19.2 us  [score_net(): pl.pallas_call(net_kernel, grid=(slice_count,), in_specs=[pl.BlockSpec((1...]
  transfers between devices with their start and end apart: 4 -> 4, of which waited for: 1 -> 1; matrix products, arithmetic and copies ran while one was open for 9% -> 8% of each run, Pallas kernels for 20% -> 24%
where the time goes in v19:
time: 80.7 us; the launch traced here: 80.3 us
  Pallas kernels  33 us (41%)
  starting transfers between devices  21.6 us (27%)
  waiting for transfers between devices  12 us (15%)
  local copies, waits for them, and re-layouts  8.02 us (10%)
  other arithmetic  5.3 us (7%)
    pallas_call x1, Pallas kernels, score_net(): pl.pallas_call(net_kernel, grid=(slice_count,), in_specs=[pl.BlockSpec((1...  19.2 us
    pallas_call x1, Pallas kernels, coil_adjoint(): pl.pallas_call(adjoint_kernel, grid=(coils,), in_specs=[pl.BlockSpec((2,...  13.8 us
    all_to_all x1, waiting for transfers between devices, on_device(): lax.all_to_all(copies, ('slab', 'coil'), split_axis=2, concat_axis=0, til...  12 us
    all_to_all x1, starting transfers between devices, on_device(): lax.all_to_all(copies, ('slab', 'coil'), split_axis=2, concat_axis=0, til...  10.9 us
    ppermute x1, starting transfers between devices, with_halo(): before = lax.ppermute(last, axis, up)  5.07 us
    all_to_all x1, starting transfers between devices, on_device(): lax.all_to_all(by_depth, ('slab', 'coil'), split_axis=0, concat_axis=2, t...  3.72 us
    unnamed x24, local copies, waits for them, and re-layouts  2.05 us
    transpose x1, local copies, waits for them, and re-layouts, on_device(): by_depth = jnp.transpose(partial_sum, (3, 0, 1, 2))  1.94 us
  transfers between devices with their start and end apart: 4, of which 1 were waited for; matrix products, arithmetic and copies ran while one was open for 8% of the time, Pallas kernels for 24%

profile of v19, /device:TPU:1, one launch (start us, length us, event | category | flops | bytes accessed | tf_op | source)
XLA Modules:
  0.0 80.3 jit_solution(3622425602488256837)
XLA Ops:
  0.0 0.0 copy-start.4
  0.0 1.0 %convert_element_type.69 = bf16[2,2,32,384]{3,2,1,0:T(8,128)(2,1)S(1)} convert(f32[2,2,32,384]{3,2,1,0:T(8,128)} %param.14) | non-fusion elementwise | flops 49152 | bytes 294912 | tf_op jit(solution)/shard_map/convert_element_type | solution.py:215
  1.0 0.0 copy-start.7
  1.0 0.0 copy-start.8
  1.0 0.0 copy-start.9
  1.0 5.1 %collective-permute-start = (bf16[2,2,32,384]{3,2,1,0:T(8,128)(2,1)S(1)}, bf16[2,2,32,384]{3,2,1,0:T(8,128)(2,1)S(1)}, u32[]{:S(2)}, u32[]{:S(2)}) collective-permute-start(bf16[2,2,32,384]{3,2,1,0:T(8,128)(2,1)S(1)} %convert_element_type.69), channel_id=1, source_target_pairs={{0,1},{1,2},{2,3},{3,4},{4,5},{5,6},{6,7},{7,8},{8,9},{9,10},{10,1... | collective-permute-start | bytes 294920 | tf_op jit(solution)/shard_map/ppermute | solution.py:20
  6.1 1.9 %collective-permute-start.1 = (bf16[2,2,32,384]{3,2,1,0:T(8,128)(2,1)S(1)}, bf16[2,2,32,384]{3,2,1,0:T(8,128)(2,1)S(1)}, u32[]{:S(2)}, u32[]{:S(2)}) collective-permute-start(bf16[2,2,32,384]{3,2,1,0:T(8,128)(2,1)S(1)} %convert_element_type.69), channel_id=1, source_target_pairs={{1,0},{2,1},{3,2},{4,3},{5,4},{6,5},{7,6},{8,7},{9,8},{10,9},{11,1... | collective-permute-start | bytes 294920 | tf_op jit(solution)/shard_map/ppermute | solution.py:21
  8.0 1.1 %copy.60 = f32[2,2,32,384]{3,1,0,2:T(2,128)S(1)} copy(f32[2,2,32,384]{3,2,1,0:T(8,128)} %param.14) | data formatting | bytes 393216 | tf_op args[0]
  9.1 1.1 %broadcast_in_dim.2 = f32[2,2,32,4,384]{4,1,0,3,2:T(2,128)} broadcast(f32[2,2,32,384]{3,1,0,2:T(2,128)S(1)} %copy.60), dimensions={0,1,2,4} | broadcast | bytes 983040 | tf_op jit(solution)/shard_map/broadcast_in_dim | solution.py:218
  10.3 10.9 %all-to-all-start = ((f32[2,2,128,384]{3,1,0,2:T(2,128)}), f32[2,2,128,384]{3,1,0,2:T(2,128)S(1)}, u32[]{:S(2)}, u32[]{:S(2)}) async-start(f32[2,2,128,384]{3,1,0,2:T(2,128)} %bitcast.8), calls=%async_computation | async-start | bytes 1572864 | tf_op jit(solution)/shard_map/all_to_all | solution.py:220
  21.3 0.1 copy.52
  21.5 0.1 copy.54
  21.6 0.1 copy.56
  21.8 0.1 copy.57
  21.9 0.1 copy.58
  22.1 0.1 copy.59
  22.3 0.8 %pad_maximum_fusion.1.p_ref = f32[152,768]{1,0:T(8,128)} fusion(f32[24,768]{1,0:T(8,128)S(1)} %pad_convert_fusion, f32[128,768]{1,0:T(8,128)S(1)} %pad_dynamic-update-slice_fusion), kind=kLoop, calls=%fused_computation.12 | loop fusion | flops 116736 | bytes 933888 | tf_op jit(solution)/shard_map/concatenate | solution.py:174
  23.1 0.0 collective-permute-done
  23.1 0.0 collective-permute-done.1
  23.2 1.1 %pad_slice_fusion.10 = (bf16[2,10,34,384]{3,2,1,0:T(8,128)(2,1)S(1)}, bf16[2,10,34,384]{3,2,1,0:T(8,128)(2,1)S(1)}, bf16[2,10,34,384]{3,2,1,0:T(8,128)(2,1)S(1)}) fusion(bf16[2,10,32,384]{3,2,1,0:T(8,128)(2,1)S(1)} %constant_dynamic-update-slice_fusion), kind=kLoop, calls=%fused_computation.11 | loop fusion | bytes 2058240 | tf_op jit(solution)/shard_map/slice | solution.py:158
  24.3 1.6 %pad_maximum_fusion.x_ref = bf16[2,30,34,384]{3,2,1,0:T(8,128)(2,1)} fusion(bf16[2,10,34,384]{3,2,1,0:T(8,128)(2,1)S(1)} %get-tuple-element.13, bf16[2,10,34,384]{3,2,1,0:T(8,128)(2,1)S(1)} %get-tuple-element.12, bf16[2,10,34,384]{3,2,1,0:T(8,128)(2,1)S(1)} %get-tuple-element.11), kind=kLoop, calls=%fused_computation.8 | loop fusion | flops 1566720 | bytes 3133440 | tf_op jit(solution)/shard_map/concatenate | solution.py:157
  25.8 12.0 %all-to-all-done = f32[2,2,128,384]{3,1,0,2:T(2,128)S(1)} async-done(((f32[2,2,128,384]{3,1,0,2:T(2,128)}), f32[2,2,128,384]{3,1,0,2:T(2,128)S(1)}, u32[]{:S(2)}, u32[]{:S(2)}) %all-to-all-start) | async-done | bytes 786464 | tf_op jit(solution)/shard_map/all_to_all | solution.py:220
  37.9 1.2 %copy.61 = f32[256,2,1,384]{0,3,2,1:T(8,128)} copy(f32[256,2,1,384]{3,1,0,2:T(2,128)S(1)} %bitcast.23) | data formatting | bytes 1572864 | tf_op jit(solution)/shard_map/optimization_barrier | solution.py:175
  39.1 13.8 %shard_map.137 = bf16[2,1,384,256]{3,2,1,0:T(8,128)(2,1)} custom-call(f32[2,1,384,256]{3,2,1,0:T(8,128)} %bitcast.25, bf16[4,2,1,384,256]{4,3,2,1,0:T(8,128)(2,1)} %sens_ref.1, bf16[4,2,1,384,256]{4,3,2,1,0:T(8,128)(2,1)} %meas_ref.1, s32[384,256]{1,0:T(8,128)} %mask_ref.1, bf16[768,384]{1,0:T(8,128)(2,1)} %constant.13.clone.ty_ref, ...), custom_call_target="tpu_custom_call" | custom-call | tf_op jit(solution)/shard_map/pallas_call | solution.py:101
  52.8 1.9 %copy.62 = bf16[256,2,1,384]{3,1,2,0:T(2,128)(2,1)} copy(bf16[256,2,1,384]{0,3,2,1:T(8,128)(2,1)} %bitcast.27) | data formatting | bytes 786432 | tf_op jit(solution)/shard_map/transpose | solution.py:226
  54.8 3.7 %all-to-all-start.1 = ((bf16[256,2,1,384]{3,1,2,0:T(2,128)(2,1)}), bf16[256,2,1,384]{3,1,2,0:T(2,128)(2,1)S(1)}, u32[]{:S(2)}, u32[]{:S(2)}) async-start(bf16[256,2,1,384]{3,1,2,0:T(2,128)(2,1)} %copy.62), calls=%async_computation.1 | async-start | bytes 786432 | tf_op jit(solution)/shard_map/all_to_all | solution.py:227
  58.5 19.2 %shard_map.136 = f32[2,18,32,384]{3,2,1,0:T(8,128)} custom-call(bf16[2,30,34,384]{3,2,1,0:T(8,128)(2,1)} %pad_maximum_fusion.x_ref, f32[152,768]{1,0:T(8,128)} %pad_maximum_fusion.1.p_ref), custom_call_target="tpu_custom_call" | custom-call | tf_op jit(solution)/shard_map/pallas_call | solution.py:176
  77.8 0.0 all-to-all-done.1
  77.8 0.3 convert.20
  78.0 0.5 reduce_sum.9
  78.5 0.7 copy-done
  79.2 1.1 %add_add_fusion = f32[2,2,32,384]{3,2,1,0:T(8,128)} fusion(f32[2,2,32,384]{3,2,1,0:T(8,128)S(1)} %copy-done.2, f32[2,2,32,384]{3,2,1,0:T(8,128)S(1)} %copy-done.1, f32[2,2,32,384]{3,1,0,2:T(2,128)S(1)} %reduce_sum.9, f32[2,18,32,384]{3,2,1,0:T(8,128)S(1)} %copy-done), kind=kLoop, calls=%fused_computation.22 | loop fusion | flops 589824 | bytes 2752512 | tf_op jit(solution)/shard_map/add | solution.py:230
  (36 shorter events, 0.3 us)
Async XLA Ops:
  0.0 21.2 %copy-start.6 = (bf16[3,3,2,128]{3,2,1,0:T(2,128)(2,1)S(1)}, bf16[3,3,2,128]{3,2,1,0:T(2,128)(2,1)}, u32[]{:S(2)}) copy-start(bf16[3,3,2,128]{3,2,1,0:T(2,128)(2,1)} %param.25) | copy-start | bytes 13828
  0.0 21.3 %copy-start.5 = (bf16[3,3,10,128]{3,1,2,0:T(4,128)(2,1)S(1)}, bf16[3,3,10,128]{3,1,2,0:T(4,128)(2,1)}, u32[]{:S(2)}) copy-start(bf16[3,3,10,128]{3,1,2,0:T(4,128)(2,1)} %param.19) | copy-start | bytes 69124
  0.0 21.8 %copy-start.3 = (bf16[128,128]{1,0:T(8,128)(2,1)S(1)}, bf16[128,128]{1,0:T(8,128)(2,1)}, u32[]{:S(2)}) copy-start(bf16[128,128]{1,0:T(8,128)(2,1)} %param.21) | copy-start | bytes 98308
  0.0 21.9 %copy-start.4 = (bf16[128,128]{1,0:T(8,128)(2,1)S(1)}, bf16[128,128]{1,0:T(8,128)(2,1)}, u32[]{:S(2)}) copy-start(bf16[128,128]{1,0:T(8,128)(2,1)} %param.23) | copy-start | bytes 98308
  1.0 21.0 %copy-start.7 = (f32[128]{0:T(128)S(1)}, f32[128]{0:T(128)}, u32[]{:S(2)}) copy-start(f32[128]{0:T(128)} %param.24) | copy-start | bytes 1540
  1.0 21.0 %copy-start.8 = (f32[128]{0:T(128)S(1)}, f32[128]{0:T(128)}, u32[]{:S(2)}) copy-start(f32[128]{0:T(128)} %param.22) | copy-start | bytes 1540
  1.0 21.0 %copy-start.9 = (f32[128]{0:T(128)S(1)}, f32[128]{0:T(128)}, u32[]{:S(2)}) copy-start(f32[128]{0:T(128)} %param.20) | copy-start | bytes 1540
  1.0 22.0 %collective-permute-start = (bf16[2,2,32,384]{3,2,1,0:T(8,128)(2,1)S(1)}, bf16[2,2,32,384]{3,2,1,0:T(8,128)(2,1)S(1)}, u32[]{:S(2)}, u32[]{:S(2)}) collective-permute-start(bf16[2,2,32,384]{3,2,1,0:T(8,128)(2,1)S(1)} %convert_element_type.69), channel_id=1, source_target_pairs={{0,1},{1,2},{2,3},{3,4},{4,5},{5,6},{6,7},{7,8},{8,9},{9,10},{10,1... | collective-permute-start | bytes 294920 | tf_op jit(solution)/shard_map/ppermute | solution.py:20
  6.1 17.0 %collective-permute-start.1 = (bf16[2,2,32,384]{3,2,1,0:T(8,128)(2,1)S(1)}, bf16[2,2,32,384]{3,2,1,0:T(8,128)(2,1)S(1)}, u32[]{:S(2)}, u32[]{:S(2)}) collective-permute-start(bf16[2,2,32,384]{3,2,1,0:T(8,128)(2,1)S(1)} %convert_element_type.69), channel_id=1, source_target_pairs={{1,0},{2,1},{3,2},{4,3},{5,4},{6,5},{7,6},{8,7},{9,8},{10,9},{11,1... | collective-permute-start | bytes 294920 | tf_op jit(solution)/shard_map/ppermute | solution.py:21
  10.3 12.8 %copy-start.1 = (f32[2,2,32,384]{3,2,1,0:T(8,128)S(1)}, f32[2,2,32,384]{3,2,1,0:T(8,128)}, u32[]{:S(2)}) copy-start(f32[2,2,32,384]{3,2,1,0:T(8,128)} %param.14) | copy-start | bytes 589828
  10.3 27.6 %all-to-all-start = ((f32[2,2,128,384]{3,1,0,2:T(2,128)}), f32[2,2,128,384]{3,1,0,2:T(2,128)S(1)}, u32[]{:S(2)}, u32[]{:S(2)}) async-start(f32[2,2,128,384]{3,1,0,2:T(2,128)} %bitcast.8), calls=%async_computation | async-start | bytes 1572864 | tf_op jit(solution)/shard_map/all_to_all | solution.py:220
  54.8 23.0 %all-to-all-start.1 = ((bf16[256,2,1,384]{3,1,2,0:T(2,128)(2,1)}), bf16[256,2,1,384]{3,1,2,0:T(2,128)(2,1)S(1)}, u32[]{:S(2)}, u32[]{:S(2)}) async-start(bf16[256,2,1,384]{3,1,2,0:T(2,128)(2,1)} %copy.62), calls=%async_computation.1 | async-start | bytes 786432 | tf_op jit(solution)/shard_map/all_to_all | solution.py:227
  77.7 1.5 %copy-start = (f32[2,18,32,384]{3,2,1,0:T(8,128)S(1)}, f32[2,18,32,384]{3,2,1,0:T(8,128)}, u32[]{:S(2)}) copy-start(f32[2,18,32,384]{3,2,1,0:T(8,128)} %shard_map.136) | copy-start | bytes 5308420
  77.8 1.5 %copy-start.2 = (f32[2,2,32,384]{3,2,1,0:T(8,128)S(1)}, f32[2,2,32,384]{3,2,1,0:T(8,128)}, u32[]{:S(2)}) copy-start(f32[2,2,32,384]{3,2,1,0:T(8,128)} %param.15) | copy-start | bytes 589828

commit v20 on v18

--- a/solution.py
+++ b/solution.py
@@ -67,21 +67,25 @@
     image_imag = planes_ref[1]
     coil_real = (sens_real * image_real - sens_imag * image_imag).astype(jnp.bfloat16)
     coil_imag = (sens_real * image_imag + sens_imag * image_real).astype(jnp.bfloat16)
-    half = jnp.dot(ty, jnp.concatenate([coil_real, coil_imag], axis=1), preferred_element_type=jnp.float32)
-    half_real = (half[:ny, :nz] + half[ny:, nz:]).astype(jnp.bfloat16)
-    half_imag = (half[:ny, nz:] - half[ny:, :nz]).astype(jnp.bfloat16)
-    full = jnp.dot(jnp.concatenate([half_real, half_imag], axis=0), tz, preferred_element_type=jnp.float32)
-    spec_real = full[:ny, :nz] + full[ny:, nz:]
-    spec_imag = full[ny:, :nz] - full[:ny, nz:]
+    of_real = jnp.dot(ty, coil_real, preferred_element_type=jnp.float32)
+    of_imag = jnp.dot(ty, coil_imag, preferred_element_type=jnp.float32)
+    half_real = (of_real[:ny] + of_imag[ny:]).astype(jnp.bfloat16)
+    half_imag = (of_imag[:ny] - of_real[ny:]).astype(jnp.bfloat16)
+    of_real = jnp.dot(half_real, tz, preferred_element_type=jnp.float32)
+    of_imag = jnp.dot(half_imag, tz, preferred_element_type=jnp.float32)
+    spec_real = of_real[:, :nz] + of_imag[:, nz:]
+    spec_imag = of_imag[:, :nz] - of_real[:, nz:]
     sampled = mask_ref[...].astype(jnp.float32)
     miss_real = (sampled * (spec_real - meas_ref[0].astype(jnp.float32))).astype(jnp.bfloat16)
     miss_imag = (sampled * (spec_imag - meas_ref[1].astype(jnp.float32))).astype(jnp.bfloat16)
-    half = jnp.dot(ty, jnp.concatenate([miss_real, miss_imag], axis=1), preferred_element_type=jnp.float32)
-    back_real = (half[:ny, :nz] - half[ny:, nz:]).astype(jnp.bfloat16)
-    back_imag = (half[:ny, nz:] + half[ny:, :nz]).astype(jnp.bfloat16)
-    full = jnp.dot(jnp.concatenate([back_real, back_imag], axis=0), tz, preferred_element_type=jnp.float32)
-    grad_real = full[:ny, :nz] - full[ny:, nz:]
-    grad_imag = full[ny:, :nz] + full[:ny, nz:]
+    of_real = jnp.dot(ty, miss_real, preferred_element_type=jnp.float32)
+    of_imag = jnp.dot(ty, miss_imag, preferred_element_type=jnp.float32)
+    back_real = (of_real[:ny] - of_imag[ny:]).astype(jnp.bfloat16)
+    back_imag = (of_imag[:ny] + of_real[ny:]).astype(jnp.bfloat16)
+    of_real = jnp.dot(back_real, tz, preferred_element_type=jnp.float32)
+    of_imag = jnp.dot(back_imag, tz, preferred_element_type=jnp.float32)
+    grad_real = of_real[:, :nz] - of_imag[:, nz:]
+    grad_imag = of_imag[:, :nz] + of_real[:, nz:]
     acc_ref[0] += sens_real * grad_real + sens_imag * grad_imag
     acc_ref[1] += sens_real * grad_imag - sens_imag * grad_real
 

time: 76.6 us -> 76.6 us (level)
  no operation moved by 1% of the time
where the time goes in v20:
time: 76.6 us; the launch traced here: 76.3 us
  Pallas kernels  29 us (38%)
  starting transfers between devices  21.6 us (28%)
  waiting for transfers between devices  12 us (16%)
  local copies, waits for them, and re-layouts  8.02 us (10%)
  other arithmetic  5.3 us (7%)
    pallas_call x1, Pallas kernels, score_net(): pl.pallas_call(net_kernel, grid=(slice_count,), in_specs=[pl.BlockSpec((1...  15.2 us
    pallas_call x1, Pallas kernels, coil_adjoint(): pl.pallas_call(adjoint_kernel, grid=(coils,), in_specs=[pl.BlockSpec((2,...  13.8 us
    all_to_all x1, waiting for transfers between devices, on_device(): lax.all_to_all(copies, ('slab', 'coil'), split_axis=2, concat_axis=0, til...  12 us
    all_to_all x1, starting transfers between devices, on_device(): lax.all_to_all(copies, ('slab', 'coil'), split_axis=2, concat_axis=0, til...  10.9 us
    ppermute x1, starting transfers between devices, with_halo(): before = lax.ppermute(last, axis, up)  5.07 us
    all_to_all x1, starting transfers between devices, on_device(): lax.all_to_all(by_depth, ('slab', 'coil'), split_axis=0, concat_axis=2, t...  3.72 us
    unnamed x24, local copies, waits for them, and re-layouts  2.05 us
    transpose x1, local copies, waits for them, and re-layouts, on_device(): by_depth = jnp.transpose(partial_sum, (3, 0, 1, 2))  1.94 us
  transfers between devices with their start and end apart: 4, of which 1 were waited for; matrix products, arithmetic and copies ran while one was open for 9% of the time, Pallas kernels for 20%

profile of v20, /device:TPU:1, one launch (start us, length us, event | category | flops | bytes accessed | tf_op | source)
XLA Modules:
  0.0 76.3 jit_solution(10658942588502610520)
XLA Ops:
  0.0 1.0 %convert_element_type.69 = bf16[2,2,32,384]{3,2,1,0:T(8,128)(2,1)S(1)} convert(f32[2,2,32,384]{3,2,1,0:T(8,128)} %param.14) | non-fusion elementwise | flops 49152 | bytes 294912 | tf_op jit(solution)/shard_map/convert_element_type | solution.py:219
  1.0 0.0 copy-start.7
  1.0 0.0 copy-start.8
  1.0 0.0 copy-start.9
  1.0 5.1 %collective-permute-start = (bf16[2,2,32,384]{3,2,1,0:T(8,128)(2,1)S(1)}, bf16[2,2,32,384]{3,2,1,0:T(8,128)(2,1)S(1)}, u32[]{:S(2)}, u32[]{:S(2)}) collective-permute-start(bf16[2,2,32,384]{3,2,1,0:T(8,128)(2,1)S(1)} %convert_element_type.69), channel_id=1, source_target_pairs={{0,1},{1,2},{2,3},{3,4},{4,5},{5,6},{6,7},{7,8},{8,9},{9,10},{10,1... | collective-permute-start | bytes 294920 | tf_op jit(solution)/shard_map/ppermute | solution.py:20
  6.1 1.9 %collective-permute-start.1 = (bf16[2,2,32,384]{3,2,1,0:T(8,128)(2,1)S(1)}, bf16[2,2,32,384]{3,2,1,0:T(8,128)(2,1)S(1)}, u32[]{:S(2)}, u32[]{:S(2)}) collective-permute-start(bf16[2,2,32,384]{3,2,1,0:T(8,128)(2,1)S(1)} %convert_element_type.69), channel_id=1, source_target_pairs={{1,0},{2,1},{3,2},{4,3},{5,4},{6,5},{7,6},{8,7},{9,8},{10,9},{11,1... | collective-permute-start | bytes 294920 | tf_op jit(solution)/shard_map/ppermute | solution.py:21
  8.0 1.1 %copy.60 = f32[2,2,32,384]{3,1,0,2:T(2,128)S(1)} copy(f32[2,2,32,384]{3,2,1,0:T(8,128)} %param.14) | data formatting | bytes 393216 | tf_op args[0]
  9.1 1.1 %broadcast_in_dim.2 = f32[2,2,32,4,384]{4,1,0,3,2:T(2,128)} broadcast(f32[2,2,32,384]{3,1,0,2:T(2,128)S(1)} %copy.60), dimensions={0,1,2,4} | broadcast | bytes 983040 | tf_op jit(solution)/shard_map/broadcast_in_dim | solution.py:222
  10.3 10.9 %all-to-all-start = ((f32[2,2,128,384]{3,1,0,2:T(2,128)}), f32[2,2,128,384]{3,1,0,2:T(2,128)S(1)}, u32[]{:S(2)}, u32[]{:S(2)}) async-start(f32[2,2,128,384]{3,1,0,2:T(2,128)} %bitcast.8), calls=%async_computation | async-start | bytes 1572864 | tf_op jit(solution)/shard_map/all_to_all | solution.py:224
  21.3 0.1 copy.52
  21.5 0.1 copy.54
  21.6 0.1 copy.56
  21.8 0.1 copy.57
  21.9 0.1 copy.58
  22.0 0.0 copy-done.7
  22.1 0.1 copy.59
  22.3 0.8 %pad_maximum_fusion.1.p_ref = f32[152,768]{1,0:T(8,128)} fusion(f32[24,768]{1,0:T(8,128)S(1)} %pad_convert_fusion, f32[128,768]{1,0:T(8,128)S(1)} %pad_dynamic-update-slice_fusion), kind=kLoop, calls=%fused_computation.12 | loop fusion | flops 116736 | bytes 933888 | tf_op jit(solution)/shard_map/concatenate | solution.py:178
  23.1 0.0 collective-permute-done
  23.1 0.0 collective-permute-done.1
  23.2 1.1 %pad_slice_fusion.10 = (bf16[2,10,34,384]{3,2,1,0:T(8,128)(2,1)S(1)}, bf16[2,10,34,384]{3,2,1,0:T(8,128)(2,1)S(1)}, bf16[2,10,34,384]{3,2,1,0:T(8,128)(2,1)S(1)}) fusion(bf16[2,10,32,384]{3,2,1,0:T(8,128)(2,1)S(1)} %constant_dynamic-update-slice_fusion), kind=kLoop, calls=%fused_computation.11 | loop fusion | bytes 2058240 | tf_op jit(solution)/shard_map/slice | solution.py:162
  24.3 1.6 %pad_maximum_fusion.x_ref = bf16[2,30,34,384]{3,2,1,0:T(8,128)(2,1)} fusion(bf16[2,10,34,384]{3,2,1,0:T(8,128)(2,1)S(1)} %get-tuple-element.13, bf16[2,10,34,384]{3,2,1,0:T(8,128)(2,1)S(1)} %get-tuple-element.12, bf16[2,10,34,384]{3,2,1,0:T(8,128)(2,1)S(1)} %get-tuple-element.11), kind=kLoop, calls=%fused_computation.8 | loop fusion | flops 1566720 | bytes 3133440 | tf_op jit(solution)/shard_map/concatenate | solution.py:161
  25.8 12.0 %all-to-all-done = f32[2,2,128,384]{3,1,0,2:T(2,128)S(1)} async-done(((f32[2,2,128,384]{3,1,0,2:T(2,128)}), f32[2,2,128,384]{3,1,0,2:T(2,128)S(1)}, u32[]{:S(2)}, u32[]{:S(2)}) %all-to-all-start) | async-done | bytes 786464 | tf_op jit(solution)/shard_map/all_to_all | solution.py:224
  37.9 1.2 %copy.61 = f32[256,2,1,384]{0,3,2,1:T(8,128)} copy(f32[256,2,1,384]{3,1,0,2:T(2,128)S(1)} %bitcast.23) | data formatting | bytes 1572864 | tf_op jit(solution)/shard_map/optimization_barrier | solution.py:179
  39.1 13.8 %shard_map.137 = bf16[2,1,384,256]{3,2,1,0:T(8,128)(2,1)} custom-call(f32[2,1,384,256]{3,2,1,0:T(8,128)} %bitcast.25, bf16[4,2,1,384,256]{4,3,2,1,0:T(8,128)(2,1)} %sens_ref.1, bf16[4,2,1,384,256]{4,3,2,1,0:T(8,128)(2,1)} %meas_ref.1, s32[384,256]{1,0:T(8,128)} %mask_ref.1, bf16[768,384]{1,0:T(8,128)(2,1)} %constant.13.clone.ty_ref, ...), custom_call_target="tpu_custom_call" | custom-call | tf_op jit(solution)/shard_map/pallas_call | solution.py:105
  52.8 1.9 %copy.62 = bf16[256,2,1,384]{3,1,2,0:T(2,128)(2,1)} copy(bf16[256,2,1,384]{0,3,2,1:T(8,128)(2,1)} %bitcast.27) | data formatting | bytes 786432 | tf_op jit(solution)/shard_map/transpose | solution.py:230
  54.8 3.7 %all-to-all-start.1 = ((bf16[256,2,1,384]{3,1,2,0:T(2,128)(2,1)}), bf16[256,2,1,384]{3,1,2,0:T(2,128)(2,1)S(1)}, u32[]{:S(2)}, u32[]{:S(2)}) async-start(bf16[256,2,1,384]{3,1,2,0:T(2,128)(2,1)} %copy.62), calls=%async_computation.1 | async-start | bytes 786432 | tf_op jit(solution)/shard_map/all_to_all | solution.py:231
  58.5 15.2 %shard_map.136 = f32[2,18,32,384]{3,2,1,0:T(8,128)} custom-call(bf16[2,30,34,384]{3,2,1,0:T(8,128)(2,1)} %pad_maximum_fusion.x_ref, f32[152,768]{1,0:T(8,128)} %pad_maximum_fusion.1.p_ref), custom_call_target="tpu_custom_call" | custom-call | tf_op jit(solution)/shard_map/pallas_call | solution.py:180
  73.7 0.0 all-to-all-done.1
  73.7 0.3 convert.20
  74.0 0.5 reduce_sum.9
  74.5 0.7 copy-done
  75.2 1.1 %add_add_fusion = f32[2,2,32,384]{3,2,1,0:T(8,128)} fusion(f32[2,2,32,384]{3,2,1,0:T(8,128)S(1)} %copy-done.2, f32[2,2,32,384]{3,2,1,0:T(8,128)S(1)} %copy-done.1, f32[2,2,32,384]{3,1,0,2:T(2,128)S(1)} %reduce_sum.9, f32[2,18,32,384]{3,2,1,0:T(8,128)S(1)} %copy-done), kind=kLoop, calls=%fused_computation.22 | loop fusion | flops 589824 | bytes 2752512 | tf_op jit(solution)/shard_map/add | solution.py:234
  (36 shorter events, 0.3 us)
Async XLA Ops:
  0.0 21.2 %copy-start.6 = (bf16[3,3,2,128]{3,2,1,0:T(2,128)(2,1)S(1)}, bf16[3,3,2,128]{3,2,1,0:T(2,128)(2,1)}, u32[]{:S(2)}) copy-start(bf16[3,3,2,128]{3,2,1,0:T(2,128)(2,1)} %param.25) | copy-start | bytes 13828
  0.0 21.3 %copy-start.5 = (bf16[3,3,10,128]{3,1,2,0:T(4,128)(2,1)S(1)}, bf16[3,3,10,128]{3,1,2,0:T(4,128)(2,1)}, u32[]{:S(2)}) copy-start(bf16[3,3,10,128]{3,1,2,0:T(4,128)(2,1)} %param.19) | copy-start | bytes 69124
  0.0 21.8 %copy-start.3 = (bf16[128,128]{1,0:T(8,128)(2,1)S(1)}, bf16[128,128]{1,0:T(8,128)(2,1)}, u32[]{:S(2)}) copy-start(bf16[128,128]{1,0:T(8,128)(2,1)} %param.21) | copy-start | bytes 98308
  0.0 21.9 %copy-start.4 = (bf16[128,128]{1,0:T(8,128)(2,1)S(1)}, bf16[128,128]{1,0:T(8,128)(2,1)}, u32[]{:S(2)}) copy-start(bf16[128,128]{1,0:T(8,128)(2,1)} %param.23) | copy-start | bytes 98308
  1.0 21.0 %copy-start.7 = (f32[128]{0:T(128)S(1)}, f32[128]{0:T(128)}, u32[]{:S(2)}) copy-start(f32[128]{0:T(128)} %param.24) | copy-start | bytes 1540
  1.0 21.0 %copy-start.8 = (f32[128]{0:T(128)S(1)}, f32[128]{0:T(128)}, u32[]{:S(2)}) copy-start(f32[128]{0:T(128)} %param.22) | copy-start | bytes 1540
  1.0 21.0 %copy-start.9 = (f32[128]{0:T(128)S(1)}, f32[128]{0:T(128)}, u32[]{:S(2)}) copy-start(f32[128]{0:T(128)} %param.20) | copy-start | bytes 1540
  1.0 22.0 %collective-permute-start = (bf16[2,2,32,384]{3,2,1,0:T(8,128)(2,1)S(1)}, bf16[2,2,32,384]{3,2,1,0:T(8,128)(2,1)S(1)}, u32[]{:S(2)}, u32[]{:S(2)}) collective-permute-start(bf16[2,2,32,384]{3,2,1,0:T(8,128)(2,1)S(1)} %convert_element_type.69), channel_id=1, source_target_pairs={{0,1},{1,2},{2,3},{3,4},{4,5},{5,6},{6,7},{7,8},{8,9},{9,10},{10,1... | collective-permute-start | bytes 294920 | tf_op jit(solution)/shard_map/ppermute | solution.py:20
  6.1 17.0 %collective-permute-start.1 = (bf16[2,2,32,384]{3,2,1,0:T(8,128)(2,1)S(1)}, bf16[2,2,32,384]{3,2,1,0:T(8,128)(2,1)S(1)}, u32[]{:S(2)}, u32[]{:S(2)}) collective-permute-start(bf16[2,2,32,384]{3,2,1,0:T(8,128)(2,1)S(1)} %convert_element_type.69), channel_id=1, source_target_pairs={{1,0},{2,1},{3,2},{4,3},{5,4},{6,5},{7,6},{8,7},{9,8},{10,9},{11,1... | collective-permute-start | bytes 294920 | tf_op jit(solution)/shard_map/ppermute | solution.py:21
  10.3 12.8 %copy-start.1 = (f32[2,2,32,384]{3,2,1,0:T(8,128)S(1)}, f32[2,2,32,384]{3,2,1,0:T(8,128)}, u32[]{:S(2)}) copy-start(f32[2,2,32,384]{3,2,1,0:T(8,128)} %param.14) | copy-start | bytes 589828
  10.3 27.6 %all-to-all-start = ((f32[2,2,128,384]{3,1,0,2:T(2,128)}), f32[2,2,128,384]{3,1,0,2:T(2,128)S(1)}, u32[]{:S(2)}, u32[]{:S(2)}) async-start(f32[2,2,128,384]{3,1,0,2:T(2,128)} %bitcast.8), calls=%async_computation | async-start | bytes 1572864 | tf_op jit(solution)/shard_map/all_to_all | solution.py:224
  54.8 18.9 %all-to-all-start.1 = ((bf16[256,2,1,384]{3,1,2,0:T(2,128)(2,1)}), bf16[256,2,1,384]{3,1,2,0:T(2,128)(2,1)S(1)}, u32[]{:S(2)}, u32[]{:S(2)}) async-start(bf16[256,2,1,384]{3,1,2,0:T(2,128)(2,1)} %copy.62), calls=%async_computation.1 | async-start | bytes 786432 | tf_op jit(solution)/shard_map/all_to_all | solution.py:231
  73.7 1.5 %copy-start = (f32[2,18,32,384]{3,2,1,0:T(8,128)S(1)}, f32[2,18,32,384]{3,2,1,0:T(8,128)}, u32[]{:S(2)}) copy-start(f32[2,18,32,384]{3,2,1,0:T(8,128)} %shard_map.136) | copy-start | bytes 5308420
  73.7 1.5 %copy-start.2 = (f32[2,2,32,384]{3,2,1,0:T(8,128)S(1)}, f32[2,2,32,384]{3,2,1,0:T(8,128)}, u32[]{:S(2)}) copy-start(f32[2,2,32,384]{3,2,1,0:T(8,128)} %param.15) | copy-start | bytes 589828
